TPU v7x, 32 devices: a whole 2x2x4 slice. The times are simulated.
32 devices in a mesh: orb: 8 (over z, x), box: 4 (over y, core).
Axes of the slice: x: 2, y: 2, z: 4, core: 2. Of those that a mesh axis runs over, the one named last changes fastest.
Arguments:
- psi: float32 [64, 64, 4096], P('orb', 'box'), may hold values from -6 to 6
- potential: float32 [64, 4096], P('box'), may hold values from -3 to 3
- orbital_slot: int32 [32], replicated, may hold values from 0 to 63, as said below
Outputs:
- residual: float32 [32, 64, 4096], P('orb', 'box')
- direction: float32 [32, 64, 4096], P('orb', 'box')
- multipliers: float32 [32, 32], replicated
Inputs may be any that keep to these rules, and one draw needn't show every extreme that they name: The values are distinct slots: orbital j sits in slot orbital_slot[j]. The 8 slots of one index of orb hold up to 8 orbitals, and in every draw all slots of one index are filled.
All inputs are finite; a program needn't handle non-finite values.
Results may differ from a plain program's by a relative error of at most 0.0002.
Values sent between devices are 32-bit elements; how exact they have to be, the bound alone decides.
No kernel may reach another device: no remote copies, remote signals or barrier semaphores. Data moves between devices by JAX's collectives and lax.ppermute only.
A program may use at most 64 MiB of HBM per device.

v0:
```python
import functools
import math

import jax
import jax.numpy as jnp
import numpy as np
from jax import lax
from jax.experimental import pallas as pl
from jax.experimental.pallas import tpu as pltpu
from jax.sharding import PartitionSpec as P

MTAPS = 16
KREACH = 14
SWEEPS = 4
LANES = 128

highest = lax.Precision.HIGHEST
coupling_z = 4.0
coupling_xy = 1.0


def magic_weights(tap_count):
    half_len = tap_count // 2
    offsets = np.arange(1 - half_len, half_len + 1) * 1.0
    weights = np.ones(tap_count)
    for index_a in range(tap_count):
        for index_b in range(tap_count):
            if index_b != index_a:
                weights[index_a] *= (0.25 - offsets[index_b]) / (
                    offsets[index_a] - offsets[index_b]
                )
    return weights


def second_weights(reach_cells):
    factor = math.factorial(reach_cells) ** 2
    weights = np.zeros(2 * reach_cells + 1)
    for distance in range(1, reach_cells + 1):
        entry_value = (
            2.0
            * (-1) ** (distance + 1)
            * factor
            / (
                distance
                * distance
                * math.factorial(reach_cells - distance)
                * math.factorial(reach_cells + distance)
            )
        )
        weights[reach_cells + distance] = entry_value
        weights[reach_cells - distance] = entry_value
    weights[reach_cells] = -weights.sum()
    return -0.5 * weights


def banded(row_count, col_count, row_start, col_start, weights, offset_low):
    row_index = np.arange(row_count)[:, None] + row_start
    col_index = np.arange(col_count)[None, :] + col_start
    position = row_index - col_index - offset_low
    inside = (position >= 0) & (position < len(weights))
    return np.where(inside, weights[np.clip(position, 0, len(weights) - 1)], 0.0)


def f32(value):
    return float(np.float32(value))


MAGIC = {k: f32(w) for k, w in zip(range(1 - MTAPS // 2, MTAPS // 2 + 1), magic_weights(MTAPS))}
MAGIC_T = {-k: w for k, w in MAGIC.items()}
KINETIC = {
    d: f32(w) for d, w in zip(range(-KREACH, KREACH + 1), second_weights(KREACH))
}
LOW = MTAPS // 2
HIGH = MTAPS // 2 - 1


def two_part(matrix):
    width = matrix.shape[0]
    block = np.kron(np.eye(LANES // width), matrix).astype(np.float32)
    high = block.astype(jnp.bfloat16)
    low = (block - high.astype(np.float32)).astype(jnp.bfloat16)
    return np.block([[high, low], [high, np.zeros_like(low)]])


def split(value):
    high = value.astype(jnp.bfloat16)
    low = (value - high.astype(jnp.float32)).astype(jnp.bfloat16)
    return high, low


def lane_product(parts, matrix):
    both = jnp.dot(parts, matrix, preferred_element_type=jnp.float32)
    return both[:, :LANES] + both[:, LANES:]


def params(**kw):
    return pltpu.CompilerParams(vmem_limit_bytes=56 << 20, **kw)


def cost(flops, bytes_accessed):
    return pl.CostEstimate(flops=flops, bytes_accessed=bytes_accessed, transcendentals=0)


class Shape:
    def __init__(self, slots, depth, plane, owners):
        self.slots, self.depth, self.plane, self.owners = slots, depth, plane, owners
        self.side = math.isqrt(plane)
        self.chunks = plane // LANES
        self.across = min(owners, self.chunks)
        self.layered = owners // self.across
        self.layers = depth // self.layered
        self.width = plane // self.across
        self.inner = self.width // LANES

    def at(self, layer, block, inner):
        piece = (layer // self.layers) * self.across + block
        lanes = slice(inner * LANES, (inner + 1) * LANES)
        return piece, layer % self.layers, slice(None), lanes


def reorder_kernel(sh, psi_ref, out_ref):
    for group in range(sh.layered):
        rows = psi_ref[:, group * sh.layers : (group + 1) * sh.layers, :]
        rows = jnp.transpose(rows, (1, 0, 2))
        for block in range(sh.across):
            out_ref[group * sh.across + block] = rows[
                :, :, block * sh.width : (block + 1) * sh.width
            ]


def reorder(sh, psi):
    return pl.pallas_call(
        functools.partial(reorder_kernel, sh),
        out_shape=jax.ShapeDtypeStruct((sh.owners, sh.layers, sh.slots, sh.width), jnp.float32),
        compiler_params=params(),
        name="reorder",
    )(psi)


def odd_pairs(even, lane):
    turned = [pltpu.roll(v, LANES // 2, 1) for v in even]
    zero = jnp.zeros_like(even[0])
    low = [zero] + turned
    high = turned + [zero]
    return [jnp.where(lane, a, b) for a, b in zip(low, high)]


def row_filter(even, odd, weights):
    count = len(even)
    out = []
    for b in range(count):
        total = None
        for d, w in weights.items():
            e = b + d // 2
            if d % 2 == 0:
                if not 0 <= e < count:
                    continue
                term = even[e]
            else:
                if not 0 <= e + 1 <= count:
                    continue
                term = odd[e + 1]
            total = term * w if total is None else total + term * w
        out.append(total)
    return out


def row_filter_even(even, odd, weights, reach):
    count = len(even)
    out = []
    for b in range(count):
        total = even[b] * weights[0]
        for d in range(1, reach + 1):
            if d % 2 == 0:
                places = [e for e in (b + d // 2, b - d // 2) if 0 <= e < count]
                terms = [even[e] for e in places]
            else:
                places = [e for e in (b + d // 2 + 1, b - d // 2) if 0 <= e <= count]
                terms = [odd[e] for e in places]
            if not terms:
                continue
            term = terms[0] if len(terms) == 1 else terms[0] + terms[1]
            total = total + term * weights[d]
        out.append(total)
    return out


def half_mask(slots):
    return lax.broadcasted_iota(jnp.int32, (slots, LANES), 1) < LANES // 2


def lane_pass(sh, source, matrices, targets, layers):
    def body(block, carry):
        parts = []
        for inner in range(sh.inner):
            rows = jnp.concatenate(
                [source[sh.at(layer, block, inner)] for layer in range(layers)], 0
            )
            high, low = split(rows)
            parts.append(jnp.concatenate([high, low], 1))
        parts = jnp.concatenate(parts, 0)
        for matrix, target in zip(matrices, targets):
            result = lane_product(parts, matrix[...])
            result = result.reshape(sh.inner, layers, sh.slots, LANES)
            for inner in range(sh.inner):
                for layer in range(layers):
                    target[layer, block * sh.inner + inner] = result[inner, layer]
        return carry

    lax.fori_loop(0, sh.across, body, 0)


def own_kernel(sh, c_ref, fwd_ref, kin_ref, w_out, kin_out, x_ref):
    lane_pass(sh, c_ref, [fwd_ref, kin_ref], [x_ref, kin_out], sh.depth)
    lane = half_mask(sh.slots)

    for group in range(sh.layered):

        def body(i, carry):
            layer = group * sh.layers + i
            even = [x_ref[layer, b] for b in range(sh.chunks)]
            for b, v in enumerate(row_filter(even, odd_pairs(even, lane), MAGIC)):
                w_out[layer, b] = v
            even = [
                c_ref[
                    group * sh.across + b // sh.inner,
                    i,
                    :,
                    (b % sh.inner) * LANES : (b % sh.inner + 1) * LANES,
                ]
                for b in range(sh.chunks)
            ]
            sums = row_filter_even(even, odd_pairs(even, lane), KINETIC, KREACH)
            for b, v in enumerate(sums):
                kin_out[layer, b] += v
            return carry

        lax.fori_loop(0, sh.layers, body, 0)


def own_part(sh, c, fwd, kin):
    full = jax.ShapeDtypeStruct((sh.depth, sh.chunks, sh.slots, LANES), jnp.float32)
    return pl.pallas_call(
        functools.partial(own_kernel, sh),
        out_shape=(full, full),
        scratch_shapes=[pltpu.VMEM(full.shape, jnp.float32)],
        compiler_params=params(),
        cost_estimate=cost(10**10, 10**7),
        name="own_part",
    )(c, fwd, kin)


def halo_kernel(
    sh, lo_ref, c_ref, hi_ref, w_ref, kin_ref, vlo_ref, v_ref, vhi_ref, fwd_ref, bwd_ref,
    out_ref, x_ref, wlo_ref, whi_ref,
):
    lane = half_mask(sh.slots)
    depth = sh.depth
    for side_ref, target in ((lo_ref, wlo_ref), (hi_ref, whi_ref)):
        lane_pass(sh, side_ref, [fwd_ref], [x_ref], depth)

        def filter_rows(layer, carry):
            even = [x_ref[layer, b] for b in range(sh.chunks)]
            for b, v in enumerate(row_filter(even, odd_pairs(even, lane), MAGIC)):
                target[layer, b] = v
            return carry

        lax.fori_loop(0, depth, filter_rows, 0)

    def along_z(block, carry):
        for inner in range(sh.inner):
            chunk = block * sh.inner + inner
            lanes = pl.ds(pl.multiple_of(chunk * LANES, LANES), LANES)

            def coeff(z):
                ref = lo_ref if z < 0 else (c_ref if z < depth else hi_ref)
                return ref[sh.at(z % depth, block, inner)]

            def mixed(z):
                ref = wlo_ref if z < 0 else (w_ref if z < depth else whi_ref)
                return ref[z % depth, chunk]

            def level(z):
                ref = vlo_ref if z < 0 else (v_ref if z < depth else vhi_ref)
                return jnp.broadcast_to(ref[pl.ds(z % depth, 1), lanes], (sh.slots, LANES))

            values = {z: mixed(z) for z in range(-LOW - HIGH, depth + LOW + HIGH)}
            grid = {}
            for p in range(-LOW, depth + HIGH):
                total = None
                for k, w in MAGIC.items():
                    term = values[p + k] * w
                    total = term if total is None else total + term
                grid[p] = total * level(p)
            for q in range(depth):
                total = None
                for k, w in MAGIC.items():
                    term = grid[q - k] * w
                    total = term if total is None else total + term
                x_ref[q, chunk] = total
            cs = {z: coeff(z) for z in range(-KREACH, depth + KREACH)}
            for q in range(depth):
                total = kin_ref[q, chunk] + cs[q] * KINETIC[0]
                for d in range(1, KREACH + 1):
                    total = total + (cs[q + d] + cs[q - d]) * KINETIC[d]
                whi_ref[q, chunk] = total
        return carry

    lax.fori_loop(0, sh.across, along_z, 0)

    def filter_back(layer, carry):
        even = [x_ref[layer, b] for b in range(sh.chunks)]
        for b, v in enumerate(row_filter(even, odd_pairs(even, lane), MAGIC_T)):
            wlo_ref[layer, b] = v
        return carry

    lax.fori_loop(0, depth, filter_back, 0)

    def finish(block, carry):
        parts = []
        for inner in range(sh.inner):
            chunk = block * sh.inner + inner
            rows = jnp.concatenate([wlo_ref[layer, chunk] for layer in range(depth)], 0)
            high, low = split(rows)
            parts.append(jnp.concatenate([high, low], 1))
        result = lane_product(jnp.concatenate(parts, 0), bwd_ref[...])
        result = result.reshape(sh.inner, depth, sh.slots, LANES)
        for inner in range(sh.inner):
            chunk = block * sh.inner + inner
            for layer in range(depth):
                out_ref[sh.at(layer, block, inner)] = result[inner, layer] + whi_ref[layer, chunk]
        return carry

    lax.fori_loop(0, sh.across, finish, 0)


def halo_part(sh, lo, c, hi, w, kin, v_lo, v, v_hi, fwd, bwd):
    full = pltpu.VMEM((sh.depth, sh.chunks, sh.slots, LANES), jnp.float32)
    return pl.pallas_call(
        functools.partial(halo_kernel, sh),
        out_shape=jax.ShapeDtypeStruct(c.shape, jnp.float32),
        scratch_shapes=[full] * 3,
        compiler_params=params(),
        cost_estimate=cost(3 * 10**10, 10**7),
        name="halo_part",
    )(lo, c, hi, w, kin, v_lo, v, v_hi, fwd, bwd)


def selection(slot_ref, count, slots_all):
    column = lax.broadcasted_iota(jnp.int32, (count, slots_all), 1)
    return (column == slot_ref[...]).astype(jnp.float32)


def packed_rows(matrix, fold):
    rows = matrix.shape[0] // fold
    return jnp.concatenate([matrix[i * rows : (i + 1) * rows] for i in range(fold)], 1)


def unpacked_rows(matrix, fold):
    cols = matrix.shape[1] // fold
    return jnp.concatenate([matrix[:, i * cols : (i + 1) * cols] for i in range(fold)], 0)


def gram_kernel(sh, fold, c_ref, a_ref, slot_ref, out_ref):
    total_slots = sh.owners * sh.slots
    count = slot_ref.shape[0]

    def parts(ref, layer):
        rows = ref[:, layer].reshape(total_slots, sh.width)
        return jnp.concatenate(split(rows), 0)

    def body(layer, total):
        return total + lax.dot_general(
            parts(c_ref, layer),
            parts(a_ref, layer),
            (((1,), (1,)), ((), ())),
            preferred_element_type=jnp.float32,
        )

    both = jnp.zeros((2 * total_slots, 2 * total_slots), jnp.float32)
    both = lax.fori_loop(0, sh.layers, body, both, unroll=sh.layers <= 16 and total_slots <= 64)
    wide = both[:total_slots] + both[total_slots:]
    full = wide[:, :total_slots] + wide[:, total_slots:]
    chosen = selection(slot_ref, count, total_slots)
    rows = jnp.dot(chosen, full, precision=highest, preferred_element_type=jnp.float32)
    picked = lax.dot_general(
        rows, chosen, (((1,), (1,)), ((), ())), precision=highest,
        preferred_element_type=jnp.float32,
    ) * (1.0 / sh.side**3)
    picked = packed_rows(picked, fold)
    if len(out_ref.shape) == 2:
        out_ref[...] = picked
    else:
        out_ref[...] = jnp.broadcast_to(picked[None], out_ref.shape)


def gram(sh, c, a, slot, fold, copies):
    count = slot.shape[0]
    shape = (count // fold, count * fold)
    if copies:
        shape = (copies,) + shape
    return pl.pallas_call(
        functools.partial(gram_kernel, sh, fold),
        out_shape=jax.ShapeDtypeStruct(shape, jnp.float32),
        compiler_params=params(),
        cost_estimate=cost(10**9, 10**7),
        name="gram",
    )(c, a, slot)


def correct_kernel(sh, fold, own, c_ref, a_ref, slot_ref, part_ref, out_ref, mult_ref, inv_ref):
    total_slots = sh.owners * sh.slots
    count = slot_ref.shape[0]
    packed = part_ref[...]
    if packed.ndim == 3:
        packed = packed.sum(0)
    multipliers = unpacked_rows(packed, fold)
    mult_ref[...] = multipliers
    row = lax.broadcasted_iota(jnp.int32, (count, count), 0)
    col = lax.broadcasted_iota(jnp.int32, (count, count), 1)
    diagonal = jnp.sum(jnp.where(row == col, multipliers, 0.0), axis=1, keepdims=True)
    denominator = 2.0 * coupling_z + 4.0 * coupling_xy + 1.0 + jnp.abs(diagonal)
    inv_ref[...] = jnp.broadcast_to(1.0 / denominator, (count, LANES))
    chosen = selection(slot_ref, count, total_slots)
    mixing = lax.dot_general(
        multipliers, chosen, (((0,), (0,)), ((), ())), precision=highest,
        preferred_element_type=jnp.float32,
    )
    weights = jnp.concatenate([chosen, -mixing], 1)
    high, low = split(weights)
    weights = jnp.concatenate(
        [
            jnp.concatenate([high, high], 1),
            jnp.concatenate([low, jnp.zeros_like(low)], 1),
        ],
        0,
    )

    def body(layer):
        a_rows = split(a_ref[:, layer].reshape(total_slots, sh.width))
        c_rows = split(c_ref[:, layer].reshape(total_slots, sh.width))
        data = jnp.concatenate([a_rows[0], c_rows[0], a_rows[1], c_rows[1]], 0)
        both = jnp.dot(weights, data, preferred_element_type=jnp.float32)
        result = both[:count] + both[count:]
        for owner in range(sh.owners):
            out_ref[owner, layer * own : (layer + 1) * own] = result[
                owner * own : (owner + 1) * own
            ]

    for layer in range(sh.layers):
        body(layer)


def correct(sh, c, a, slot, part, fold):
    count = slot.shape[0]
    own = count // sh.owners
    return pl.pallas_call(
        functools.partial(correct_kernel, sh, fold, own),
        out_shape=(
            jax.ShapeDtypeStruct((sh.owners, sh.layers * own, sh.width), jnp.float32),
            jax.ShapeDtypeStruct((count, count), jnp.float32),
            jax.ShapeDtypeStruct((count, LANES), jnp.float32),
        ),
        compiler_params=params(),
        cost_estimate=cost(10**9, 10**7),
        name="correct",
    )(c, a, slot, part)


def relax_kernel(
    sh, own, ends_ref, r_ref, lo_ref, hi_ref, inv_ref, res_out, dir_out, res_ref, one_ref, two_ref
):
    rows = sh.depth * own
    edge = SWEEPS * own
    first = pl.multiple_of(ends_ref[0] * own, own)
    inverse = inv_ref[pl.ds(first, own), :]
    inverse = jnp.concatenate([inverse] * (8 // own), 0)
    keep_lo = inverse * ends_ref[1].astype(jnp.float32)
    keep_hi = inverse * ends_ref[2].astype(jnp.float32)
    tiles = (rows + 2 * edge) // 8
    edge_tiles = edge // 8

    def scale(tile):
        if tile < edge_tiles:
            return keep_lo
        return keep_hi if tile >= tiles - edge_tiles else inverse

    def gather(block, carry):
        for inner in range(sh.inner):
            chunk = block * sh.inner + inner
            lanes = slice(inner * LANES, (inner + 1) * LANES)
            pieces = [lo_ref[block, :, lanes]]
            pieces += [r_ref[g * sh.across + block, :, lanes] for g in range(sh.layered)]
            pieces += [hi_ref[block, :, lanes]]
            column = jnp.concatenate(pieces, 0)
            for tile in range(tiles):
                value = column[tile * 8 : (tile + 1) * 8]
                res_ref[chunk, tile * 8 : (tile + 1) * 8] = value
                one_ref[chunk, tile * 8 : (tile + 1) * 8] = value * scale(tile)
            out_lanes = pl.ds(pl.multiple_of(chunk * LANES, LANES), LANES)
            for orbital in range(own):
                res_out[orbital, :, out_lanes] = res_ref[
                    chunk, pl.ds(edge + orbital, sh.depth, stride=own), :
                ]
        return carry

    lax.fori_loop(0, sh.across, gather, 0)

    sub = lax.broadcasted_iota(jnp.int32, (8, LANES), 0)
    lane = lax.broadcasted_iota(jnp.int32, (8, LANES), 1)
    upper = sub >= own
    right_half = lane >= LANES // 2
    not_last = (lane % sh.side) != sh.side - 1
    not_first = (lane % sh.side) != 0
    half = 8 // own
    assert half == 2

    def sweep(source, target, tile_list):
        def body(chunk, carry):
            before = jnp.maximum(chunk - 1, 0)
            after = jnp.minimum(chunk + 1, sh.chunks - 1)
            has_before = (chunk > 0).astype(jnp.float32)
            has_after = (chunk < sh.chunks - 1).astype(jnp.float32)
            for tile in tile_list:
                here = pl.ds(tile * 8, 8)
                value = source[chunk, here]
                zero = jnp.zeros_like(value)
                below = source[chunk, pl.ds(tile * 8 - 8, 8)] if tile > 0 else zero
                above = source[chunk, pl.ds(tile * 8 + 8, 8)] if tile < tiles - 1 else zero
                along_z = pltpu.roll(value + jnp.where(upper, below, above), own, 0)
                along_y = pltpu.roll(
                    value
                    + jnp.where(
                        right_half,
                        source[before, here] * has_before,
                        source[after, here] * has_after,
                    ),
                    LANES // 2,
                    1,
                )
                along_x = pltpu.roll(jnp.where(not_last, value, 0.0), 1, 1) + pltpu.roll(
                    jnp.where(not_first, value, 0.0), LANES - 1, 1
                )
                total = (
                    res_ref[chunk, here]
                    + coupling_xy * (along_y + along_x)
                    + coupling_z * along_z
                )
                target[chunk, here] = total * scale(tile)
            return carry

        lax.fori_loop(0, sh.chunks, body, 0)

    source, target = one_ref, two_ref
    for done in range(1, SWEEPS + 1):
        first_tile = done * own // 8
        sweep(source, target, range(first_tile, tiles - first_tile))
        source, target = target, source

    def spread(chunk, carry):
        out_lanes = pl.ds(pl.multiple_of(chunk * LANES, LANES), LANES)
        for orbital in range(own):
            dir_out[orbital, :, out_lanes] = source[
                chunk, pl.ds(edge + orbital, sh.depth, stride=own), :
            ]
        return carry

    lax.fori_loop(0, sh.chunks, spread, 0)


def relax(sh, own, ends, r, lo, hi, inverse):
    rows = (sh.depth + 2 * SWEEPS) * own
    scratch = pltpu.VMEM((sh.chunks, rows, LANES), jnp.float32)
    out = jax.ShapeDtypeStruct((own, sh.depth, sh.plane), jnp.float32)
    vmem = pl.BlockSpec(memory_space=pltpu.VMEM)
    return pl.pallas_call(
        functools.partial(relax_kernel, sh, own),
        out_shape=(out, out),
        in_specs=[pl.BlockSpec(memory_space=pltpu.SMEM)] + [vmem] * 4,
        scratch_shapes=[scratch] * 3,
        compiler_params=params(),
        cost_estimate=cost(10**9, 10**7),
        name="relax",
    )(ends, r, lo, hi, inverse)


def exchange(value, axis):
    count = lax.axis_size(axis)
    forward = [(i, i + 1) for i in range(count - 1)]
    backward = [(target, source) for source, target in forward]
    return lax.ppermute(value, axis, forward), lax.ppermute(value, axis, backward)


def to_all(value, axes):
    return lax.all_to_all(value, axes, split_axis=0, concat_axis=0, tiled=True)


def local(psi, potential, orbital_slot):
    slots, depth, plane = psi.shape
    owners = lax.axis_size("orb")
    boxes = lax.axis_size("box")
    sh = Shape(slots, depth, plane, owners)
    count = orbital_slot.shape[0]
    own = count // owners
    magic = banded(sh.side, sh.side, 0, 0, magic_weights(MTAPS), 1 - MTAPS // 2)
    kinetic = banded(sh.side, sh.side, 0, 0, second_weights(KREACH), -KREACH)
    fwd, bwd, kin = (jnp.asarray(two_part(m)) for m in (magic, magic.T, kinetic))

    c = reorder(sh, psi)
    pieces = to_all(c, "orb")
    lo, hi = exchange(c, "box")
    v_lo, v_hi = exchange(potential, "box")
    w, kin_own = own_part(sh, c, fwd, kin)
    applied = halo_part(sh, lo, c, hi, w, kin_own, v_lo, potential, v_hi, fwd, bwd)
    applied_pieces = to_all(applied, "orb")

    slot = orbital_slot.reshape(count, 1)
    fold = max(1, LANES // count)
    devices = owners * boxes
    copies = devices if devices * count * count <= 1 << 20 else 0
    part = gram(sh, pieces, applied_pieces, slot, fold, copies)
    part = to_all(part, ("orb", "box")) if copies else lax.psum(part, ("orb", "box"))
    corrected, multipliers, inverse = correct(sh, pieces, applied_pieces, slot, part, fold)
    returned = to_all(corrected, "orb")
    edge = SWEEPS * own
    box = lax.axis_index("box")
    from_low = lax.ppermute(
        returned[-sh.across :, -edge:], "box", [(i, i + 1) for i in range(boxes - 1)]
    )
    from_high = lax.ppermute(
        returned[: sh.across, :edge], "box", [(i + 1, i) for i in range(boxes - 1)]
    )
    ends = jnp.stack(
        [lax.axis_index("orb"), (box > 0).astype(jnp.int32), (box < boxes - 1).astype(jnp.int32)]
    ).astype(jnp.int32)
    residual, direction = relax(sh, own, ends, returned, from_low, from_high, inverse)
    return (residual, direction, multipliers)


def solution(mesh):
    in_specs = (P("orb", "box", None), P("box", None), P())
    out_specs = (P("orb", "box", None), P("orb", "box", None), P())
    return jax.shard_map(local, mesh=mesh, in_specs=in_specs, out_specs=out_specs, check_vma=False)
```

profile of v0, /device:TPU:1, one launch (start us, length us, event | category | flops | bytes accessed | tf_op | source)
XLA Modules:
  0.0 200.4 jit_solution(18003505109029148597)
XLA Ops:
  0.6 0.0 copy-start.3
  0.6 3.3 %reorder.1.c_ref = f32[8,16,8,512]{3,2,1,0:T(8,128)} custom-call(f32[8,16,4096]{2,1,0:T(8,128)} %psi_ref.1), custom_call_target="tpu_custom_call" | custom-call | tf_op jit(solution)/shard_map/reorder/pallas_call | solution.py:132
  4.0 4.5 %collective-permute-start = (f32[8,16,8,512]{3,2,1,0:T(8,128)}, f32[8,16,8,512]{3,2,1,0:T(8,128)}, u32[]{:S(2)}, u32[]{:S(2)}) collective-permute-start(f32[8,16,8,512]{3,2,1,0:T(8,128)} %reorder.1.c_ref), channel_id=1, source_target_pairs={{0,1},{1,2},{2,3},{4,5},{5,6},{6,7},{8,9},{9,10},{10,11},{12,13},{... | collective-permute-start | bytes 6291464 | tf_op jit(solution)/shard_map/ppermute | solution.py:591
  8.5 1.9 collective-permute-start.1
  10.4 0.0 copy-done.3
  10.4 3.6 %collective-permute-start.2 = (f32[16,4096]{1,0:T(8,128)S(1)}, f32[16,4096]{1,0:T(8,128)S(1)}, u32[]{:S(2)}, u32[]{:S(2)}) collective-permute-start(f32[16,4096]{1,0:T(8,128)S(1)} %copy-done.3), channel_id=1, source_target_pairs={{0,1},{1,2},{2,3},{4,5},{5,6},{6,7},{8,9},{9,10},{10,11},{12,13},{... | collective-permute-start | bytes 786440 | tf_op jit(solution)/shard_map/ppermute | solution.py:591
  14.1 1.9 collective-permute-start.3
  16.0 5.5 %all-to-all-start = ((f32[8,16,8,512]{3,2,1,0:T(8,128)}), f32[8,16,8,512]{3,2,1,0:T(8,128)S(1)}, u32[]{:S(2)}, u32[]{:S(2)}) async-start(f32[8,16,8,512]{3,2,1,0:T(8,128)} %reorder.1.c_ref), calls=%async_computation | async-start | bytes 4194304 | tf_op jit(solution)/shard_map/all_to_all | solution.py:595
  21.6 12.1 %own_part.1 = (f32[16,32,8,128]{3,2,1,0:T(8,128)}, f32[16,32,8,128]{3,2,1,0:T(8,128)}) custom-call(f32[8,16,8,512]{3,2,1,0:T(8,128)} %reorder.1.c_ref, bf16[256,256]{1,0:T(8,128)(2,1)} %constant.19.clone.fwd_ref, bf16[256,256]{1,0:T(8,128)(2,1)} %constant.21.clone.kin_ref), custom_call_target="tpu_custom_call" | custom-call | flops 10000000000 | bytes 10000000 | tf_op jit(solution)/shard_map/own_part/pallas_call | solution.py:243
  33.7 0.8 collective-permute-done.2.vlo_ref
  34.5 0.0 copy-start.6
  34.5 4.7 %collective-permute-done.3.vhi_ref = f32[16,4096]{1,0:T(8,128)S(1)} collective-permute-done((f32[16,4096]{1,0:T(8,128)S(1)}, f32[16,4096]{1,0:T(8,128)S(1)}, u32[]{:S(2)}, u32[]{:S(2)}) %collective-permute-start.3) | collective-permute-done | bytes 262176 | tf_op jit(solution)/shard_map/ppermute | solution.py:591
  39.2 0.0 copy-start.7
  39.2 0.0 collective-permute-done.lo_ref
  39.2 0.0 collective-permute-done.1.hi_ref
  39.2 0.0 copy-done.6
  39.2 0.7 copy-done.7
  39.9 30.6 %halo_part.1 = f32[8,16,8,512]{3,2,1,0:T(8,128)} custom-call(f32[8,16,8,512]{3,2,1,0:T(8,128)} %collective-permute-done.lo_ref, f32[8,16,8,512]{3,2,1,0:T(8,128)} %reorder.1.c_ref, f32[8,16,8,512]{3,2,1,0:T(8,128)} %collective-permute-done.1.hi_ref, f32[16,32,8,128]{3,2,1,0:T(8,128)} %get-tuple-element.10.w_ref, ...), custom_call_target="tpu_custom_call" | custom-call | flops 30000001024 | bytes 10000000 | tf_op jit(solution)/shard_map/halo_part/pallas_call | solution.py:339
  70.5 0.0 copy-start.2
  70.5 0.0 all-to-all-done.c_ref
  70.5 0.0 copy-start
  70.5 1.3 copy-done
  71.8 5.2 %all-to-all-start.1 = ((f32[8,16,8,512]{3,2,1,0:T(8,128)}), f32[8,16,8,512]{3,2,1,0:T(8,128)}, u32[]{:S(2)}, u32[]{:S(2)}) async-start(f32[8,16,8,512]{3,2,1,0:T(8,128)} %halo_part.1), calls=%async_computation.1 | async-start | bytes 4194304 | tf_op jit(solution)/shard_map/all_to_all | solution.py:595
  77.1 0.0 copy-done.2
  77.1 0.7 copy.10.slot_ref
  77.8 46.3 %all-to-all-done.1.a_ref = f32[8,16,8,512]{3,2,1,0:T(8,128)} async-done(((f32[8,16,8,512]{3,2,1,0:T(8,128)}), f32[8,16,8,512]{3,2,1,0:T(8,128)}, u32[]{:S(2)}, u32[]{:S(2)}) %all-to-all-start.1) | async-done | bytes 2097184 | tf_op jit(solution)/shard_map/all_to_all | solution.py:595
  124.1 4.1 %gram.1 = f32[32,8,128]{2,1,0:T(8,128)} custom-call(f32[8,16,8,512]{3,2,1,0:T(8,128)} %copy-done, f32[8,16,8,512]{3,2,1,0:T(8,128)} %all-to-all-done.1.a_ref, s32[32,1]{1,0:T(8,128)} %copy.10.slot_ref), custom_call_target="tpu_custom_call" | custom-call | flops 1000000000 | bytes 10000000 | tf_op jit(solution)/shard_map/gram/pallas_call | solution.py:402
  128.2 10.9 %all_to_all.20.part_ref = f32[32,8,128]{2,1,0:T(8,128)} all-to-all(f32[32,8,128]{2,1,0:T(8,128)} %gram.1), channel_id=1, replica_groups=mesh['orb'=8,'box'=4] {'orb','box'}, dimensions={0} | all-to-all | bytes 262144 | tf_op jit(solution)/shard_map/all_to_all | solution.py:595
  139.2 4.4 %correct.1 = (f32[8,64,512]{2,1,0:T(8,128)}, f32[32,32]{1,0:T(8,128)}, f32[32,128]{1,0:T(8,128)}) custom-call(f32[8,16,8,512]{3,2,1,0:T(8,128)} %copy-done, f32[8,16,8,512]{3,2,1,0:T(8,128)} %all-to-all-done.1.a_ref, s32[32,1]{1,0:T(8,128)} %copy.10.slot_ref, f32[32,8,128]{2,1,0:T(8,128)} %all_to_all.20.part_ref), custom_call_target="tpu_custom_call" | custom-call | flops 1000000000 | bytes 10000000 | tf_op jit(solution)/shard_map/correct/pallas_call | solution.py:457
  143.6 29.0 %all_to_all.21.r_ref = f32[8,64,512]{2,1,0:T(8,128)S(1)} all-to-all(f32[8,64,512]{2,1,0:T(8,128)} %get-tuple-element.12), channel_id=1, replica_groups=mesh['orb'=8,'box'=4] {'orb'}, dimensions={0} | all-to-all | bytes 2097152 | tf_op jit(solution)/shard_map/all_to_all | solution.py:595
  172.6 0.0 copy-start.1
  172.6 3.0 %collective-permute-start.4 = (f32[8,16,512]{2,1,0:T(8,128)S(1)}, f32[8,16,512]{2,1,0:T(8,128)S(1)}, u32[]{:S(2)}, u32[]{:S(2)}) collective-permute-start(f32[8,16,512]{2,1,0:T(8,128)S(1)} %get-tuple-element.18), channel_id=1, source_target_pairs={{0,1},{1,2},{2,3},{4,5},{5,6},{6,7},{8,9},{9,10},{10,11},{12,13},{... | collective-permute-start | bytes 786440 | tf_op jit(solution)/shard_map/ppermute | solution.py:627
  175.6 1.9 collective-permute-start.5
  177.6 0.6 pad_add_fusion.ends_ref
  178.2 0.8 collective-permute-done.4.lo_ref
  178.9 0.0 copy-start.4
  178.9 4.4 %collective-permute-done.5.hi_ref = f32[8,16,512]{2,1,0:T(8,128)S(1)} collective-permute-done((f32[8,16,512]{2,1,0:T(8,128)S(1)}, f32[8,16,512]{2,1,0:T(8,128)S(1)}, u32[]{:S(2)}, u32[]{:S(2)}) %collective-permute-start.5) | collective-permute-done | bytes 262176 | tf_op jit(solution)/shard_map/ppermute | solution.py:630
  183.3 0.0 copy-start.5
  183.3 0.0 copy-done.1
  183.3 0.0 copy-done.4
  183.3 0.7 copy-done.5
  184.0 16.4 %relax.1 = (f32[4,16,4096]{2,1,0:T(8,128)}, f32[4,16,4096]{2,1,0:T(8,128)}) custom-call(s32[3]{0:T(128)} %pad_add_fusion.ends_ref, f32[8,64,512]{2,1,0:T(8,128)} %copy-done.1, f32[8,16,512]{2,1,0:T(8,128)} %copy-done.4, f32[8,16,512]{2,1,0:T(8,128)} %copy-done.5, f32[32,128]{1,0:T(8,128)} %get-tuple-element.13.inv_ref), custom_call_target="tpu_custom_call" | custom-call | flops 1000000000 | bytes 10000000 | tf_op jit(solution)/shard_map/relax/pallas_call | solution.py:576
  (1 shorter events, 0.0 us)
Async XLA Ops:
  0.6 9.8 %copy-start.3 = (f32[16,4096]{1,0:T(8,128)S(1)}, f32[16,4096]{1,0:T(8,128)}, u32[]{:S(2)}) copy-start(f32[16,4096]{1,0:T(8,128)} %v_ref.1) | copy-start | bytes 786436
  4.0 35.2 %collective-permute-start = (f32[8,16,8,512]{3,2,1,0:T(8,128)}, f32[8,16,8,512]{3,2,1,0:T(8,128)}, u32[]{:S(2)}, u32[]{:S(2)}) collective-permute-start(f32[8,16,8,512]{3,2,1,0:T(8,128)} %reorder.1.c_ref), channel_id=1, source_target_pairs={{0,1},{1,2},{2,3},{4,5},{5,6},{6,7},{8,9},{9,10},{10,11},{12,13},{... | collective-permute-start | bytes 6291464 | tf_op jit(solution)/shard_map/ppermute | solution.py:591
  8.5 30.7 %collective-permute-start.1 = (f32[8,16,8,512]{3,2,1,0:T(8,128)}, f32[8,16,8,512]{3,2,1,0:T(8,128)}, u32[]{:S(2)}, u32[]{:S(2)}) collective-permute-start(f32[8,16,8,512]{3,2,1,0:T(8,128)} %reorder.1.c_ref), channel_id=1, source_target_pairs={{1,0},{2,1},{3,2},{5,4},{6,5},{7,6},{9,8},{10,9},{11,10},{13,12},{... | collective-permute-start | bytes 6291464 | tf_op jit(solution)/shard_map/ppermute | solution.py:591
  10.4 24.0 %collective-permute-start.2 = (f32[16,4096]{1,0:T(8,128)S(1)}, f32[16,4096]{1,0:T(8,128)S(1)}, u32[]{:S(2)}, u32[]{:S(2)}) collective-permute-start(f32[16,4096]{1,0:T(8,128)S(1)} %copy-done.3), channel_id=1, source_target_pairs={{0,1},{1,2},{2,3},{4,5},{5,6},{6,7},{8,9},{9,10},{10,11},{12,13},{... | collective-permute-start | bytes 786440 | tf_op jit(solution)/shard_map/ppermute | solution.py:591
  14.1 25.1 %collective-permute-start.3 = (f32[16,4096]{1,0:T(8,128)S(1)}, f32[16,4096]{1,0:T(8,128)S(1)}, u32[]{:S(2)}, u32[]{:S(2)}) collective-permute-start(f32[16,4096]{1,0:T(8,128)S(1)} %copy-done.3), channel_id=1, source_target_pairs={{1,0},{2,1},{3,2},{5,4},{6,5},{7,6},{9,8},{10,9},{11,10},{13,12},{... | collective-permute-start | bytes 786440 | tf_op jit(solution)/shard_map/ppermute | solution.py:591
  16.0 54.5 %all-to-all-start = ((f32[8,16,8,512]{3,2,1,0:T(8,128)}), f32[8,16,8,512]{3,2,1,0:T(8,128)S(1)}, u32[]{:S(2)}, u32[]{:S(2)}) async-start(f32[8,16,8,512]{3,2,1,0:T(8,128)} %reorder.1.c_ref), calls=%async_computation | async-start | bytes 4194304 | tf_op jit(solution)/shard_map/all_to_all | solution.py:595
  34.5 4.7 %copy-start.6 = (f32[16,4096]{1,0:T(8,128)}, f32[16,4096]{1,0:T(8,128)S(1)}, u32[]{:S(2)}) copy-start(f32[16,4096]{1,0:T(8,128)S(1)} %collective-permute-done.2.vlo_ref) | copy-start | bytes 786436
  39.2 0.7 copy-start.7
  70.5 6.6 %copy-start.2 = (s32[32]{0:T(128)S(1)}, s32[32]{0:T(128)}, u32[]{:S(2)}) copy-start(s32[32]{0:T(128)} %param.8) | copy-start | bytes 388
  70.5 1.3 copy-start
  71.8 52.3 %all-to-all-start.1 = ((f32[8,16,8,512]{3,2,1,0:T(8,128)}), f32[8,16,8,512]{3,2,1,0:T(8,128)}, u32[]{:S(2)}, u32[]{:S(2)}) async-start(f32[8,16,8,512]{3,2,1,0:T(8,128)} %halo_part.1), calls=%async_computation.1 | async-start | bytes 4194304 | tf_op jit(solution)/shard_map/all_to_all | solution.py:595
  172.6 10.8 %copy-start.1 = (f32[8,64,512]{2,1,0:T(8,128)}, f32[8,64,512]{2,1,0:T(8,128)S(1)}, u32[]{:S(2)}) copy-start(f32[8,64,512]{2,1,0:T(8,128)S(1)} %all_to_all.21.r_ref) | copy-start | bytes 3145732
  172.6 6.3 %collective-permute-start.4 = (f32[8,16,512]{2,1,0:T(8,128)S(1)}, f32[8,16,512]{2,1,0:T(8,128)S(1)}, u32[]{:S(2)}, u32[]{:S(2)}) collective-permute-start(f32[8,16,512]{2,1,0:T(8,128)S(1)} %get-tuple-element.18), channel_id=1, source_target_pairs={{0,1},{1,2},{2,3},{4,5},{5,6},{6,7},{8,9},{9,10},{10,11},{12,13},{... | collective-permute-start | bytes 786440 | tf_op jit(solution)/shard_map/ppermute | solution.py:627
  175.6 7.7 %collective-permute-start.5 = (f32[8,16,512]{2,1,0:T(8,128)S(1)}, f32[8,16,512]{2,1,0:T(8,128)S(1)}, u32[]{:S(2)}, u32[]{:S(2)}) collective-permute-start(f32[8,16,512]{2,1,0:T(8,128)S(1)} %get-tuple-element.17), channel_id=1, source_target_pairs={{1,0},{2,1},{3,2},{5,4},{6,5},{7,6},{9,8},{10,9},{11,10},{13,12},{... | collective-permute-start | bytes 786440 | tf_op jit(solution)/shard_map/ppermute | solution.py:630
  178.9 4.4 %copy-start.4 = (f32[8,16,512]{2,1,0:T(8,128)}, f32[8,16,512]{2,1,0:T(8,128)S(1)}, u32[]{:S(2)}) copy-start(f32[8,16,512]{2,1,0:T(8,128)S(1)} %collective-permute-done.4.lo_ref) | copy-start | bytes 786436
  183.3 0.7 copy-start.5
where the time goes:
time: 201 us; the launch traced here: 200 us
  Pallas kernels  71 us (35%)
  waiting for transfers between devices  57 us (28%)
  blocking collectives  39.9 us (20%)
  starting transfers between devices  27.7 us (14%)
  local copies, waits for them, and re-layouts  3.47 us (2%)
    all_to_all x2, waiting for transfers between devices, to_all(): return lax.all_to_all(value, axes, split_axis=0, concat_axis=0, tiled=True)  46.3 us
    all_to_all x2, blocking collectives, to_all(): return lax.all_to_all(value, axes, split_axis=0, concat_axis=0, tiled=True)  39.9 us
    pallas_call x1, Pallas kernels, halo_part(): pl.pallas_call(functools.partial(halo_kernel, sh), out_shape=jax.ShapeDty...  30.6 us
    pallas_call x1, Pallas kernels, relax(): pl.pallas_call(functools.partial(relax_kernel, sh, own), out_shape=(out,...  16.4 us
    pallas_call x1, Pallas kernels, own_part(): pl.pallas_call(functools.partial(own_kernel, sh), out_shape=(full, full),...  12.1 us
    all_to_all x2, starting transfers between devices, to_all(): return lax.all_to_all(value, axes, split_axis=0, concat_axis=0, tiled=True)  10.8 us
    ppermute x2, starting transfers between devices, exchange(): lax.ppermute(value, axis, forward)  8.16 us
    ppermute x2, waiting for transfers between devices, exchange(): lax.ppermute(value, axis, backward)  4.69 us
  transfers between devices with their start and end apart: 8, of which 5 were waited for; matrix products, arithmetic and copies ran while one was open for 1% of the time, Pallas kernels for 21%

commit v1 on v0

--- a/solution.py
+++ b/solution.py
@@ -93,8 +93,8 @@
     return both[:, :LANES] + both[:, LANES:]
 
 
-def params(**kw):
-    return pltpu.CompilerParams(vmem_limit_bytes=56 << 20, **kw)
+def params(mib):
+    return pltpu.CompilerParams(vmem_limit_bytes=mib << 20)
 
 
 def cost(flops, bytes_accessed):
@@ -104,7 +104,7 @@
 class Shape:
     def __init__(self, slots, depth, plane, owners):
         self.slots, self.depth, self.plane, self.owners = slots, depth, plane, owners
-        self.side = math.isqrt(plane)
+        self.box = math.isqrt(plane)
         self.chunks = plane // LANES
         self.across = min(owners, self.chunks)
         self.layered = owners // self.across
@@ -117,24 +117,39 @@
         lanes = slice(inner * LANES, (inner + 1) * LANES)
         return piece, layer % self.layers, slice(None), lanes
 
-
-def reorder_kernel(sh, psi_ref, out_ref):
+    def side(self, layer, block, inner):
+        return block, layer, slice(None), slice(inner * LANES, (inner + 1) * LANES)
+
+
+def reorder_kernel(sh, psi_ref, v_ref, out_ref, up_ref, down_ref):
     for group in range(sh.layered):
-        rows = psi_ref[:, group * sh.layers : (group + 1) * sh.layers, :]
-        rows = jnp.transpose(rows, (1, 0, 2))
+        first = group * sh.layers
+        rows = jnp.transpose(psi_ref[:, first : first + sh.layers, :], (1, 0, 2))
         for block in range(sh.across):
-            out_ref[group * sh.across + block] = rows[
-                :, :, block * sh.width : (block + 1) * sh.width
-            ]
-
-
-def reorder(sh, psi):
+            lanes = slice(block * sh.width, (block + 1) * sh.width)
+            out_ref[group * sh.across + block] = rows[:, :, lanes]
+            skip = 1 if group == 0 else 0
+            up_ref[block, first - 1 + skip : first - 1 + sh.layers] = rows[skip:, :, lanes]
+            keep = sh.layers - (1 if group == sh.layered - 1 else 0)
+            down_ref[block, first : first + keep] = rows[:keep, :, lanes]
+    for block in range(sh.across):
+        lanes = slice(block * sh.width, (block + 1) * sh.width)
+        up_ref[block, sh.depth - 1] = v_ref[sh.depth - sh.slots :, lanes]
+        down_ref[block, sh.depth - 1] = v_ref[: sh.slots, lanes]
+
+
+def reorder(sh, psi, potential):
+    send = jax.ShapeDtypeStruct((sh.across, sh.depth, sh.slots, sh.width), jnp.float32)
     return pl.pallas_call(
         functools.partial(reorder_kernel, sh),
-        out_shape=jax.ShapeDtypeStruct((sh.owners, sh.layers, sh.slots, sh.width), jnp.float32),
-        compiler_params=params(),
+        out_shape=(
+            jax.ShapeDtypeStruct((sh.owners, sh.layers, sh.slots, sh.width), jnp.float32),
+            send,
+            send,
+        ),
+        compiler_params=params(14),
         name="reorder",
-    )(psi)
+    )(psi, potential)
 
 
 def odd_pairs(even, lane):
@@ -189,12 +204,12 @@
     return lax.broadcasted_iota(jnp.int32, (slots, LANES), 1) < LANES // 2
 
 
-def lane_pass(sh, source, matrices, targets, layers):
+def lane_pass(sh, source, at, matrices, targets, layers):
     def body(block, carry):
         parts = []
         for inner in range(sh.inner):
             rows = jnp.concatenate(
-                [source[sh.at(layer, block, inner)] for layer in range(layers)], 0
+                [source[at(layer, block, inner)] for layer in range(layers)], 0
             )
             high, low = split(rows)
             parts.append(jnp.concatenate([high, low], 1))
@@ -211,7 +226,7 @@
 
 
 def own_kernel(sh, c_ref, fwd_ref, kin_ref, w_out, kin_out, x_ref):
-    lane_pass(sh, c_ref, [fwd_ref, kin_ref], [x_ref, kin_out], sh.depth)
+    lane_pass(sh, c_ref, sh.at, [fwd_ref, kin_ref], [x_ref, kin_out], sh.depth)
     lane = half_mask(sh.slots)
 
     for group in range(sh.layered):
@@ -244,20 +259,21 @@
         functools.partial(own_kernel, sh),
         out_shape=(full, full),
         scratch_shapes=[pltpu.VMEM(full.shape, jnp.float32)],
-        compiler_params=params(),
+        compiler_params=params(16),
         cost_estimate=cost(10**10, 10**7),
         name="own_part",
     )(c, fwd, kin)
 
 
 def halo_kernel(
-    sh, lo_ref, c_ref, hi_ref, w_ref, kin_ref, vlo_ref, v_ref, vhi_ref, fwd_ref, bwd_ref,
-    out_ref, x_ref, wlo_ref, whi_ref,
+    sh, lo_ref, c_ref, hi_ref, w_ref, kin_ref, v_ref, fwd_ref, bwd_ref, out_ref,
+    x_ref, wlo_ref, whi_ref,
 ):
     lane = half_mask(sh.slots)
     depth = sh.depth
+    reach = depth - 1
     for side_ref, target in ((lo_ref, wlo_ref), (hi_ref, whi_ref)):
-        lane_pass(sh, side_ref, [fwd_ref], [x_ref], depth)
+        lane_pass(sh, side_ref, sh.side, [fwd_ref], [x_ref], reach)
 
         def filter_rows(layer, carry):
             even = [x_ref[layer, b] for b in range(sh.chunks)]
@@ -265,7 +281,7 @@
                 target[layer, b] = v
             return carry
 
-        lax.fori_loop(0, depth, filter_rows, 0)
+        lax.fori_loop(0, reach, filter_rows, 0)
 
     def along_z(block, carry):
         for inner in range(sh.inner):
@@ -273,16 +289,26 @@
             lanes = pl.ds(pl.multiple_of(chunk * LANES, LANES), LANES)
 
             def coeff(z):
-                ref = lo_ref if z < 0 else (c_ref if z < depth else hi_ref)
-                return ref[sh.at(z % depth, block, inner)]
+                if z < 0:
+                    return lo_ref[sh.side(z + reach, block, inner)]
+                if z < depth:
+                    return c_ref[sh.at(z, block, inner)]
+                return hi_ref[sh.side(z - depth, block, inner)]
 
             def mixed(z):
-                ref = wlo_ref if z < 0 else (w_ref if z < depth else whi_ref)
-                return ref[z % depth, chunk]
+                if z < 0:
+                    return wlo_ref[z + reach, chunk]
+                return w_ref[z, chunk] if z < depth else whi_ref[z - depth, chunk]
 
             def level(z):
-                ref = vlo_ref if z < 0 else (v_ref if z < depth else vhi_ref)
-                return jnp.broadcast_to(ref[pl.ds(z % depth, 1), lanes], (sh.slots, LANES))
+                part = slice(inner * LANES, (inner + 1) * LANES)
+                if z < 0:
+                    row = lo_ref[block, reach, z + sh.slots : z + sh.slots + 1, part]
+                elif z < depth:
+                    row = v_ref[z : z + 1, lanes]
+                else:
+                    row = hi_ref[block, reach, z - depth : z - depth + 1, part]
+                return jnp.broadcast_to(row, (sh.slots, LANES))
 
             values = {z: mixed(z) for z in range(-LOW - HIGH, depth + LOW + HIGH)}
             grid = {}
@@ -334,16 +360,16 @@
     lax.fori_loop(0, sh.across, finish, 0)
 
 
-def halo_part(sh, lo, c, hi, w, kin, v_lo, v, v_hi, fwd, bwd):
+def halo_part(sh, lo, c, hi, w, kin, v, fwd, bwd):
     full = pltpu.VMEM((sh.depth, sh.chunks, sh.slots, LANES), jnp.float32)
     return pl.pallas_call(
         functools.partial(halo_kernel, sh),
         out_shape=jax.ShapeDtypeStruct(c.shape, jnp.float32),
         scratch_shapes=[full] * 3,
-        compiler_params=params(),
+        compiler_params=params(26),
         cost_estimate=cost(3 * 10**10, 10**7),
         name="halo_part",
-    )(lo, c, hi, w, kin, v_lo, v, v_hi, fwd, bwd)
+    )(lo, c, hi, w, kin, v, fwd, bwd)
 
 
 def selection(slot_ref, count, slots_all):
@@ -386,7 +412,7 @@
     picked = lax.dot_general(
         rows, chosen, (((1,), (1,)), ((), ())), precision=highest,
         preferred_element_type=jnp.float32,
-    ) * (1.0 / sh.side**3)
+    ) * (1.0 / sh.box**3)
     picked = packed_rows(picked, fold)
     if len(out_ref.shape) == 2:
         out_ref[...] = picked
@@ -402,7 +428,7 @@
     return pl.pallas_call(
         functools.partial(gram_kernel, sh, fold),
         out_shape=jax.ShapeDtypeStruct(shape, jnp.float32),
-        compiler_params=params(),
+        compiler_params=params(16),
         cost_estimate=cost(10**9, 10**7),
         name="gram",
     )(c, a, slot)
@@ -461,7 +487,7 @@
             jax.ShapeDtypeStruct((count, count), jnp.float32),
             jax.ShapeDtypeStruct((count, LANES), jnp.float32),
         ),
-        compiler_params=params(),
+        compiler_params=params(16),
         cost_estimate=cost(10**9, 10**7),
         name="correct",
     )(c, a, slot, part)
@@ -485,6 +511,12 @@
             return keep_lo
         return keep_hi if tile >= tiles - edge_tiles else inverse
 
+    group = min(4, sh.chunks)
+    blank = jnp.zeros((rows + 2 * edge, LANES), jnp.float32)
+    for ref in (one_ref, two_ref):
+        ref[0] = blank
+        ref[sh.chunks + 1] = blank
+
     def gather(block, carry):
         for inner in range(sh.inner):
             chunk = block * sh.inner + inner
@@ -496,12 +528,7 @@
             for tile in range(tiles):
                 value = column[tile * 8 : (tile + 1) * 8]
                 res_ref[chunk, tile * 8 : (tile + 1) * 8] = value
-                one_ref[chunk, tile * 8 : (tile + 1) * 8] = value * scale(tile)
-            out_lanes = pl.ds(pl.multiple_of(chunk * LANES, LANES), LANES)
-            for orbital in range(own):
-                res_out[orbital, :, out_lanes] = res_ref[
-                    chunk, pl.ds(edge + orbital, sh.depth, stride=own), :
-                ]
+                one_ref[chunk + 1, tile * 8 : (tile + 1) * 8] = value * scale(tile)
         return carry
 
     lax.fori_loop(0, sh.across, gather, 0)
@@ -510,46 +537,45 @@
     lane = lax.broadcasted_iota(jnp.int32, (8, LANES), 1)
     upper = sub >= own
     right_half = lane >= LANES // 2
-    not_last = (lane % sh.side) != sh.side - 1
-    not_first = (lane % sh.side) != 0
-    half = 8 // own
-    assert half == 2
+    not_last = (lane % sh.box) != sh.box - 1
+    not_first = (lane % sh.box) != 0
+    assert 8 // own == 2
 
     def sweep(source, target, tile_list):
-        def body(chunk, carry):
-            before = jnp.maximum(chunk - 1, 0)
-            after = jnp.minimum(chunk + 1, sh.chunks - 1)
-            has_before = (chunk > 0).astype(jnp.float32)
-            has_after = (chunk < sh.chunks - 1).astype(jnp.float32)
-            for tile in tile_list:
-                here = pl.ds(tile * 8, 8)
-                value = source[chunk, here]
-                zero = jnp.zeros_like(value)
-                below = source[chunk, pl.ds(tile * 8 - 8, 8)] if tile > 0 else zero
-                above = source[chunk, pl.ds(tile * 8 + 8, 8)] if tile < tiles - 1 else zero
-                along_z = pltpu.roll(value + jnp.where(upper, below, above), own, 0)
-                along_y = pltpu.roll(
-                    value
-                    + jnp.where(
-                        right_half,
-                        source[before, here] * has_before,
-                        source[after, here] * has_after,
-                    ),
-                    LANES // 2,
-                    1,
-                )
-                along_x = pltpu.roll(jnp.where(not_last, value, 0.0), 1, 1) + pltpu.roll(
-                    jnp.where(not_first, value, 0.0), LANES - 1, 1
-                )
-                total = (
-                    res_ref[chunk, here]
-                    + coupling_xy * (along_y + along_x)
-                    + coupling_z * along_z
-                )
-                target[chunk, here] = total * scale(tile)
+        def body(step, carry):
+            seen = {}
+
+            def value_at(column, tile):
+                if not 0 <= tile < tiles:
+                    return jnp.zeros((8, LANES), jnp.float32)
+                if (column, tile) not in seen:
+                    seen[column, tile] = source[step * group + column + 1, pl.ds(tile * 8, 8)]
+                return seen[column, tile]
+
+            for column in range(group):
+                for tile in tile_list:
+                    here = pl.ds(tile * 8, 8)
+                    value = value_at(column, tile)
+                    beside = jnp.where(
+                        upper, value_at(column, tile - 1), value_at(column, tile + 1)
+                    )
+                    along_z = pltpu.roll(value + beside, own, 0)
+                    beside = jnp.where(
+                        right_half, value_at(column - 1, tile), value_at(column + 1, tile)
+                    )
+                    along_y = pltpu.roll(value + beside, LANES // 2, 1)
+                    along_x = pltpu.roll(jnp.where(not_last, value, 0.0), 1, 1) + pltpu.roll(
+                        jnp.where(not_first, value, 0.0), LANES - 1, 1
+                    )
+                    total = (
+                        res_ref[step * group + column, here]
+                        + coupling_xy * (along_y + along_x)
+                        + coupling_z * along_z
+                    )
+                    target[step * group + column + 1, here] = total * scale(tile)
             return carry
 
-        lax.fori_loop(0, sh.chunks, body, 0)
+        lax.fori_loop(0, sh.chunks // group, body, 0)
 
     source, target = one_ref, two_ref
     for done in range(1, SWEEPS + 1):
@@ -557,38 +583,34 @@
         sweep(source, target, range(first_tile, tiles - first_tile))
         source, target = target, source
 
-    def spread(chunk, carry):
-        out_lanes = pl.ds(pl.multiple_of(chunk * LANES, LANES), LANES)
-        for orbital in range(own):
-            dir_out[orbital, :, out_lanes] = source[
-                chunk, pl.ds(edge + orbital, sh.depth, stride=own), :
-            ]
+    def spread(step, carry):
+        for column in range(group):
+            chunk = step * group + column
+            out_lanes = pl.ds(pl.multiple_of(chunk * LANES, LANES), LANES)
+            for orbital in range(own):
+                here = pl.ds(edge + orbital, sh.depth, stride=own)
+                res_out[orbital, :, out_lanes] = res_ref[chunk, here, :]
+                dir_out[orbital, :, out_lanes] = source[chunk + 1, here, :]
         return carry
 
-    lax.fori_loop(0, sh.chunks, spread, 0)
+    lax.fori_loop(0, sh.chunks // group, spread, 0)
 
 
 def relax(sh, own, ends, r, lo, hi, inverse):
     rows = (sh.depth + 2 * SWEEPS) * own
     scratch = pltpu.VMEM((sh.chunks, rows, LANES), jnp.float32)
+    padded = pltpu.VMEM((sh.chunks + 2, rows, LANES), jnp.float32)
     out = jax.ShapeDtypeStruct((own, sh.depth, sh.plane), jnp.float32)
     vmem = pl.BlockSpec(memory_space=pltpu.VMEM)
     return pl.pallas_call(
         functools.partial(relax_kernel, sh, own),
         out_shape=(out, out),
         in_specs=[pl.BlockSpec(memory_space=pltpu.SMEM)] + [vmem] * 4,
-        scratch_shapes=[scratch] * 3,
-        compiler_params=params(),
+        scratch_shapes=[scratch, padded, padded],
+        compiler_params=params(14),
         cost_estimate=cost(10**9, 10**7),
         name="relax",
     )(ends, r, lo, hi, inverse)
-
-
-def exchange(value, axis):
-    count = lax.axis_size(axis)
-    forward = [(i, i + 1) for i in range(count - 1)]
-    backward = [(target, source) for source, target in forward]
-    return lax.ppermute(value, axis, forward), lax.ppermute(value, axis, backward)
 
 
 def to_all(value, axes):
@@ -602,16 +624,16 @@
     sh = Shape(slots, depth, plane, owners)
     count = orbital_slot.shape[0]
     own = count // owners
-    magic = banded(sh.side, sh.side, 0, 0, magic_weights(MTAPS), 1 - MTAPS // 2)
-    kinetic = banded(sh.side, sh.side, 0, 0, second_weights(KREACH), -KREACH)
+    magic = banded(sh.box, sh.box, 0, 0, magic_weights(MTAPS), 1 - MTAPS // 2)
+    kinetic = banded(sh.box, sh.box, 0, 0, second_weights(KREACH), -KREACH)
     fwd, bwd, kin = (jnp.asarray(two_part(m)) for m in (magic, magic.T, kinetic))
 
-    c = reorder(sh, psi)
+    c, up, down = reorder(sh, psi, potential)
+    lo = lax.ppermute(up, "box", [(i, i + 1) for i in range(boxes - 1)])
+    hi = lax.ppermute(down, "box", [(i + 1, i) for i in range(boxes - 1)])
     pieces = to_all(c, "orb")
-    lo, hi = exchange(c, "box")
-    v_lo, v_hi = exchange(potential, "box")
     w, kin_own = own_part(sh, c, fwd, kin)
-    applied = halo_part(sh, lo, c, hi, w, kin_own, v_lo, potential, v_hi, fwd, bwd)
+    applied = halo_part(sh, lo, c, hi, w, kin_own, potential, fwd, bwd)
     applied_pieces = to_all(applied, "orb")
 
     slot = orbital_slot.reshape(count, 1)

time: 201 us -> 186 us (0.925)
  Pallas kernels: 71 us -> 51.8 us
  waiting for transfers between devices: 57 us -> 64.8 us
  starting transfers between devices: 27.7 us -> 21.8 us
  local copies, waits for them, and re-layouts: 3.47 us -> 6.9 us
    pallas_call x1, Pallas kernels: 16.4 us -> 8.67 us  [relax(): pl.pallas_call(functools.partial(relax_kernel, sh, own), out_shape=(out,...]
    ppermute x4 -> x2, starting transfers between devices: 12 us -> 6.44 us  [the longest x1 4.52 us: local(): lo = lax.ppermute(up, 'box', [(i, i + 1) for i in range(boxes - 1)])]
    ppermute x4 -> x2, waiting for transfers between devices: 5.51 us -> 10.1 us  [the longest x1 5.49 us: local(): lo = lax.ppermute(up, 'box', [(i, i + 1) for i in range(boxes - 1)])]
    unnamed x16 -> x22, local copies, waits for them, and re-layouts: 2.74 us -> 6.78 us
    pallas_call x1, Pallas kernels: 30.6 us -> 26.6 us  [halo_part(): pl.pallas_call(functools.partial(halo_kernel, sh), out_shape=jax.ShapeDty...]
    pallas_call x1, Pallas kernels: 12.1 us -> 8.46 us  [own_part(): pl.pallas_call(functools.partial(own_kernel, sh), out_shape=(full, full),...]
    all_to_all x2, waiting for transfers between devices: 46.3 us -> 49.1 us  [to_all(): return lax.all_to_all(value, axes, split_axis=0, concat_axis=0, tiled=True)]
  transfers between devices with their start and end apart: 8 -> 6, of which waited for: 5 -> 6; matrix products, arithmetic and copies ran while one was open for 1% -> 0% of each run, Pallas kernels for 21% -> 19%
where the time goes in v1:
time: 186 us
  waiting for transfers between devices  64.8 us (35%)
  Pallas kernels  51.8 us (28%)
  blocking collectives  39.3 us (21%)
  starting transfers between devices  21.8 us (12%)
  local copies, waits for them, and re-layouts  6.9 us (4%)
    all_to_all x2, waiting for transfers between devices, to_all(): return lax.all_to_all(value, axes, split_axis=0, concat_axis=0, tiled=True)  49.1 us
    all_to_all x2, blocking collectives, to_all(): return lax.all_to_all(value, axes, split_axis=0, concat_axis=0, tiled=True)  39.3 us
    pallas_call x1, Pallas kernels, halo_part(): pl.pallas_call(functools.partial(halo_kernel, sh), out_shape=jax.ShapeDty...  26.6 us
    all_to_all x2, starting transfers between devices, to_all(): return lax.all_to_all(value, axes, split_axis=0, concat_axis=0, tiled=True)  10.4 us
    pallas_call x1, Pallas kernels, relax(): pl.pallas_call(functools.partial(relax_kernel, sh, own), out_shape=(out,...  8.67 us
    pallas_call x1, Pallas kernels, own_part(): pl.pallas_call(functools.partial(own_kernel, sh), out_shape=(full, full),...  8.46 us
    unnamed x22, local copies, waits for them, and re-layouts  6.78 us
    ppermute x1, waiting for transfers between devices, local(): lo = lax.ppermute(up, 'box', [(i, i + 1) for i in range(boxes - 1)])  5.49 us
  transfers between devices with their start and end apart: 6, of which 6 were waited for; matrix products, arithmetic and copies ran while one was open for 0% of the time, Pallas kernels for 19%

profile of v1, /device:TPU:1, one launch (start us, length us, event | category | flops | bytes accessed | tf_op | source)
XLA Modules:
  0.0 185.5 jit_solution(5939957469980167699)
XLA Ops:
  0.6 0.0 copy-start
  0.6 1.6 copy-done
  2.2 0.0 copy-start.5
  2.2 0.9 copy-done.5
  3.2 2.5 %reorder.1 = (f32[8,16,8,512]{3,2,1,0:T(8,128)S(1)}, f32[8,16,8,512]{3,2,1,0:T(8,128)}, f32[8,16,8,512]{3,2,1,0:T(8,128)}) custom-call(f32[8,16,4096]{2,1,0:T(8,128)S(1)} %copy-done, f32[16,4096]{1,0:T(8,128)S(1)} %copy-done.5), custom_call_target="tpu_custom_call" | custom-call | tf_op jit(solution)/shard_map/reorder/pallas_call | solution.py:143
  5.7 0.0 copy-start.1
  5.7 1.3 copy-done.1
  7.0 4.5 %collective-permute-start = (f32[8,16,8,512]{3,2,1,0:T(8,128)}, f32[8,16,8,512]{3,2,1,0:T(8,128)}, u32[]{:S(2)}, u32[]{:S(2)}) collective-permute-start(f32[8,16,8,512]{3,2,1,0:T(8,128)} %get-tuple-element.14), channel_id=1, source_target_pairs={{0,1},{1,2},{2,3},{4,5},{5,6},{6,7},{8,9},{9,10},{10,11},{12,13},{... | collective-permute-start | bytes 6291464 | tf_op jit(solution)/shard_map/ppermute | solution.py:632
  11.5 1.9 %collective-permute-start.1 = (f32[8,16,8,512]{3,2,1,0:T(8,128)}, f32[8,16,8,512]{3,2,1,0:T(8,128)}, u32[]{:S(2)}, u32[]{:S(2)}) collective-permute-start(f32[8,16,8,512]{3,2,1,0:T(8,128)} %get-tuple-element.15), channel_id=1, source_target_pairs={{1,0},{2,1},{3,2},{5,4},{6,5},{7,6},{9,8},{10,9},{11,10},{13,12},{... | collective-permute-start | bytes 6291464 | tf_op jit(solution)/shard_map/ppermute | solution.py:633
  13.4 0.0 copy-start.7
  13.5 0.0 copy-start.9
  13.5 5.7 %all-to-all-start = ((f32[8,16,8,512]{3,2,1,0:T(8,128)}), f32[8,16,8,512]{3,2,1,0:T(8,128)S(1)}, u32[]{:S(2)}, u32[]{:S(2)}) async-start(f32[8,16,8,512]{3,2,1,0:T(8,128)} %copy-done.1), calls=%async_computation | async-start | bytes 4194304 | tf_op jit(solution)/shard_map/all_to_all | solution.py:617
  19.2 0.0 copy-done.7
  19.2 0.0 copy-done.9
  19.2 0.0 copy-start.2
  19.2 1.6 copy-done.2
  20.8 0.0 copy-start.3
  20.8 0.0 copy-start.6
  20.8 0.0 copy-start.8
  20.8 8.5 %own_part.1 = (f32[16,32,8,128]{3,2,1,0:T(8,128)S(1)}, f32[16,32,8,128]{3,2,1,0:T(8,128)S(1)}) custom-call(f32[8,16,8,512]{3,2,1,0:T(8,128)S(1)} %copy-done.2, bf16[256,256]{1,0:T(8,128)(2,1)S(1)} %copy-done.7, bf16[256,256]{1,0:T(8,128)(2,1)S(1)} %copy-done.9), custom_call_target="tpu_custom_call" | custom-call | flops 10000000000 | bytes 10000000 | tf_op jit(solution)/shard_map/own_part/pallas_call | solution.py:258
  29.3 5.5 %collective-permute-done.lo_ref = f32[8,16,8,512]{3,2,1,0:T(8,128)} collective-permute-done((f32[8,16,8,512]{3,2,1,0:T(8,128)}, f32[8,16,8,512]{3,2,1,0:T(8,128)}, u32[]{:S(2)}, u32[]{:S(2)}) %collective-permute-start) | collective-permute-done | bytes 2097184 | tf_op jit(solution)/shard_map/ppermute | solution.py:632
  34.8 4.6 %collective-permute-done.1.hi_ref = f32[8,16,8,512]{3,2,1,0:T(8,128)} collective-permute-done((f32[8,16,8,512]{3,2,1,0:T(8,128)}, f32[8,16,8,512]{3,2,1,0:T(8,128)}, u32[]{:S(2)}, u32[]{:S(2)}) %collective-permute-start.1) | collective-permute-done | bytes 2097184 | tf_op jit(solution)/shard_map/ppermute | solution.py:633
  39.4 0.0 copy-done.3
  39.4 0.0 copy-done.6
  39.4 0.0 copy-done.8
  39.4 26.6 %halo_part.1 = f32[8,16,8,512]{3,2,1,0:T(8,128)S(1)} custom-call(f32[8,16,8,512]{3,2,1,0:T(8,128)} %collective-permute-done.lo_ref, f32[8,16,8,512]{3,2,1,0:T(8,128)S(1)} %copy-done.3, f32[8,16,8,512]{3,2,1,0:T(8,128)} %collective-permute-done.1.hi_ref, f32[16,32,8,128]{3,2,1,0:T(8,128)S(1)} %get-tuple-element.16.w_ref, ...), custom_call_target="tpu_custom_call" | custom-call | flops 30000001024 | bytes 10000000 | tf_op jit(solution)/shard_map/halo_part/pallas_call | solution.py:365
  66.0 0.0 copy-start.4
  66.0 1.3 copy-done.4
  67.3 0.0 copy-start.10
  67.3 0.8 all-to-all-done.c_ref
  68.1 4.6 %all-to-all-start.1 = ((f32[8,16,8,512]{3,2,1,0:T(8,128)}), f32[8,16,8,512]{3,2,1,0:T(8,128)}, u32[]{:S(2)}, u32[]{:S(2)}) async-start(f32[8,16,8,512]{3,2,1,0:T(8,128)} %copy-done.4), calls=%async_computation.1 | async-start | bytes 4194304 | tf_op jit(solution)/shard_map/all_to_all | solution.py:617
  72.8 0.0 copy-done.10
  72.8 0.1 copy.10.slot_ref
  72.8 48.2 %all-to-all-done.1.a_ref = f32[8,16,8,512]{3,2,1,0:T(8,128)} async-done(((f32[8,16,8,512]{3,2,1,0:T(8,128)}), f32[8,16,8,512]{3,2,1,0:T(8,128)}, u32[]{:S(2)}, u32[]{:S(2)}) %all-to-all-start.1) | async-done | bytes 2097184 | tf_op jit(solution)/shard_map/all_to_all | solution.py:617
  121.1 2.8 %gram.1 = f32[32,8,128]{2,1,0:T(8,128)S(1)} custom-call(f32[8,16,8,512]{3,2,1,0:T(8,128)S(1)} %all-to-all-done.c_ref, f32[8,16,8,512]{3,2,1,0:T(8,128)} %all-to-all-done.1.a_ref, s32[32,1]{1,0:T(8,128)S(1)} %copy.10.slot_ref), custom_call_target="tpu_custom_call" | custom-call | flops 1000000000 | bytes 10000000 | tf_op jit(solution)/shard_map/gram/pallas_call | solution.py:428
  123.9 11.4 %all_to_all.20.part_ref = f32[32,8,128]{2,1,0:T(8,128)S(1)} all-to-all(f32[32,8,128]{2,1,0:T(8,128)S(1)} %gram.1), channel_id=1, replica_groups=mesh['orb'=8,'box'=4] {'orb','box'}, dimensions={0} | all-to-all | bytes 262144 | tf_op jit(solution)/shard_map/all_to_all | solution.py:617
  135.3 2.8 %correct.1 = (f32[8,64,512]{2,1,0:T(8,128)S(1)}, f32[32,32]{1,0:T(8,128)}, f32[32,128]{1,0:T(8,128)S(1)}) custom-call(f32[8,16,8,512]{3,2,1,0:T(8,128)S(1)} %all-to-all-done.c_ref, f32[8,16,8,512]{3,2,1,0:T(8,128)} %all-to-all-done.1.a_ref, s32[32,1]{1,0:T(8,128)S(1)} %copy.10.slot_ref, f32[32,8,128]{2,1,0:T(8,128)S(1)} %all_to_all.20.part_ref), custom_call_target="tpu_custom_call" | custom-call | flops 1000000000 | bytes 10000000 | tf_op jit(solution)/shard_map/correct/pallas_call | solution.py:483
  138.1 27.9 %all_to_all.21.r_ref = f32[8,64,512]{2,1,0:T(8,128)S(1)} all-to-all(f32[8,64,512]{2,1,0:T(8,128)S(1)} %get-tuple-element.18), channel_id=1, replica_groups=mesh['orb'=8,'box'=4] {'orb'}, dimensions={0} | all-to-all | bytes 2097152 | tf_op jit(solution)/shard_map/all_to_all | solution.py:617
  166.0 3.1 %collective-permute-start.2 = (f32[8,16,512]{2,1,0:T(8,128)S(1)}, f32[8,16,512]{2,1,0:T(8,128)S(1)}, u32[]{:S(2)}, u32[]{:S(2)}) collective-permute-start(f32[8,16,512]{2,1,0:T(8,128)S(1)} %get-tuple-element.24), channel_id=1, source_target_pairs={{0,1},{1,2},{2,3},{4,5},{5,6},{6,7},{8,9},{9,10},{10,11},{12,13},{... | collective-permute-start | bytes 786440 | tf_op jit(solution)/shard_map/ppermute | solution.py:649
  169.1 1.9 %collective-permute-start.3 = (f32[8,16,512]{2,1,0:T(8,128)S(1)}, f32[8,16,512]{2,1,0:T(8,128)S(1)}, u32[]{:S(2)}, u32[]{:S(2)}) collective-permute-start(f32[8,16,512]{2,1,0:T(8,128)S(1)} %get-tuple-element.23), channel_id=1, source_target_pairs={{1,0},{2,1},{3,2},{5,4},{6,5},{7,6},{9,8},{10,9},{11,10},{13,12},{... | collective-permute-start | bytes 786440 | tf_op jit(solution)/shard_map/ppermute | solution.py:652
  171.1 0.1 pad_add_fusion.ends_ref
  171.2 1.3 collective-permute-done.2.lo_ref
  172.4 4.4 %collective-permute-done.3.hi_ref = f32[8,16,512]{2,1,0:T(8,128)S(1)} collective-permute-done((f32[8,16,512]{2,1,0:T(8,128)S(1)}, f32[8,16,512]{2,1,0:T(8,128)S(1)}, u32[]{:S(2)}, u32[]{:S(2)}) %collective-permute-start.3) | collective-permute-done | bytes 262176 | tf_op jit(solution)/shard_map/ppermute | solution.py:652
  176.8 8.7 %relax.1 = (f32[4,16,4096]{2,1,0:T(8,128)}, f32[4,16,4096]{2,1,0:T(8,128)}) custom-call(s32[3]{0:T(128)S(1)} %pad_add_fusion.ends_ref, f32[8,64,512]{2,1,0:T(8,128)S(1)} %all_to_all.21.r_ref, f32[8,16,512]{2,1,0:T(8,128)S(1)} %collective-permute-done.2.lo_ref, f32[8,16,512]{2,1,0:T(8,128)S(1)} %collective-permute-done.3.hi_ref, ...), custom_call_target="tpu_custom_call" | custom-call | flops 1000000000 | bytes 10000000 | tf_op jit(solution)/shard_map/relax/pallas_call | solution.py:605
  (1 shorter events, 0.0 us)
Async XLA Ops:
  0.6 1.6 copy-start
  2.2 0.9 copy-start.5
  5.7 1.3 copy-start.1
  7.0 27.8 %collective-permute-start = (f32[8,16,8,512]{3,2,1,0:T(8,128)}, f32[8,16,8,512]{3,2,1,0:T(8,128)}, u32[]{:S(2)}, u32[]{:S(2)}) collective-permute-start(f32[8,16,8,512]{3,2,1,0:T(8,128)} %get-tuple-element.14), channel_id=1, source_target_pairs={{0,1},{1,2},{2,3},{4,5},{5,6},{6,7},{8,9},{9,10},{10,11},{12,13},{... | collective-permute-start | bytes 6291464 | tf_op jit(solution)/shard_map/ppermute | solution.py:632
  11.5 27.9 %collective-permute-start.1 = (f32[8,16,8,512]{3,2,1,0:T(8,128)}, f32[8,16,8,512]{3,2,1,0:T(8,128)}, u32[]{:S(2)}, u32[]{:S(2)}) collective-permute-start(f32[8,16,8,512]{3,2,1,0:T(8,128)} %get-tuple-element.15), channel_id=1, source_target_pairs={{1,0},{2,1},{3,2},{5,4},{6,5},{7,6},{9,8},{10,9},{11,10},{13,12},{... | collective-permute-start | bytes 6291464 | tf_op jit(solution)/shard_map/ppermute | solution.py:633
  13.4 5.8 %copy-start.7 = (bf16[256,256]{1,0:T(8,128)(2,1)S(1)}, bf16[256,256]{1,0:T(8,128)(2,1)}, u32[]{:S(2)}) copy-start(bf16[256,256]{1,0:T(8,128)(2,1)} %constant.19.clone.fwd_ref) | copy-start | bytes 393220
  13.5 5.7 %copy-start.9 = (bf16[256,256]{1,0:T(8,128)(2,1)S(1)}, bf16[256,256]{1,0:T(8,128)(2,1)}, u32[]{:S(2)}) copy-start(bf16[256,256]{1,0:T(8,128)(2,1)} %constant.21.clone.kin_ref) | copy-start | bytes 393220
  13.5 54.7 %all-to-all-start = ((f32[8,16,8,512]{3,2,1,0:T(8,128)}), f32[8,16,8,512]{3,2,1,0:T(8,128)S(1)}, u32[]{:S(2)}, u32[]{:S(2)}) async-start(f32[8,16,8,512]{3,2,1,0:T(8,128)} %copy-done.1), calls=%async_computation | async-start | bytes 4194304 | tf_op jit(solution)/shard_map/all_to_all | solution.py:617
  19.2 1.6 copy-start.2
  20.8 18.6 %copy-start.3 = (f32[8,16,8,512]{3,2,1,0:T(8,128)S(1)}, f32[8,16,8,512]{3,2,1,0:T(8,128)}, u32[]{:S(2)}) copy-start(f32[8,16,8,512]{3,2,1,0:T(8,128)} %copy-done.1) | copy-start | bytes 6291460
  20.8 18.6 %copy-start.6 = (f32[16,4096]{1,0:T(8,128)S(1)}, f32[16,4096]{1,0:T(8,128)}, u32[]{:S(2)}) copy-start(f32[16,4096]{1,0:T(8,128)} %v_ref.3) | copy-start | bytes 786436
  20.8 18.6 %copy-start.8 = (bf16[256,256]{1,0:T(8,128)(2,1)S(1)}, bf16[256,256]{1,0:T(8,128)(2,1)}, u32[]{:S(2)}) copy-start(bf16[256,256]{1,0:T(8,128)(2,1)} %constant.20.clone.bwd_ref) | copy-start | bytes 393220
  66.0 1.3 copy-start.4
  67.3 5.5 %copy-start.10 = (s32[32]{0:T(128)S(1)}, s32[32]{0:T(128)}, u32[]{:S(2)}) copy-start(s32[32]{0:T(128)} %param.8) | copy-start | bytes 388
  68.1 52.9 %all-to-all-start.1 = ((f32[8,16,8,512]{3,2,1,0:T(8,128)}), f32[8,16,8,512]{3,2,1,0:T(8,128)}, u32[]{:S(2)}, u32[]{:S(2)}) async-start(f32[8,16,8,512]{3,2,1,0:T(8,128)} %copy-done.4), calls=%async_computation.1 | async-start | bytes 4194304 | tf_op jit(solution)/shard_map/all_to_all | solution.py:617
  166.0 6.4 %collective-permute-start.2 = (f32[8,16,512]{2,1,0:T(8,128)S(1)}, f32[8,16,512]{2,1,0:T(8,128)S(1)}, u32[]{:S(2)}, u32[]{:S(2)}) collective-permute-start(f32[8,16,512]{2,1,0:T(8,128)S(1)} %get-tuple-element.24), channel_id=1, source_target_pairs={{0,1},{1,2},{2,3},{4,5},{5,6},{6,7},{8,9},{9,10},{10,11},{12,13},{... | collective-permute-start | bytes 786440 | tf_op jit(solution)/shard_map/ppermute | solution.py:649
  169.1 7.7 %collective-permute-start.3 = (f32[8,16,512]{2,1,0:T(8,128)S(1)}, f32[8,16,512]{2,1,0:T(8,128)S(1)}, u32[]{:S(2)}, u32[]{:S(2)}) collective-permute-start(f32[8,16,512]{2,1,0:T(8,128)S(1)} %get-tuple-element.23), channel_id=1, source_target_pairs={{1,0},{2,1},{3,2},{5,4},{6,5},{7,6},{9,8},{10,9},{11,10},{13,12},{... | collective-permute-start | bytes 786440 | tf_op jit(solution)/shard_map/ppermute | solution.py:652

commit v2 on v1

--- a/solution.py
+++ b/solution.py
@@ -117,39 +117,58 @@
         lanes = slice(inner * LANES, (inner + 1) * LANES)
         return piece, layer % self.layers, slice(None), lanes
 
-    def side(self, layer, block, inner):
-        return block, layer, slice(None), slice(inner * LANES, (inner + 1) * LANES)
-
-
-def reorder_kernel(sh, psi_ref, v_ref, out_ref, up_ref, down_ref):
-    for group in range(sh.layered):
-        first = group * sh.layers
-        rows = jnp.transpose(psi_ref[:, first : first + sh.layers, :], (1, 0, 2))
-        for block in range(sh.across):
-            lanes = slice(block * sh.width, (block + 1) * sh.width)
-            out_ref[group * sh.across + block] = rows[:, :, lanes]
-            skip = 1 if group == 0 else 0
-            up_ref[block, first - 1 + skip : first - 1 + sh.layers] = rows[skip:, :, lanes]
-            keep = sh.layers - (1 if group == sh.layered - 1 else 0)
-            down_ref[block, first : first + keep] = rows[:keep, :, lanes]
-    for block in range(sh.across):
-        lanes = slice(block * sh.width, (block + 1) * sh.width)
-        up_ref[block, sh.depth - 1] = v_ref[sh.depth - sh.slots :, lanes]
-        down_ref[block, sh.depth - 1] = v_ref[: sh.slots, lanes]
-
-
-def reorder(sh, psi, potential):
-    send = jax.ShapeDtypeStruct((sh.across, sh.depth, sh.slots, sh.width), jnp.float32)
+
+def pack_kernel(sh, psi_hbm, out_hbm, buffer, sems_in, sems_out):
+    def pair(index):
+        first = (index // sh.across) * sh.layers
+        lane = (index % sh.across) * sh.width
+        source = psi_hbm.at[:, pl.ds(first, sh.layers), pl.ds(lane, sh.width)]
+        return (
+            pltpu.make_async_copy(source, buffer.at[index], sems_in.at[index]),
+            pltpu.make_async_copy(buffer.at[index], out_hbm.at[index], sems_out.at[index]),
+        )
+
+    copies = [pair(index) for index in range(sh.owners)]
+    for arrive, leave in copies:
+        arrive.start()
+    for arrive, leave in copies:
+        arrive.wait()
+        leave.start()
+    for arrive, leave in copies:
+        leave.wait()
+
+
+def pack(sh, psi):
+    shape = (sh.owners, sh.slots, sh.layers, sh.width)
     return pl.pallas_call(
-        functools.partial(reorder_kernel, sh),
-        out_shape=(
-            jax.ShapeDtypeStruct((sh.owners, sh.layers, sh.slots, sh.width), jnp.float32),
-            send,
-            send,
-        ),
-        compiler_params=params(14),
-        name="reorder",
-    )(psi, potential)
+        functools.partial(pack_kernel, sh),
+        out_shape=pltpu.HBM(shape, jnp.float32),
+        in_specs=[pl.BlockSpec(memory_space=pltpu.HBM)],
+        out_specs=pl.BlockSpec(memory_space=pltpu.HBM),
+        scratch_shapes=[
+            pltpu.VMEM(shape, jnp.float32),
+            pltpu.SemaphoreType.DMA((sh.owners,)),
+            pltpu.SemaphoreType.DMA((sh.owners,)),
+        ],
+        compiler_params=params(8),
+        cost_estimate=cost(0, 2 * psi.size * 4),
+        name="pack",
+    )(pltpu.with_memory_space_constraint(psi, pltpu.HBM))
+
+
+def turn_kernel(sh, in_ref, out_ref):
+    for index in range(sh.owners):
+        out_ref[index] = jnp.transpose(in_ref[index], (1, 0, 2))
+
+
+def turn(sh, pieces):
+    return pl.pallas_call(
+        functools.partial(turn_kernel, sh),
+        out_shape=pltpu.VMEM((sh.owners, sh.layers, sh.slots, sh.width), jnp.float32),
+        compiler_params=params(10),
+        cost_estimate=cost(10**8, 2 * pieces.size * 4),
+        name="turn",
+    )(pltpu.with_memory_space_constraint(pieces, pltpu.HBM))
 
 
 def odd_pairs(even, lane):
@@ -204,76 +223,79 @@
     return lax.broadcasted_iota(jnp.int32, (slots, LANES), 1) < LANES // 2
 
 
-def lane_pass(sh, source, at, matrices, targets, layers):
+def lane_pass(sh, slab, kept, matrices, targets):
+    depth = sh.depth
+
     def body(block, carry):
         parts = []
         for inner in range(sh.inner):
-            rows = jnp.concatenate(
-                [source[at(layer, block, inner)] for layer in range(layers)], 0
-            )
-            high, low = split(rows)
+            chunk = block * sh.inner + inner
+            lanes = pl.ds(pl.multiple_of(chunk * LANES, LANES), LANES)
+            rows = jnp.transpose(slab[:, :, lanes], (1, 0, 2))
+            for layer in range(depth):
+                kept[layer, chunk] = rows[layer]
+            high, low = split(rows.reshape(depth * sh.slots, LANES))
             parts.append(jnp.concatenate([high, low], 1))
         parts = jnp.concatenate(parts, 0)
         for matrix, target in zip(matrices, targets):
             result = lane_product(parts, matrix[...])
-            result = result.reshape(sh.inner, layers, sh.slots, LANES)
+            result = result.reshape(sh.inner, depth, sh.slots, LANES)
             for inner in range(sh.inner):
-                for layer in range(layers):
+                for layer in range(depth):
                     target[layer, block * sh.inner + inner] = result[inner, layer]
         return carry
 
     lax.fori_loop(0, sh.across, body, 0)
 
 
-def own_kernel(sh, c_ref, fwd_ref, kin_ref, w_out, kin_out, x_ref):
-    lane_pass(sh, c_ref, sh.at, [fwd_ref, kin_ref], [x_ref, kin_out], sh.depth)
+def own_kernel(sh, psi_ref, fwd_ref, kin_ref, c_out, w_out, kin_out, x_ref):
+    lane_pass(sh, psi_ref, c_out, [fwd_ref, kin_ref], [x_ref, kin_out])
     lane = half_mask(sh.slots)
 
-    for group in range(sh.layered):
-
-        def body(i, carry):
-            layer = group * sh.layers + i
-            even = [x_ref[layer, b] for b in range(sh.chunks)]
-            for b, v in enumerate(row_filter(even, odd_pairs(even, lane), MAGIC)):
-                w_out[layer, b] = v
-            even = [
-                c_ref[
-                    group * sh.across + b // sh.inner,
-                    i,
-                    :,
-                    (b % sh.inner) * LANES : (b % sh.inner + 1) * LANES,
-                ]
-                for b in range(sh.chunks)
-            ]
-            sums = row_filter_even(even, odd_pairs(even, lane), KINETIC, KREACH)
-            for b, v in enumerate(sums):
-                kin_out[layer, b] += v
-            return carry
-
-        lax.fori_loop(0, sh.layers, body, 0)
-
-
-def own_part(sh, c, fwd, kin):
+    def body(layer, carry):
+        even = [x_ref[layer, b] for b in range(sh.chunks)]
+        for b, v in enumerate(row_filter(even, odd_pairs(even, lane), MAGIC)):
+            w_out[layer, b] = v
+        even = [c_out[layer, b] for b in range(sh.chunks)]
+        sums = row_filter_even(even, odd_pairs(even, lane), KINETIC, KREACH)
+        for b, v in enumerate(sums):
+            kin_out[layer, b] += v
+        return carry
+
+    lax.fori_loop(0, sh.depth, body, 0)
+
+
+def own_part(sh, psi, fwd, kin):
     full = jax.ShapeDtypeStruct((sh.depth, sh.chunks, sh.slots, LANES), jnp.float32)
     return pl.pallas_call(
         functools.partial(own_kernel, sh),
-        out_shape=(full, full),
+        out_shape=(full, full, full),
         scratch_shapes=[pltpu.VMEM(full.shape, jnp.float32)],
-        compiler_params=params(16),
+        compiler_params=params(14),
         cost_estimate=cost(10**10, 10**7),
         name="own_part",
-    )(c, fwd, kin)
+    )(psi, fwd, kin)
 
 
 def halo_kernel(
-    sh, lo_ref, c_ref, hi_ref, w_ref, kin_ref, v_ref, fwd_ref, bwd_ref, out_ref,
-    x_ref, wlo_ref, whi_ref,
+    sh, lo_hbm, hi_hbm, c_ref, w_ref, kin_ref, vlo_ref, v_ref, vhi_ref, fwd_ref, bwd_ref,
+    out_hbm, lo_ref, hi_ref, clo_ref, chi_ref, x_ref, wlo_ref, whi_ref, out_ref, sems, in_sems,
 ):
     lane = half_mask(sh.slots)
     depth = sh.depth
     reach = depth - 1
-    for side_ref, target in ((lo_ref, wlo_ref), (hi_ref, whi_ref)):
-        lane_pass(sh, side_ref, sh.side, [fwd_ref], [x_ref], reach)
+    arrivals = [
+        pltpu.make_async_copy(lo_hbm, lo_ref, in_sems.at[0]),
+        pltpu.make_async_copy(hi_hbm, hi_ref, in_sems.at[1]),
+    ]
+    for copy in arrivals:
+        copy.start()
+    for copy, side_ref, kept, target, first in (
+        (arrivals[0], lo_ref, clo_ref, wlo_ref, 1),
+        (arrivals[1], hi_ref, chi_ref, whi_ref, 0),
+    ):
+        copy.wait()
+        lane_pass(sh, side_ref, kept, [fwd_ref], [x_ref])
 
         def filter_rows(layer, carry):
             even = [x_ref[layer, b] for b in range(sh.chunks)]
@@ -281,58 +303,44 @@
                 target[layer, b] = v
             return carry
 
-        lax.fori_loop(0, reach, filter_rows, 0)
-
-    def along_z(block, carry):
-        for inner in range(sh.inner):
-            chunk = block * sh.inner + inner
-            lanes = pl.ds(pl.multiple_of(chunk * LANES, LANES), LANES)
-
-            def coeff(z):
-                if z < 0:
-                    return lo_ref[sh.side(z + reach, block, inner)]
-                if z < depth:
-                    return c_ref[sh.at(z, block, inner)]
-                return hi_ref[sh.side(z - depth, block, inner)]
-
-            def mixed(z):
-                if z < 0:
-                    return wlo_ref[z + reach, chunk]
-                return w_ref[z, chunk] if z < depth else whi_ref[z - depth, chunk]
-
-            def level(z):
-                part = slice(inner * LANES, (inner + 1) * LANES)
-                if z < 0:
-                    row = lo_ref[block, reach, z + sh.slots : z + sh.slots + 1, part]
-                elif z < depth:
-                    row = v_ref[z : z + 1, lanes]
-                else:
-                    row = hi_ref[block, reach, z - depth : z - depth + 1, part]
-                return jnp.broadcast_to(row, (sh.slots, LANES))
-
-            values = {z: mixed(z) for z in range(-LOW - HIGH, depth + LOW + HIGH)}
-            grid = {}
-            for p in range(-LOW, depth + HIGH):
-                total = None
-                for k, w in MAGIC.items():
-                    term = values[p + k] * w
-                    total = term if total is None else total + term
-                grid[p] = total * level(p)
-            for q in range(depth):
-                total = None
-                for k, w in MAGIC.items():
-                    term = grid[q - k] * w
-                    total = term if total is None else total + term
-                x_ref[q, chunk] = total
-            cs = {z: coeff(z) for z in range(-KREACH, depth + KREACH)}
-            for q in range(depth):
-                total = kin_ref[q, chunk] + cs[q] * KINETIC[0]
-                for d in range(1, KREACH + 1):
-                    total = total + (cs[q + d] + cs[q - d]) * KINETIC[d]
-                whi_ref[q, chunk] = total
+        lax.fori_loop(first, first + reach, filter_rows, 0)
+
+    def along_z(chunk, carry):
+        lanes = pl.ds(pl.multiple_of(chunk * LANES, LANES), LANES)
+
+        def pick(below, here, above, z):
+            ref = below if z < 0 else (here if z < depth else above)
+            return ref[z % depth, chunk]
+
+        def level(z):
+            ref = vlo_ref if z < 0 else (v_ref if z < depth else vhi_ref)
+            return jnp.broadcast_to(ref[z % depth : z % depth + 1, lanes], (sh.slots, LANES))
+
+        values = {
+            z: pick(wlo_ref, w_ref, whi_ref, z) for z in range(-LOW - HIGH, depth + LOW + HIGH)
+        }
+        grid = {}
+        for p in range(-LOW, depth + HIGH):
+            total = None
+            for k, w in MAGIC.items():
+                term = values[p + k] * w
+                total = term if total is None else total + term
+            grid[p] = total * level(p)
+        for q in range(depth):
+            total = None
+            for k, w in MAGIC.items():
+                term = grid[q - k] * w
+                total = term if total is None else total + term
+            x_ref[q, chunk] = total
+        cs = {z: pick(clo_ref, c_ref, chi_ref, z) for z in range(-KREACH, depth + KREACH)}
+        for q in range(depth):
+            total = kin_ref[q, chunk] + cs[q] * KINETIC[0]
+            for d in range(1, KREACH + 1):
+                total = total + (cs[q + d] + cs[q - d]) * KINETIC[d]
+            whi_ref[q, chunk] = total
         return carry
 
-    lax.fori_loop(0, sh.across, along_z, 0)
+    lax.fori_loop(0, sh.chunks, along_z, 0)
 
     def filter_back(layer, carry):
         even = [x_ref[layer, b] for b in range(sh.chunks)]
@@ -341,6 +349,9 @@
         return carry
 
     lax.fori_loop(0, depth, filter_back, 0)
+
+    def piece(index):
+        return pltpu.make_async_copy(out_ref.at[index], out_hbm.at[index], sems.at[index])
 
     def finish(block, carry):
         parts = []
@@ -355,21 +366,37 @@
             chunk = block * sh.inner + inner
             for layer in range(depth):
                 out_ref[sh.at(layer, block, inner)] = result[inner, layer] + whi_ref[layer, chunk]
+        for group in range(sh.layered):
+            piece(group * sh.across + block).start()
         return carry
 
     lax.fori_loop(0, sh.across, finish, 0)
-
-
-def halo_part(sh, lo, c, hi, w, kin, v, fwd, bwd):
+    for index in range(sh.owners):
+        piece(index).wait()
+
+
+def halo_part(sh, lo, hi, c, w, kin, v_lo, v, v_hi, fwd, bwd):
     full = pltpu.VMEM((sh.depth, sh.chunks, sh.slots, LANES), jnp.float32)
+    out = (sh.owners, sh.layers, sh.slots, sh.width)
+    hbm = pl.BlockSpec(memory_space=pltpu.HBM)
+    vmem = pl.BlockSpec(memory_space=pltpu.VMEM)
+    lo, hi = (pltpu.with_memory_space_constraint(x, pltpu.HBM) for x in (lo, hi))
     return pl.pallas_call(
         functools.partial(halo_kernel, sh),
-        out_shape=jax.ShapeDtypeStruct(c.shape, jnp.float32),
-        scratch_shapes=[full] * 3,
+        out_shape=pltpu.HBM(out, jnp.float32),
+        in_specs=[hbm] * 2 + [vmem] * 8,
+        out_specs=hbm,
+        scratch_shapes=[pltpu.VMEM(lo.shape, jnp.float32)] * 2
+        + [full] * 5
+        + [
+            pltpu.VMEM(out, jnp.float32),
+            pltpu.SemaphoreType.DMA((sh.owners,)),
+            pltpu.SemaphoreType.DMA((2,)),
+        ],
         compiler_params=params(26),
         cost_estimate=cost(3 * 10**10, 10**7),
         name="halo_part",
-    )(lo, c, hi, w, kin, v, fwd, bwd)
+    )(lo, hi, c, w, kin, v_lo, v, v_hi, fwd, bwd)
 
 
 def selection(slot_ref, count, slots_all):
@@ -434,7 +461,8 @@
     )(c, a, slot)
 
 
-def correct_kernel(sh, fold, own, c_ref, a_ref, slot_ref, part_ref, out_ref, mult_ref, inv_ref):
+def correct_kernel(sh, fold, own, parts, c_ref, a_ref, slot_ref, part_ref, *outs):
+    *out_refs, mult_ref, inv_ref = outs
     total_slots = sh.owners * sh.slots
     count = slot_ref.shape[0]
     packed = part_ref[...]
@@ -462,28 +490,32 @@
         0,
     )
 
-    def body(layer):
+    def body(layer, place, out_ref):
         a_rows = split(a_ref[:, layer].reshape(total_slots, sh.width))
         c_rows = split(c_ref[:, layer].reshape(total_slots, sh.width))
         data = jnp.concatenate([a_rows[0], c_rows[0], a_rows[1], c_rows[1]], 0)
         both = jnp.dot(weights, data, preferred_element_type=jnp.float32)
         result = both[:count] + both[count:]
         for owner in range(sh.owners):
-            out_ref[owner, layer * own : (layer + 1) * own] = result[
+            out_ref[owner, place * own : (place + 1) * own] = result[
                 owner * own : (owner + 1) * own
             ]
 
-    for layer in range(sh.layers):
-        body(layer)
-
-
-def correct(sh, c, a, slot, part, fold):
+    for part, out_ref in zip(parts, out_refs):
+        for place, layer in enumerate(part):
+            body(layer, place, out_ref)
+
+
+def correct(sh, c, a, slot, part, fold, parts):
     count = slot.shape[0]
     own = count // sh.owners
     return pl.pallas_call(
-        functools.partial(correct_kernel, sh, fold, own),
-        out_shape=(
-            jax.ShapeDtypeStruct((sh.owners, sh.layers * own, sh.width), jnp.float32),
+        functools.partial(correct_kernel, sh, fold, own, parts),
+        out_shape=tuple(
+            jax.ShapeDtypeStruct((sh.owners, len(layers) * own, sh.width), jnp.float32)
+            for layers in parts
+        )
+        + (
             jax.ShapeDtypeStruct((count, count), jnp.float32),
             jax.ShapeDtypeStruct((count, LANES), jnp.float32),
         ),
@@ -493,9 +525,10 @@
     )(c, a, slot, part)
 
 
-def relax_kernel(
-    sh, own, ends_ref, r_ref, lo_ref, hi_ref, inv_ref, res_out, dir_out, res_ref, one_ref, two_ref
-):
+def relax_kernel(sh, own, parts, ends_ref, *refs):
+    r_refs = refs[: len(parts)]
+    lo_ref, hi_ref, inv_ref, res_out, dir_out, res_ref, one_ref, two_ref = refs[len(parts) :]
+    places = {layer: (ref, i) for part, ref in zip(parts, r_refs) for i, layer in enumerate(part)}
     rows = sh.depth * own
     edge = SWEEPS * own
     first = pl.multiple_of(ends_ref[0] * own, own)
@@ -522,7 +555,10 @@
             chunk = block * sh.inner + inner
             lanes = slice(inner * LANES, (inner + 1) * LANES)
             pieces = [lo_ref[block, :, lanes]]
-            pieces += [r_ref[g * sh.across + block, :, lanes] for g in range(sh.layered)]
+            for g in range(sh.layered):
+                for layer in range(sh.layers):
+                    ref, i = places[layer]
+                    pieces.append(ref[g * sh.across + block, i * own : (i + 1) * own, lanes])
             pieces += [hi_ref[block, :, lanes]]
             column = jnp.concatenate(pieces, 0)
             for tile in range(tiles):
@@ -596,21 +632,21 @@
     lax.fori_loop(0, sh.chunks // group, spread, 0)
 
 
-def relax(sh, own, ends, r, lo, hi, inverse):
+def relax(sh, own, parts, ends, pieces, lo, hi, inverse):
     rows = (sh.depth + 2 * SWEEPS) * own
     scratch = pltpu.VMEM((sh.chunks, rows, LANES), jnp.float32)
     padded = pltpu.VMEM((sh.chunks + 2, rows, LANES), jnp.float32)
     out = jax.ShapeDtypeStruct((own, sh.depth, sh.plane), jnp.float32)
     vmem = pl.BlockSpec(memory_space=pltpu.VMEM)
     return pl.pallas_call(
-        functools.partial(relax_kernel, sh, own),
+        functools.partial(relax_kernel, sh, own, parts),
         out_shape=(out, out),
-        in_specs=[pl.BlockSpec(memory_space=pltpu.SMEM)] + [vmem] * 4,
+        in_specs=[pl.BlockSpec(memory_space=pltpu.SMEM)] + [vmem] * (3 + len(parts)),
         scratch_shapes=[scratch, padded, padded],
         compiler_params=params(14),
         cost_estimate=cost(10**9, 10**7),
         name="relax",
-    )(ends, r, lo, hi, inverse)
+    )(ends, *pieces, lo, hi, inverse)
 
 
 def to_all(value, axes):
@@ -628,12 +664,16 @@
     kinetic = banded(sh.box, sh.box, 0, 0, second_weights(KREACH), -KREACH)
     fwd, bwd, kin = (jnp.asarray(two_part(m)) for m in (magic, magic.T, kinetic))
 
-    c, up, down = reorder(sh, psi, potential)
-    lo = lax.ppermute(up, "box", [(i, i + 1) for i in range(boxes - 1)])
-    hi = lax.ppermute(down, "box", [(i + 1, i) for i in range(boxes - 1)])
-    pieces = to_all(c, "orb")
-    w, kin_own = own_part(sh, c, fwd, kin)
-    applied = halo_part(sh, lo, c, hi, w, kin_own, potential, fwd, bwd)
+    upward = [(i, i + 1) for i in range(boxes - 1)]
+    downward = [(i + 1, i) for i in range(boxes - 1)]
+    lo = lax.ppermute(psi, "box", upward)
+    hi = lax.ppermute(psi, "box", downward)
+    pieces = turn(sh, to_all(pack(sh, psi), "orb"))
+    c, w, kin_own = own_part(sh, psi, fwd, kin)
+    w, sent = lax.optimization_barrier((w, potential))
+    v_lo = lax.ppermute(sent, "box", upward)
+    v_hi = lax.ppermute(sent, "box", downward)
+    applied = halo_part(sh, lo, hi, c, w, kin_own, v_lo, potential, v_hi, fwd, bwd)
     applied_pieces = to_all(applied, "orb")
 
     slot = orbital_slot.reshape(count, 1)
@@ -642,20 +682,31 @@
     copies = devices if devices * count * count <= 1 << 20 else 0
     part = gram(sh, pieces, applied_pieces, slot, fold, copies)
     part = to_all(part, ("orb", "box")) if copies else lax.psum(part, ("orb", "box"))
-    corrected, multipliers, inverse = correct(sh, pieces, applied_pieces, slot, part, fold)
-    returned = to_all(corrected, "orb")
+    if sh.layered == 1 and depth > 2 * SWEEPS:
+        parts = (
+            tuple(range(SWEEPS)) + tuple(range(depth - SWEEPS, depth)),
+            tuple(range(SWEEPS, depth - SWEEPS)),
+        )
+    else:
+        parts = (tuple(range(sh.layers)),)
+    *corrected, multipliers, inverse = correct(
+        sh, pieces, applied_pieces, slot, part, fold, parts
+    )
+    returned = [to_all(value, "orb") for value in corrected]
     edge = SWEEPS * own
     box = lax.axis_index("box")
     from_low = lax.ppermute(
-        returned[-sh.across :, -edge:], "box", [(i, i + 1) for i in range(boxes - 1)]
+        returned[0][-sh.across :, -edge:], "box", [(i, i + 1) for i in range(boxes - 1)]
     )
     from_high = lax.ppermute(
-        returned[: sh.across, :edge], "box", [(i + 1, i) for i in range(boxes - 1)]
+        returned[0][: sh.across, :edge], "box", [(i + 1, i) for i in range(boxes - 1)]
     )
     ends = jnp.stack(
         [lax.axis_index("orb"), (box > 0).astype(jnp.int32), (box < boxes - 1).astype(jnp.int32)]
     ).astype(jnp.int32)
-    residual, direction = relax(sh, own, ends, returned, from_low, from_high, inverse)
+    residual, direction = relax(
+        sh, own, parts, ends, returned, from_low, from_high, inverse
+    )
     return (residual, direction, multipliers)
 
 

time: 186 us -> 178 us (0.957)
  blocking collectives: 39.3 us -> 28 us
  starting transfers between devices: 21.8 us -> 30.7 us
  local copies, waits for them, and re-layouts: 6.9 us -> 3.05 us
  waiting for transfers between devices: 64.8 us -> 61.2 us
    all_to_all x2, blocking collectives: 39.3 us -> 28 us  [to_all(): return lax.all_to_all(value, axes, split_axis=0, concat_axis=0, tiled=True)]
    ppermute x4 -> x6, waiting for transfers between devices: 15.8 us -> 6.29 us  [the longest x1 4.8 us: local(): v_hi = lax.ppermute(sent, 'box', downward)]
    all_to_all x2 -> x3, waiting for transfers between devices: 49.1 us -> 54.9 us  [to_all(): return lax.all_to_all(value, axes, split_axis=0, concat_axis=0, tiled=True)]
    ppermute x4 -> x6, starting transfers between devices: 11.4 us -> 16.8 us  [the longest x1 4.53 us: local(): lo = lax.ppermute(psi, 'box', upward)]
    unnamed x22 -> x16, local copies, waits for them, and re-layouts: 6.78 us -> 2.92 us
    all_to_all x2 -> x3, starting transfers between devices: 10.4 us -> 13.9 us  [to_all(): return lax.all_to_all(value, axes, split_axis=0, concat_axis=0, tiled=True)]
    pallas_call x5 -> x6, Pallas kernels: 49 us -> 50.8 us  [the longest x1 27.3 us: halo_part(): pl.pallas_call(functools.partial(halo_kernel, sh), out_shape=pltpu.HBM(ou...]
  transfers between devices with their start and end apart: 6 -> 9, of which waited for: 6 -> 5; matrix products, arithmetic and copies ran while one was open for 0% -> 0% of each run, Pallas kernels for 19% -> 23%
where the time goes in v2:
time: 178 us; the launch traced here: 176 us
  waiting for transfers between devices  61.2 us (34%)
  Pallas kernels  52.1 us (29%)
  starting transfers between devices  30.7 us (17%)
  blocking collectives  28 us (16%)
  local copies, waits for them, and re-layouts  3.05 us (2%)
    all_to_all x3, waiting for transfers between devices, to_all(): return lax.all_to_all(value, axes, split_axis=0, concat_axis=0, tiled=True)  54.9 us
    all_to_all x2, blocking collectives, to_all(): return lax.all_to_all(value, axes, split_axis=0, concat_axis=0, tiled=True)  28 us
    pallas_call x1, Pallas kernels, halo_part(): pl.pallas_call(functools.partial(halo_kernel, sh), out_shape=pltpu.HBM(ou...  27.3 us
    all_to_all x3, starting transfers between devices, to_all(): return lax.all_to_all(value, axes, split_axis=0, concat_axis=0, tiled=True)  13.9 us
    pallas_call x1, Pallas kernels, relax(): pl.pallas_call(functools.partial(relax_kernel, sh, own, parts), out_shape...  8.66 us
    pallas_call x1, Pallas kernels, own_part(): pl.pallas_call(functools.partial(own_kernel, sh), out_shape=(full, full,...  8.48 us
    ppermute x1, waiting for transfers between devices, local(): v_hi = lax.ppermute(sent, 'box', downward)  4.8 us
    ppermute x1, starting transfers between devices, local(): lo = lax.ppermute(psi, 'box', upward)  4.53 us
  transfers between devices with their start and end apart: 9, of which 5 were waited for; matrix products, arithmetic and copies ran while one was open for 0% of the time, Pallas kernels for 23%

profile of v2, /device:TPU:1, one launch (start us, length us, event | category | flops | bytes accessed | tf_op | source)
XLA Modules:
  0.0 175.9 jit_solution(5121131772266659909)
XLA Ops:
  0.6 4.5 %collective-permute-start = (f32[8,16,4096]{2,1,0:T(8,128)}, f32[8,16,4096]{2,1,0:T(8,128)}, u32[]{:S(2)}, u32[]{:S(2)}) collective-permute-start(f32[8,16,4096]{2,1,0:T(8,128)} %psi_ref.1), channel_id=1, source_target_pairs={{0,1},{1,2},{2,3},{4,5},{5,6},{6,7},{8,9},{9,10},{10,11},{12,13},{... | collective-permute-start | bytes 6291464 | tf_op jit(solution)/shard_map/ppermute | solution.py:669
  5.2 1.9 %collective-permute-start.1 = (f32[8,16,4096]{2,1,0:T(8,128)}, f32[8,16,4096]{2,1,0:T(8,128)}, u32[]{:S(2)}, u32[]{:S(2)}) collective-permute-start(f32[8,16,4096]{2,1,0:T(8,128)} %psi_ref.1), channel_id=1, source_target_pairs={{1,0},{2,1},{3,2},{5,4},{6,5},{7,6},{9,8},{10,9},{11,10},{13,12},{... | collective-permute-start | bytes 6291464 | tf_op jit(solution)/shard_map/ppermute | solution.py:670
  7.1 2.4 %pack.1 = f32[8,8,16,512]{3,2,1,0:T(8,128)} custom-call(f32[8,16,4096]{2,1,0:T(8,128)} %psi_ref.1), custom_call_target="tpu_custom_call" | custom-call | bytes 4194304 | tf_op jit(solution)/shard_map/pack/pallas_call | solution.py:143
  9.5 0.0 copy-start.2
  9.6 0.0 copy-start.4
  9.6 0.0 copy-start.6
  9.6 5.7 %all-to-all-start = ((f32[8,8,16,512]{3,2,1,0:T(8,128)}), f32[8,8,16,512]{3,2,1,0:T(8,128)}, u32[]{:S(2)}, u32[]{:S(2)}) async-start(f32[8,8,16,512]{3,2,1,0:T(8,128)} %pack.1), calls=%async_computation | async-start | bytes 4194304 | tf_op jit(solution)/shard_map/all_to_all | solution.py:653
  15.3 0.0 copy-done.2
  15.3 0.0 copy-done.4
  15.3 0.0 copy-done.6
  15.3 0.0 copy-start.3
  15.3 0.0 copy-start.5
  15.4 8.5 %own_part.1 = (f32[16,32,8,128]{3,2,1,0:T(8,128)S(1)}, f32[16,32,8,128]{3,2,1,0:T(8,128)S(1)}, f32[16,32,8,128]{3,2,1,0:T(8,128)S(1)}) custom-call(f32[8,16,4096]{2,1,0:T(8,128)S(1)} %copy-done.2, bf16[256,256]{1,0:T(8,128)(2,1)S(1)} %copy-done.4, bf16[256,256]{1,0:T(8,128)(2,1)S(1)} %copy-done.6), custom_call_target="tpu_custom_call" | custom-call | flops 10000000000 | bytes 10000000 | tf_op jit(solution)/shard_map/own_part/pallas_call | solution.py:270
  23.8 0.0 copy-done.3
  23.9 3.9 %collective-permute-start.2 = (f32[16,4096]{1,0:T(8,128)S(1)}, f32[16,4096]{1,0:T(8,128)S(1)}, u32[]{:S(2)}, u32[]{:S(2)}) collective-permute-start(f32[16,4096]{1,0:T(8,128)S(1)} %copy-done.3), channel_id=1, source_target_pairs={{0,1},{1,2},{2,3},{4,5},{5,6},{6,7},{8,9},{9,10},{10,11},{12,13},{... | collective-permute-start | bytes 786440 | tf_op jit(solution)/shard_map/ppermute | solution.py:674
  27.7 1.9 %collective-permute-start.3 = (f32[16,4096]{1,0:T(8,128)S(1)}, f32[16,4096]{1,0:T(8,128)S(1)}, u32[]{:S(2)}, u32[]{:S(2)}) collective-permute-start(f32[16,4096]{1,0:T(8,128)S(1)} %copy-done.3), channel_id=1, source_target_pairs={{1,0},{2,1},{3,2},{5,4},{6,5},{7,6},{9,8},{10,9},{11,10},{13,12},{... | collective-permute-start | bytes 786440 | tf_op jit(solution)/shard_map/ppermute | solution.py:675
  29.7 1.5 collective-permute-done.2.vlo_ref
  31.1 4.8 %collective-permute-done.3.vhi_ref = f32[16,4096]{1,0:T(8,128)S(1)} collective-permute-done((f32[16,4096]{1,0:T(8,128)S(1)}, f32[16,4096]{1,0:T(8,128)S(1)}, u32[]{:S(2)}, u32[]{:S(2)}) %collective-permute-start.3) | collective-permute-done | bytes 262176 | tf_op jit(solution)/shard_map/ppermute | solution.py:675
  35.9 0.0 collective-permute-done.lo_hbm
  35.9 0.0 collective-permute-done.1.hi_hbm
  35.9 0.0 copy-done.5
  36.0 27.3 %halo_part.1 = f32[8,16,8,512]{3,2,1,0:T(8,128)} custom-call(f32[8,16,4096]{2,1,0:T(8,128)} %collective-permute-done.lo_hbm, f32[8,16,4096]{2,1,0:T(8,128)} %collective-permute-done.1.hi_hbm, f32[16,32,8,128]{3,2,1,0:T(8,128)S(1)} %get-tuple-element.14.c_ref, f32[16,32,8,128]{3,2,1,0:T(8,128)S(1)} %get-tuple-element.16.w_ref, ...), custom_call_target="tpu_custom_call" | custom-call | flops 30000001024 | bytes 10000000 | tf_op jit(solution)/shard_map/halo_part/pallas_call | solution.py:384
  63.2 0.0 copy-start.7
  63.3 1.1 all-to-all-done.in_ref
  64.4 4.1 %all-to-all-start.1 = ((f32[8,16,8,512]{3,2,1,0:T(8,128)}), f32[8,16,8,512]{3,2,1,0:T(8,128)S(1)}, u32[]{:S(2)}, u32[]{:S(2)}) async-start(f32[8,16,8,512]{3,2,1,0:T(8,128)} %halo_part.1), calls=%async_computation.1 | async-start | bytes 4194304 | tf_op jit(solution)/shard_map/all_to_all | solution.py:653
  68.5 0.0 copy-done.7
  68.5 0.1 copy.10.slot_ref
  68.6 2.0 %turn.1.c_ref = f32[8,16,8,512]{3,2,1,0:T(8,128)S(1)} custom-call(f32[8,8,16,512]{3,2,1,0:T(8,128)} %all-to-all-done.in_ref), custom_call_target="tpu_custom_call" | custom-call | flops 100000000 | bytes 4194304 | tf_op jit(solution)/shard_map/turn/pallas_call | solution.py:165
  70.5 0.0 copy-start
  70.5 1.3 copy-done
  71.8 45.1 %all-to-all-done.1.a_ref = f32[8,16,8,512]{3,2,1,0:T(8,128)S(1)} async-done(((f32[8,16,8,512]{3,2,1,0:T(8,128)}), f32[8,16,8,512]{3,2,1,0:T(8,128)S(1)}, u32[]{:S(2)}, u32[]{:S(2)}) %all-to-all-start.1) | async-done | bytes 2097184 | tf_op jit(solution)/shard_map/all_to_all | solution.py:653
  116.9 0.0 copy-start.1
  116.9 1.6 copy-done.1
  118.5 1.2 gram.1
  119.7 11.4 %all_to_all.25.part_ref = f32[32,8,128]{2,1,0:T(8,128)S(1)} all-to-all(f32[32,8,128]{2,1,0:T(8,128)S(1)} %gram.1), channel_id=1, replica_groups=mesh['orb'=8,'box'=4] {'orb','box'}, dimensions={0} | all-to-all | bytes 262144 | tf_op jit(solution)/shard_map/all_to_all | solution.py:653
  131.1 2.0 %correct.1 = (f32[8,32,512]{2,1,0:T(8,128)S(1)}, f32[8,32,512]{2,1,0:T(8,128)}, f32[32,32]{1,0:T(8,128)}, f32[32,128]{1,0:T(8,128)S(1)}) custom-call(f32[8,16,8,512]{3,2,1,0:T(8,128)S(1)} %copy-done.1, f32[8,16,8,512]{3,2,1,0:T(8,128)S(1)} %all-to-all-done.1.a_ref, s32[32,1]{1,0:T(8,128)S(1)} %copy.10.slot_ref, f32[32,8,128]{2,1,0:T(8,128)S(1)} %all_to_all.25.part_ref), custom_call_target="tpu_custom_call" | custom-call | flops 1000000000 | bytes 10000000 | tf_op jit(solution)/shard_map/correct/pallas_call | solution.py:512
  133.1 16.6 %all_to_all.26.refs_0_ = f32[8,32,512]{2,1,0:T(8,128)S(1)} all-to-all(f32[8,32,512]{2,1,0:T(8,128)S(1)} %get-tuple-element.19), channel_id=1, replica_groups=mesh['orb'=8,'box'=4] {'orb'}, dimensions={0} | all-to-all | bytes 1048576 | tf_op jit(solution)/shard_map/all_to_all | solution.py:653
  149.7 4.0 %all-to-all-start.4 = ((f32[8,32,512]{2,1,0:T(8,128)}), f32[8,32,512]{2,1,0:T(8,128)S(1)}, u32[]{:S(2)}, u32[]{:S(2)}) async-start(f32[8,32,512]{2,1,0:T(8,128)} %get-tuple-element.20), calls=%async_computation.4 | async-start | bytes 1048576 | tf_op jit(solution)/shard_map/all_to_all | solution.py:653
  153.8 2.7 %collective-permute-start.4 = (f32[8,16,512]{2,1,0:T(8,128)S(1)}, f32[8,16,512]{2,1,0:T(8,128)S(1)}, u32[]{:S(2)}, u32[]{:S(2)}) collective-permute-start(f32[8,16,512]{2,1,0:T(8,128)S(1)} %get-tuple-element.26), channel_id=1, source_target_pairs={{0,1},{1,2},{2,3},{4,5},{5,6},{6,7},{8,9},{9,10},{10,11},{12,13},{... | collective-permute-start | bytes 786440 | tf_op jit(solution)/shard_map/ppermute | solution.py:698
  156.5 1.9 %collective-permute-start.5 = (f32[8,16,512]{2,1,0:T(8,128)S(1)}, f32[8,16,512]{2,1,0:T(8,128)S(1)}, u32[]{:S(2)}, u32[]{:S(2)}) collective-permute-start(f32[8,16,512]{2,1,0:T(8,128)S(1)} %get-tuple-element.25), channel_id=1, source_target_pairs={{1,0},{2,1},{3,2},{5,4},{6,5},{7,6},{9,8},{10,9},{11,10},{13,12},{... | collective-permute-start | bytes 786440 | tf_op jit(solution)/shard_map/ppermute | solution.py:701
  158.4 0.1 pad_add_fusion.ends_ref
  158.5 8.7 %all-to-all-done.4.refs_1_ = f32[8,32,512]{2,1,0:T(8,128)S(1)} async-done(((f32[8,32,512]{2,1,0:T(8,128)}), f32[8,32,512]{2,1,0:T(8,128)S(1)}, u32[]{:S(2)}, u32[]{:S(2)}) %all-to-all-start.4) | async-done | bytes 524320 | tf_op jit(solution)/shard_map/all_to_all | solution.py:653
  167.2 0.0 collective-permute-done.4.refs_2_
  167.2 0.0 collective-permute-done.5.refs_3_
  167.2 8.7 %relax.1 = (f32[4,16,4096]{2,1,0:T(8,128)}, f32[4,16,4096]{2,1,0:T(8,128)}) custom-call(s32[3]{0:T(128)S(1)} %pad_add_fusion.ends_ref, f32[8,32,512]{2,1,0:T(8,128)S(1)} %all_to_all.26.refs_0_, f32[8,32,512]{2,1,0:T(8,128)S(1)} %all-to-all-done.4.refs_1_, f32[8,16,512]{2,1,0:T(8,128)S(1)} %collective-permute-done.4.refs_2_, ...), custom_call_target="tpu_custom_call" | custom-call | flops 1000000000 | bytes 10000000 | tf_op jit(solution)/shard_map/relax/pallas_call | solution.py:641
  (1 shorter events, 0.0 us)
Async XLA Ops:
  0.6 35.3 %collective-permute-start = (f32[8,16,4096]{2,1,0:T(8,128)}, f32[8,16,4096]{2,1,0:T(8,128)}, u32[]{:S(2)}, u32[]{:S(2)}) collective-permute-start(f32[8,16,4096]{2,1,0:T(8,128)} %psi_ref.1), channel_id=1, source_target_pairs={{0,1},{1,2},{2,3},{4,5},{5,6},{6,7},{8,9},{9,10},{10,11},{12,13},{... | collective-permute-start | bytes 6291464 | tf_op jit(solution)/shard_map/ppermute | solution.py:669
  5.2 30.8 %collective-permute-start.1 = (f32[8,16,4096]{2,1,0:T(8,128)}, f32[8,16,4096]{2,1,0:T(8,128)}, u32[]{:S(2)}, u32[]{:S(2)}) collective-permute-start(f32[8,16,4096]{2,1,0:T(8,128)} %psi_ref.1), channel_id=1, source_target_pairs={{1,0},{2,1},{3,2},{5,4},{6,5},{7,6},{9,8},{10,9},{11,10},{13,12},{... | collective-permute-start | bytes 6291464 | tf_op jit(solution)/shard_map/ppermute | solution.py:670
  9.5 5.8 %copy-start.2 = (f32[8,16,4096]{2,1,0:T(8,128)S(1)}, f32[8,16,4096]{2,1,0:T(8,128)}, u32[]{:S(2)}) copy-start(f32[8,16,4096]{2,1,0:T(8,128)} %psi_ref.1) | copy-start | bytes 6291460
  9.6 5.8 %copy-start.4 = (bf16[256,256]{1,0:T(8,128)(2,1)S(1)}, bf16[256,256]{1,0:T(8,128)(2,1)}, u32[]{:S(2)}) copy-start(bf16[256,256]{1,0:T(8,128)(2,1)} %constant.19.clone.fwd_ref) | copy-start | bytes 393220
  9.6 5.8 %copy-start.6 = (bf16[256,256]{1,0:T(8,128)(2,1)S(1)}, bf16[256,256]{1,0:T(8,128)(2,1)}, u32[]{:S(2)}) copy-start(bf16[256,256]{1,0:T(8,128)(2,1)} %constant.21.clone.kin_ref) | copy-start | bytes 393220
  9.6 54.8 %all-to-all-start = ((f32[8,8,16,512]{3,2,1,0:T(8,128)}), f32[8,8,16,512]{3,2,1,0:T(8,128)}, u32[]{:S(2)}, u32[]{:S(2)}) async-start(f32[8,8,16,512]{3,2,1,0:T(8,128)} %pack.1), calls=%async_computation | async-start | bytes 4194304 | tf_op jit(solution)/shard_map/all_to_all | solution.py:653
  15.3 8.5 %copy-start.3 = (f32[16,4096]{1,0:T(8,128)S(1)}, f32[16,4096]{1,0:T(8,128)}, u32[]{:S(2)}) copy-start(f32[16,4096]{1,0:T(8,128)} %v_ref.1) | copy-start | bytes 786436
  15.3 20.6 %copy-start.5 = (bf16[256,256]{1,0:T(8,128)(2,1)S(1)}, bf16[256,256]{1,0:T(8,128)(2,1)}, u32[]{:S(2)}) copy-start(bf16[256,256]{1,0:T(8,128)(2,1)} %constant.20.clone.bwd_ref) | copy-start | bytes 393220
  23.9 7.3 %collective-permute-start.2 = (f32[16,4096]{1,0:T(8,128)S(1)}, f32[16,4096]{1,0:T(8,128)S(1)}, u32[]{:S(2)}, u32[]{:S(2)}) collective-permute-start(f32[16,4096]{1,0:T(8,128)S(1)} %copy-done.3), channel_id=1, source_target_pairs={{0,1},{1,2},{2,3},{4,5},{5,6},{6,7},{8,9},{9,10},{10,11},{12,13},{... | collective-permute-start | bytes 786440 | tf_op jit(solution)/shard_map/ppermute | solution.py:674
  27.7 8.2 %collective-permute-start.3 = (f32[16,4096]{1,0:T(8,128)S(1)}, f32[16,4096]{1,0:T(8,128)S(1)}, u32[]{:S(2)}, u32[]{:S(2)}) collective-permute-start(f32[16,4096]{1,0:T(8,128)S(1)} %copy-done.3), channel_id=1, source_target_pairs={{1,0},{2,1},{3,2},{5,4},{6,5},{7,6},{9,8},{10,9},{11,10},{13,12},{... | collective-permute-start | bytes 786440 | tf_op jit(solution)/shard_map/ppermute | solution.py:675
  63.2 5.2 %copy-start.7 = (s32[32]{0:T(128)S(1)}, s32[32]{0:T(128)}, u32[]{:S(2)}) copy-start(s32[32]{0:T(128)} %param.8) | copy-start | bytes 388
  64.4 52.5 %all-to-all-start.1 = ((f32[8,16,8,512]{3,2,1,0:T(8,128)}), f32[8,16,8,512]{3,2,1,0:T(8,128)S(1)}, u32[]{:S(2)}, u32[]{:S(2)}) async-start(f32[8,16,8,512]{3,2,1,0:T(8,128)} %halo_part.1), calls=%async_computation.1 | async-start | bytes 4194304 | tf_op jit(solution)/shard_map/all_to_all | solution.py:653
  70.5 1.3 copy-start
  116.9 1.6 copy-start.1
  149.7 17.5 %all-to-all-start.4 = ((f32[8,32,512]{2,1,0:T(8,128)}), f32[8,32,512]{2,1,0:T(8,128)S(1)}, u32[]{:S(2)}, u32[]{:S(2)}) async-start(f32[8,32,512]{2,1,0:T(8,128)} %get-tuple-element.20), calls=%async_computation.4 | async-start | bytes 1048576 | tf_op jit(solution)/shard_map/all_to_all | solution.py:653
  153.8 13.4 %collective-permute-start.4 = (f32[8,16,512]{2,1,0:T(8,128)S(1)}, f32[8,16,512]{2,1,0:T(8,128)S(1)}, u32[]{:S(2)}, u32[]{:S(2)}) collective-permute-start(f32[8,16,512]{2,1,0:T(8,128)S(1)} %get-tuple-element.26), channel_id=1, source_target_pairs={{0,1},{1,2},{2,3},{4,5},{5,6},{6,7},{8,9},{9,10},{10,11},{12,13},{... | collective-permute-start | bytes 786440 | tf_op jit(solution)/shard_map/ppermute | solution.py:698
  156.5 10.7 %collective-permute-start.5 = (f32[8,16,512]{2,1,0:T(8,128)S(1)}, f32[8,16,512]{2,1,0:T(8,128)S(1)}, u32[]{:S(2)}, u32[]{:S(2)}) collective-permute-start(f32[8,16,512]{2,1,0:T(8,128)S(1)} %get-tuple-element.25), channel_id=1, source_target_pairs={{1,0},{2,1},{3,2},{5,4},{6,5},{7,6},{9,8},{10,9},{11,10},{13,12},{... | collective-permute-start | bytes 786440 | tf_op jit(solution)/shard_map/ppermute | solution.py:701

commit v3 on v2

--- a/solution.py
+++ b/solution.py
@@ -156,19 +156,30 @@
     )(pltpu.with_memory_space_constraint(psi, pltpu.HBM))
 
 
-def turn_kernel(sh, in_ref, out_ref):
-    for index in range(sh.owners):
-        out_ref[index] = jnp.transpose(in_ref[index], (1, 0, 2))
-
-
-def turn(sh, pieces):
+def choose_kernel(sh, slot_ref, in_ref, out_ref):
+    count = slot_ref.shape[0]
+    total_slots = sh.owners * sh.slots
+    chosen = selection(slot_ref, count, total_slots).astype(jnp.bfloat16)
+    turned = [
+        jnp.transpose(in_ref[index], (1, 0, 2)) for index in range(sh.owners)
+    ]
+    for layer in range(sh.layers):
+        high, low = split(jnp.concatenate([rows[layer] for rows in turned], 0))
+        high = jnp.dot(chosen, high, preferred_element_type=jnp.float32)
+        low = jnp.dot(chosen, low, preferred_element_type=jnp.float32)
+        out_ref[layer, :count] = high.astype(jnp.bfloat16)
+        out_ref[layer, count:] = low.astype(jnp.bfloat16)
+
+
+def choose(sh, slot, pieces):
+    count = slot.shape[0]
     return pl.pallas_call(
-        functools.partial(turn_kernel, sh),
-        out_shape=pltpu.VMEM((sh.owners, sh.layers, sh.slots, sh.width), jnp.float32),
-        compiler_params=params(10),
+        functools.partial(choose_kernel, sh),
+        out_shape=pltpu.HBM((sh.layers, 2 * count, sh.width), jnp.bfloat16),
+        compiler_params=params(12),
         cost_estimate=cost(10**8, 2 * pieces.size * 4),
-        name="turn",
-    )(pltpu.with_memory_space_constraint(pieces, pltpu.HBM))
+        name="choose",
+    )(slot, pltpu.with_memory_space_constraint(pieces, pltpu.HBM))
 
 
 def odd_pairs(even, lane):
@@ -272,21 +283,19 @@
         out_shape=(full, full, full),
         scratch_shapes=[pltpu.VMEM(full.shape, jnp.float32)],
         compiler_params=params(14),
-        cost_estimate=cost(10**10, 10**7),
+        cost_estimate=cost(10 * 10**9, 10**7),
         name="own_part",
     )(psi, fwd, kin)
 
 
-def halo_kernel(
-    sh, lo_hbm, hi_hbm, c_ref, w_ref, kin_ref, vlo_ref, v_ref, vhi_ref, fwd_ref, bwd_ref,
-    out_hbm, lo_ref, hi_ref, clo_ref, chi_ref, x_ref, wlo_ref, whi_ref, out_ref, sems, in_sems,
+def side_kernel(
+    sh, lo_hbm, hi_hbm, fwd_ref, clo_ref, chi_ref, wlo_ref, whi_ref, lo_ref, hi_ref, x_ref, sems
 ):
     lane = half_mask(sh.slots)
-    depth = sh.depth
-    reach = depth - 1
+    reach = sh.depth - 1
     arrivals = [
-        pltpu.make_async_copy(lo_hbm, lo_ref, in_sems.at[0]),
-        pltpu.make_async_copy(hi_hbm, hi_ref, in_sems.at[1]),
+        pltpu.make_async_copy(lo_hbm, lo_ref, sems.at[0]),
+        pltpu.make_async_copy(hi_hbm, hi_ref, sems.at[1]),
     ]
     for copy in arrivals:
         copy.start()
@@ -304,6 +313,30 @@
             return carry
 
         lax.fori_loop(first, first + reach, filter_rows, 0)
+
+
+def side_part(sh, lo, hi, fwd):
+    full = (sh.depth, sh.chunks, sh.slots, LANES)
+    hbm = pl.BlockSpec(memory_space=pltpu.HBM)
+    lo, hi = (pltpu.with_memory_space_constraint(x, pltpu.HBM) for x in (lo, hi))
+    return pl.pallas_call(
+        functools.partial(side_kernel, sh),
+        out_shape=(jax.ShapeDtypeStruct(full, jnp.float32),) * 4,
+        in_specs=[hbm] * 2 + [pl.BlockSpec(memory_space=pltpu.VMEM)],
+        scratch_shapes=[pltpu.VMEM(lo.shape, jnp.float32)] * 2
+        + [pltpu.VMEM(full, jnp.float32), pltpu.SemaphoreType.DMA((2,))],
+        compiler_params=params(12),
+        cost_estimate=cost(10 * 10**9, 10**7),
+        name="side_part",
+    )(lo, hi, fwd)
+
+
+def halo_kernel(
+    sh, c_ref, w_ref, kin_ref, clo_ref, chi_ref, wlo_ref, whi_ref, vlo_ref, v_ref, vhi_ref,
+    bwd_ref, out_hbm, x_ref, y_ref, kz_ref, out_ref, sems,
+):
+    lane = half_mask(sh.slots)
+    depth = sh.depth
 
     def along_z(chunk, carry):
         lanes = pl.ds(pl.multiple_of(chunk * LANES, LANES), LANES)
@@ -337,7 +370,7 @@
             total = kin_ref[q, chunk] + cs[q] * KINETIC[0]
             for d in range(1, KREACH + 1):
                 total = total + (cs[q + d] + cs[q - d]) * KINETIC[d]
-            whi_ref[q, chunk] = total
+            kz_ref[q, chunk] = total
         return carry
 
     lax.fori_loop(0, sh.chunks, along_z, 0)
@@ -345,7 +378,7 @@
     def filter_back(layer, carry):
         even = [x_ref[layer, b] for b in range(sh.chunks)]
         for b, v in enumerate(row_filter(even, odd_pairs(even, lane), MAGIC_T)):
-            wlo_ref[layer, b] = v
+            y_ref[layer, b] = v
         return carry
 
     lax.fori_loop(0, depth, filter_back, 0)
@@ -357,7 +390,7 @@
         parts = []
         for inner in range(sh.inner):
             chunk = block * sh.inner + inner
-            rows = jnp.concatenate([wlo_ref[layer, chunk] for layer in range(depth)], 0)
+            rows = jnp.concatenate([y_ref[layer, chunk] for layer in range(depth)], 0)
             high, low = split(rows)
             parts.append(jnp.concatenate([high, low], 1))
         result = lane_product(jnp.concatenate(parts, 0), bwd_ref[...])
@@ -365,7 +398,7 @@
         for inner in range(sh.inner):
             chunk = block * sh.inner + inner
             for layer in range(depth):
-                out_ref[sh.at(layer, block, inner)] = result[inner, layer] + whi_ref[layer, chunk]
+                out_ref[sh.at(layer, block, inner)] = result[inner, layer] + kz_ref[layer, chunk]
         for group in range(sh.layered):
             piece(group * sh.across + block).start()
         return carry
@@ -375,28 +408,20 @@
         piece(index).wait()
 
 
-def halo_part(sh, lo, hi, c, w, kin, v_lo, v, v_hi, fwd, bwd):
+def halo_part(sh, own, sides, v_lo, v, v_hi, bwd):
     full = pltpu.VMEM((sh.depth, sh.chunks, sh.slots, LANES), jnp.float32)
     out = (sh.owners, sh.layers, sh.slots, sh.width)
-    hbm = pl.BlockSpec(memory_space=pltpu.HBM)
-    vmem = pl.BlockSpec(memory_space=pltpu.VMEM)
-    lo, hi = (pltpu.with_memory_space_constraint(x, pltpu.HBM) for x in (lo, hi))
     return pl.pallas_call(
         functools.partial(halo_kernel, sh),
         out_shape=pltpu.HBM(out, jnp.float32),
-        in_specs=[hbm] * 2 + [vmem] * 8,
-        out_specs=hbm,
-        scratch_shapes=[pltpu.VMEM(lo.shape, jnp.float32)] * 2
-        + [full] * 5
-        + [
-            pltpu.VMEM(out, jnp.float32),
-            pltpu.SemaphoreType.DMA((sh.owners,)),
-            pltpu.SemaphoreType.DMA((2,)),
-        ],
-        compiler_params=params(26),
-        cost_estimate=cost(3 * 10**10, 10**7),
+        in_specs=[pl.BlockSpec(memory_space=pltpu.VMEM)] * 11,
+        out_specs=pl.BlockSpec(memory_space=pltpu.HBM),
+        scratch_shapes=[full] * 3
+        + [pltpu.VMEM(out, jnp.float32), pltpu.SemaphoreType.DMA((sh.owners,))],
+        compiler_params=params(14),
+        cost_estimate=cost(20 * 10**9, 10**7),
         name="halo_part",
-    )(lo, hi, c, w, kin, v_lo, v, v_hi, fwd, bwd)
+    )(*own, *sides, v_lo, v, v_hi, bwd)
 
 
 def selection(slot_ref, count, slots_all):
@@ -414,28 +439,24 @@
     return jnp.concatenate([matrix[:, i * cols : (i + 1) * cols] for i in range(fold)], 0)
 
 
-def gram_kernel(sh, fold, c_ref, a_ref, slot_ref, out_ref):
+def gram_kernel(sh, fold, c_hbm, a_ref, slot_ref, out_ref, c_ref, sem):
+    copy = pltpu.make_async_copy(c_hbm, c_ref, sem)
+    copy.start()
     total_slots = sh.owners * sh.slots
     count = slot_ref.shape[0]
-
-    def parts(ref, layer):
-        rows = ref[:, layer].reshape(total_slots, sh.width)
-        return jnp.concatenate(split(rows), 0)
-
-    def body(layer, total):
-        return total + lax.dot_general(
-            parts(c_ref, layer),
-            parts(a_ref, layer),
+    chosen = selection(slot_ref, count, total_slots)
+    both = jnp.zeros((2 * count, 2 * total_slots), jnp.float32)
+    copy.wait()
+    for layer in range(sh.layers):
+        rows = a_ref[:, layer].reshape(total_slots, sh.width)
+        both = both + lax.dot_general(
+            c_ref[layer],
+            jnp.concatenate(split(rows), 0),
             (((1,), (1,)), ((), ())),
             preferred_element_type=jnp.float32,
         )
-
-    both = jnp.zeros((2 * total_slots, 2 * total_slots), jnp.float32)
-    both = lax.fori_loop(0, sh.layers, body, both, unroll=sh.layers <= 16 and total_slots <= 64)
-    wide = both[:total_slots] + both[total_slots:]
-    full = wide[:, :total_slots] + wide[:, total_slots:]
-    chosen = selection(slot_ref, count, total_slots)
-    rows = jnp.dot(chosen, full, precision=highest, preferred_element_type=jnp.float32)
+    wide = both[:count] + both[count:]
+    rows = wide[:, :total_slots] + wide[:, total_slots:]
     picked = lax.dot_general(
         rows, chosen, (((1,), (1,)), ((), ())), precision=highest,
         preferred_element_type=jnp.float32,
@@ -454,11 +475,14 @@
         shape = (copies,) + shape
     return pl.pallas_call(
         functools.partial(gram_kernel, sh, fold),
-        out_shape=jax.ShapeDtypeStruct(shape, jnp.float32),
+        out_shape=(jax.ShapeDtypeStruct(shape, jnp.float32), pltpu.VMEM(c.shape, c.dtype)),
+        in_specs=[pl.BlockSpec(memory_space=pltpu.HBM)]
+        + [pl.BlockSpec(memory_space=pltpu.VMEM)] * 2,
+        scratch_shapes=[pltpu.SemaphoreType.DMA],
         compiler_params=params(16),
         cost_estimate=cost(10**9, 10**7),
         name="gram",
-    )(c, a, slot)
+    )(pltpu.with_memory_space_constraint(c, pltpu.HBM), a, slot)
 
 
 def correct_kernel(sh, fold, own, parts, c_ref, a_ref, slot_ref, part_ref, *outs):
@@ -476,24 +500,21 @@
     denominator = 2.0 * coupling_z + 4.0 * coupling_xy + 1.0 + jnp.abs(diagonal)
     inv_ref[...] = jnp.broadcast_to(1.0 / denominator, (count, LANES))
     chosen = selection(slot_ref, count, total_slots)
-    mixing = lax.dot_general(
-        multipliers, chosen, (((0,), (0,)), ((), ())), precision=highest,
-        preferred_element_type=jnp.float32,
-    )
-    weights = jnp.concatenate([chosen, -mixing], 1)
-    high, low = split(weights)
+    high, low = split(-multipliers.T)
+    chosen = chosen.astype(jnp.bfloat16)
     weights = jnp.concatenate(
         [
-            jnp.concatenate([high, high], 1),
-            jnp.concatenate([low, jnp.zeros_like(low)], 1),
+            jnp.concatenate([chosen, chosen, high, high], 1),
+            jnp.concatenate(
+                [jnp.zeros((count, 2 * total_slots), jnp.bfloat16), low, jnp.zeros_like(low)], 1
+            ),
         ],
         0,
     )
 
     def body(layer, place, out_ref):
-        a_rows = split(a_ref[:, layer].reshape(total_slots, sh.width))
-        c_rows = split(c_ref[:, layer].reshape(total_slots, sh.width))
-        data = jnp.concatenate([a_rows[0], c_rows[0], a_rows[1], c_rows[1]], 0)
+        rows = split(a_ref[:, layer].reshape(total_slots, sh.width))
+        data = jnp.concatenate([rows[0], rows[1], c_ref[layer]], 0)
         both = jnp.dot(weights, data, preferred_element_type=jnp.float32)
         result = both[:count] + both[count:]
         for owner in range(sh.owners):
@@ -527,7 +548,8 @@
 
 def relax_kernel(sh, own, parts, ends_ref, *refs):
     r_refs = refs[: len(parts)]
-    lo_ref, hi_ref, inv_ref, res_out, dir_out, res_ref, one_ref, two_ref = refs[len(parts) :]
+    lo_ref, hi_ref, inv_ref, res_hbm, dir_hbm, *refs = refs[len(parts) :]
+    res_ref, one_ref, two_ref, res_out, dir_out, sems = refs
     places = {layer: (ref, i) for part, ref in zip(parts, r_refs) for i, layer in enumerate(part)}
     rows = sh.depth * own
     edge = SWEEPS * own
@@ -544,11 +566,17 @@
             return keep_lo
         return keep_hi if tile >= tiles - edge_tiles else inverse
 
-    group = min(4, sh.chunks)
+    group = min(16, sh.chunks)
     blank = jnp.zeros((rows + 2 * edge, LANES), jnp.float32)
     for ref in (one_ref, two_ref):
         ref[0] = blank
         ref[sh.chunks + 1] = blank
+
+    def leave(source, target, kind, step, width):
+        lanes = pl.ds(pl.multiple_of(step * width, LANES), width)
+        return pltpu.make_async_copy(
+            source.at[:, :, lanes], target.at[:, :, lanes], sems.at[kind, step]
+        )
 
     def gather(block, carry):
         for inner in range(sh.inner):
@@ -565,6 +593,11 @@
                 value = column[tile * 8 : (tile + 1) * 8]
                 res_ref[chunk, tile * 8 : (tile + 1) * 8] = value
                 one_ref[chunk + 1, tile * 8 : (tile + 1) * 8] = value * scale(tile)
+            out_lanes = pl.ds(pl.multiple_of(chunk * LANES, LANES), LANES)
+            for orbital in range(own):
+                here = pl.ds(edge + orbital, sh.depth, stride=own)
+                res_out[orbital, :, out_lanes] = res_ref[chunk, here, :]
+        leave(res_out, res_hbm, 0, block, sh.width).start()
         return carry
 
     lax.fori_loop(0, sh.across, gather, 0)
@@ -625,24 +658,32 @@
             out_lanes = pl.ds(pl.multiple_of(chunk * LANES, LANES), LANES)
             for orbital in range(own):
                 here = pl.ds(edge + orbital, sh.depth, stride=own)
-                res_out[orbital, :, out_lanes] = res_ref[chunk, here, :]
                 dir_out[orbital, :, out_lanes] = source[chunk + 1, here, :]
+        leave(dir_out, dir_hbm, 1, step, group * LANES).start()
         return carry
 
     lax.fori_loop(0, sh.chunks // group, spread, 0)
+    for block in range(sh.across):
+        leave(res_out, res_hbm, 0, block, sh.width).wait()
+    for step in range(sh.chunks // group):
+        leave(dir_out, dir_hbm, 1, step, group * LANES).wait()
 
 
 def relax(sh, own, parts, ends, pieces, lo, hi, inverse):
     rows = (sh.depth + 2 * SWEEPS) * own
     scratch = pltpu.VMEM((sh.chunks, rows, LANES), jnp.float32)
     padded = pltpu.VMEM((sh.chunks + 2, rows, LANES), jnp.float32)
-    out = jax.ShapeDtypeStruct((own, sh.depth, sh.plane), jnp.float32)
+    out = (own, sh.depth, sh.plane)
+    hbm = pl.BlockSpec(memory_space=pltpu.HBM)
     vmem = pl.BlockSpec(memory_space=pltpu.VMEM)
     return pl.pallas_call(
         functools.partial(relax_kernel, sh, own, parts),
-        out_shape=(out, out),
+        out_shape=(pltpu.HBM(out, jnp.float32),) * 2,
+        out_specs=(hbm, hbm),
         in_specs=[pl.BlockSpec(memory_space=pltpu.SMEM)] + [vmem] * (3 + len(parts)),
-        scratch_shapes=[scratch, padded, padded],
+        scratch_shapes=[scratch, padded, padded]
+        + [pltpu.VMEM(out, jnp.float32)] * 2
+        + [pltpu.SemaphoreType.DMA((2, max(sh.across, sh.chunks)))],
         compiler_params=params(14),
         cost_estimate=cost(10**9, 10**7),
         name="relax",
@@ -668,19 +709,20 @@
     downward = [(i + 1, i) for i in range(boxes - 1)]
     lo = lax.ppermute(psi, "box", upward)
     hi = lax.ppermute(psi, "box", downward)
-    pieces = turn(sh, to_all(pack(sh, psi), "orb"))
+    slot = orbital_slot.reshape(count, 1)
+    pieces = choose(sh, slot, to_all(pack(sh, psi), "orb"))
     c, w, kin_own = own_part(sh, psi, fwd, kin)
     w, sent = lax.optimization_barrier((w, potential))
     v_lo = lax.ppermute(sent, "box", upward)
     v_hi = lax.ppermute(sent, "box", downward)
-    applied = halo_part(sh, lo, hi, c, w, kin_own, v_lo, potential, v_hi, fwd, bwd)
+    sides = side_part(sh, lo, hi, fwd)
+    applied = halo_part(sh, (c, w, kin_own), sides, v_lo, potential, v_hi, bwd)
     applied_pieces = to_all(applied, "orb")
 
-    slot = orbital_slot.reshape(count, 1)
     fold = max(1, LANES // count)
     devices = owners * boxes
     copies = devices if devices * count * count <= 1 << 20 else 0
-    part = gram(sh, pieces, applied_pieces, slot, fold, copies)
+    part, pieces = gram(sh, pieces, applied_pieces, slot, fold, copies)
     part = to_all(part, ("orb", "box")) if copies else lax.psum(part, ("orb", "box"))
     if sh.layered == 1 and depth > 2 * SWEEPS:
         parts = (

time: 178 us -> 176 us (0.989)
  waiting for transfers between devices: 61.2 us -> 57.2 us
  local copies, waits for them, and re-layouts: 3.05 us -> 0.17 us
  starting transfers between devices: 30.7 us -> 32.5 us
    pallas_call x2 -> x3, Pallas kernels: 3.19 us -> 17.3 us  [the longest x1 11.4 us: side_part(): pl.pallas_call(functools.partial(side_kernel, sh), out_shape=(jax.ShapeDt...]
    pallas_call x1, Pallas kernels: 27.3 us -> 15.9 us  [halo_part(): pl.pallas_call(functools.partial(halo_kernel, sh), out_shape=pltpu.HBM(ou...]
    ppermute x1, waiting for transfers between devices: 4.8 us -> 0.01 us  [local(): v_hi = lax.ppermute(sent, 'box', downward)]
    unnamed x16 -> x12, local copies, waits for them, and re-layouts: 2.92 us -> 0.04 us
    all_to_all x3, waiting for transfers between devices: 54.9 us -> 56.7 us  [to_all(): return lax.all_to_all(value, axes, split_axis=0, concat_axis=0, tiled=True)]
  transfers between devices with their start and end apart: 9 -> 9, of which waited for: 5 -> 4; matrix products, arithmetic and copies ran while one was open for 0% -> 0% of each run, Pallas kernels for 23% -> 24%
where the time goes in v3:
time: 176 us; the launch traced here: 173 us
  waiting for transfers between devices  57.2 us (32%)
  Pallas kernels  53 us (30%)
  starting transfers between devices  32.5 us (18%)
  blocking collectives  29.2 us (17%)
    all_to_all x3, waiting for transfers between devices, to_all(): return lax.all_to_all(value, axes, split_axis=0, concat_axis=0, tiled=True)  56.7 us
    all_to_all x2, blocking collectives, to_all(): return lax.all_to_all(value, axes, split_axis=0, concat_axis=0, tiled=True)  29.2 us
    pallas_call x1, Pallas kernels, halo_part(): pl.pallas_call(functools.partial(halo_kernel, sh), out_shape=pltpu.HBM(ou...  15.9 us
    all_to_all x3, starting transfers between devices, to_all(): return lax.all_to_all(value, axes, split_axis=0, concat_axis=0, tiled=True)  14.4 us
    pallas_call x1, Pallas kernels, side_part(): pl.pallas_call(functools.partial(side_kernel, sh), out_shape=(jax.ShapeDt...  11.4 us
    pallas_call x1, Pallas kernels, own_part(): pl.pallas_call(functools.partial(own_kernel, sh), out_shape=(full, full,...  8.48 us
    pallas_call x1, Pallas kernels, relax(): pl.pallas_call(functools.partial(relax_kernel, sh, own, parts), out_shape...  7.14 us
    ppermute x1, starting transfers between devices, local(): lo = lax.ppermute(psi, 'box', upward)  4.52 us
  transfers between devices with their start and end apart: 9, of which 4 were waited for; matrix products, arithmetic and copies ran while one was open for 0% of the time, Pallas kernels for 24%

profile of v3, /device:TPU:1, one launch (start us, length us, event | category | flops | bytes accessed | tf_op | source)
XLA Modules:
  0.0 173.0 jit_solution(5755861026339904468)
XLA Ops:
  0.6 1.9 %collective-permute-start.1 = (f32[8,16,4096]{2,1,0:T(8,128)}, f32[8,16,4096]{2,1,0:T(8,128)}, u32[]{:S(2)}, u32[]{:S(2)}) collective-permute-start(f32[8,16,4096]{2,1,0:T(8,128)} %psi_ref.1), channel_id=1, source_target_pairs={{1,0},{2,1},{3,2},{5,4},{6,5},{7,6},{9,8},{10,9},{11,10},{13,12},{... | collective-permute-start | bytes 6291464 | tf_op jit(solution)/shard_map/ppermute | solution.py:711
  2.6 4.5 %collective-permute-start = (f32[8,16,4096]{2,1,0:T(8,128)}, f32[8,16,4096]{2,1,0:T(8,128)}, u32[]{:S(2)}, u32[]{:S(2)}) collective-permute-start(f32[8,16,4096]{2,1,0:T(8,128)} %psi_ref.1), channel_id=1, source_target_pairs={{0,1},{1,2},{2,3},{4,5},{5,6},{6,7},{8,9},{9,10},{10,11},{12,13},{... | collective-permute-start | bytes 6291464 | tf_op jit(solution)/shard_map/ppermute | solution.py:710
  7.1 2.4 %pack.1 = f32[8,8,16,512]{3,2,1,0:T(8,128)} custom-call(f32[8,16,4096]{2,1,0:T(8,128)} %psi_ref.1), custom_call_target="tpu_custom_call" | custom-call | bytes 4194304 | tf_op jit(solution)/shard_map/pack/pallas_call | solution.py:143
  9.5 0.0 copy-start
  9.5 0.0 copy-start.3
  9.5 0.0 copy-start.4
  9.5 5.7 %all-to-all-start = ((f32[8,8,16,512]{3,2,1,0:T(8,128)}), f32[8,8,16,512]{3,2,1,0:T(8,128)}, u32[]{:S(2)}, u32[]{:S(2)}) async-start(f32[8,8,16,512]{3,2,1,0:T(8,128)} %pack.1), calls=%async_computation | async-start | bytes 4194304 | tf_op jit(solution)/shard_map/all_to_all | solution.py:694
  15.2 0.0 copy-done
  15.2 0.0 copy-done.3
  15.2 0.0 copy-done.4
  15.2 0.0 copy-start.1
  15.2 8.5 %own_part.1 = (f32[16,32,8,128]{3,2,1,0:T(8,128)S(1)}, f32[16,32,8,128]{3,2,1,0:T(8,128)S(1)}, f32[16,32,8,128]{3,2,1,0:T(8,128)S(1)}) custom-call(f32[8,16,4096]{2,1,0:T(8,128)S(1)} %copy-done, bf16[256,256]{1,0:T(8,128)(2,1)S(1)} %copy-done.3, bf16[256,256]{1,0:T(8,128)(2,1)S(1)} %copy-done.4), custom_call_target="tpu_custom_call" | custom-call | flops 10000000000 | bytes 10000000 | tf_op jit(solution)/shard_map/own_part/pallas_call | solution.py:281
  23.7 0.0 copy-done.1
  23.7 0.0 copy-start.2
  23.8 3.0 %collective-permute-start.3 = (f32[16,4096]{1,0:T(8,128)S(1)}, f32[16,4096]{1,0:T(8,128)S(1)}, u32[]{:S(2)}, u32[]{:S(2)}) collective-permute-start(f32[16,4096]{1,0:T(8,128)S(1)} %copy-done.1), channel_id=1, source_target_pairs={{1,0},{2,1},{3,2},{5,4},{6,5},{7,6},{9,8},{10,9},{11,10},{13,12},{... | collective-permute-start | bytes 786440 | tf_op jit(solution)/shard_map/ppermute | solution.py:717
  26.8 3.1 %collective-permute-start.2 = (f32[16,4096]{1,0:T(8,128)S(1)}, f32[16,4096]{1,0:T(8,128)S(1)}, u32[]{:S(2)}, u32[]{:S(2)}) collective-permute-start(f32[16,4096]{1,0:T(8,128)S(1)} %copy-done.1), channel_id=1, source_target_pairs={{0,1},{1,2},{2,3},{4,5},{5,6},{6,7},{8,9},{9,10},{10,11},{12,13},{... | collective-permute-start | bytes 786440 | tf_op jit(solution)/shard_map/ppermute | solution.py:716
  29.9 0.0 collective-permute-done.1.hi_hbm
  29.9 0.5 collective-permute-done.lo_hbm
  30.4 11.4 %side_part.1 = (f32[16,32,8,128]{3,2,1,0:T(8,128)S(1)}, f32[16,32,8,128]{3,2,1,0:T(8,128)S(1)}, f32[16,32,8,128]{3,2,1,0:T(8,128)S(1)}, f32[16,32,8,128]{3,2,1,0:T(8,128)S(1)}) custom-call(f32[8,16,4096]{2,1,0:T(8,128)} %collective-permute-done.lo_hbm, f32[8,16,4096]{2,1,0:T(8,128)} %collective-permute-done.1.hi_hbm, bf16[256,256]{1,0:T(8,128)(2,1)S(1)} %copy-done.3), custom_call_target="tpu_custom_call" | custom-call | flops 10000000000 | bytes 10000000 | tf_op jit(solution)/shard_map/side_part/pallas_call | solution.py:322
  41.7 0.0 collective-permute-done.3.vhi_ref
  41.8 0.0 collective-permute-done.2.vlo_ref
  41.8 0.0 copy-done.2
  41.8 15.9 %halo_part.1 = f32[8,16,8,512]{3,2,1,0:T(8,128)} custom-call(f32[16,32,8,128]{3,2,1,0:T(8,128)S(1)} %get-tuple-element.20.c_ref, f32[16,32,8,128]{3,2,1,0:T(8,128)S(1)} %get-tuple-element.22.w_ref, f32[16,32,8,128]{3,2,1,0:T(8,128)S(1)} %get-tuple-element.23.kin_ref, f32[16,32,8,128]{3,2,1,0:T(8,128)S(1)} %get-tuple-element.24.clo_ref, ...), custom_call_target="tpu_custom_call" | custom-call | flops 20000000000 | bytes 10000000 | tf_op jit(solution)/shard_map/halo_part/pallas_call | solution.py:414
  57.7 0.0 copy-start.5
  57.7 5.0 %all-to-all-done.in_ref = f32[8,8,16,512]{3,2,1,0:T(8,128)} async-done(((f32[8,8,16,512]{3,2,1,0:T(8,128)}), f32[8,8,16,512]{3,2,1,0:T(8,128)}, u32[]{:S(2)}, u32[]{:S(2)}) %all-to-all-start) | async-done | bytes 2097184 | tf_op jit(solution)/shard_map/all_to_all | solution.py:694
  62.7 4.7 %all-to-all-start.1 = ((f32[8,16,8,512]{3,2,1,0:T(8,128)}), f32[8,16,8,512]{3,2,1,0:T(8,128)S(1)}, u32[]{:S(2)}, u32[]{:S(2)}) async-start(f32[8,16,8,512]{3,2,1,0:T(8,128)} %halo_part.1), calls=%async_computation.1 | async-start | bytes 4194304 | tf_op jit(solution)/shard_map/all_to_all | solution.py:694
  67.4 0.0 copy-done.5
  67.4 0.1 copy.9.slot_ref
  67.5 3.5 %choose.1.c_hbm = bf16[16,64,512]{2,1,0:T(8,128)(2,1)} custom-call(s32[32,1]{1,0:T(8,128)S(1)} %copy.9.slot_ref, f32[8,8,16,512]{3,2,1,0:T(8,128)} %all-to-all-done.in_ref), custom_call_target="tpu_custom_call" | custom-call | flops 100000000 | bytes 4194304 | tf_op jit(solution)/shard_map/choose/pallas_call | solution.py:176
  71.0 44.0 %all-to-all-done.1.a_ref = f32[8,16,8,512]{3,2,1,0:T(8,128)S(1)} async-done(((f32[8,16,8,512]{3,2,1,0:T(8,128)}), f32[8,16,8,512]{3,2,1,0:T(8,128)S(1)}, u32[]{:S(2)}, u32[]{:S(2)}) %all-to-all-start.1) | async-done | bytes 2097184 | tf_op jit(solution)/shard_map/all_to_all | solution.py:694
  115.0 2.4 %gram.1 = (f32[32,8,128]{2,1,0:T(8,128)S(1)}, bf16[16,64,512]{2,1,0:T(8,128)(2,1)S(1)}) custom-call(bf16[16,64,512]{2,1,0:T(8,128)(2,1)} %choose.1.c_hbm, f32[8,16,8,512]{3,2,1,0:T(8,128)S(1)} %all-to-all-done.1.a_ref, s32[32,1]{1,0:T(8,128)S(1)} %copy.9.slot_ref), custom_call_target="tpu_custom_call" | custom-call | flops 1000000000 | bytes 10000000 | tf_op jit(solution)/shard_map/gram/pallas_call | solution.py:476
  117.4 12.6 %all_to_all.25.part_ref = f32[32,8,128]{2,1,0:T(8,128)S(1)} all-to-all(f32[32,8,128]{2,1,0:T(8,128)S(1)} %get-tuple-element.30), channel_id=1, replica_groups=mesh['orb'=8,'box'=4] {'orb','box'}, dimensions={0} | all-to-all | bytes 262144 | tf_op jit(solution)/shard_map/all_to_all | solution.py:694
  130.0 1.7 correct.1
  131.7 16.6 %all_to_all.26.refs_0_ = f32[8,32,512]{2,1,0:T(8,128)S(1)} all-to-all(f32[8,32,512]{2,1,0:T(8,128)S(1)} %get-tuple-element.31), channel_id=1, replica_groups=mesh['orb'=8,'box'=4] {'orb'}, dimensions={0} | all-to-all | bytes 1048576 | tf_op jit(solution)/shard_map/all_to_all | solution.py:694
  148.3 4.0 %all-to-all-start.4 = ((f32[8,32,512]{2,1,0:T(8,128)}), f32[8,32,512]{2,1,0:T(8,128)S(1)}, u32[]{:S(2)}, u32[]{:S(2)}) async-start(f32[8,32,512]{2,1,0:T(8,128)} %get-tuple-element.32), calls=%async_computation.4 | async-start | bytes 1048576 | tf_op jit(solution)/shard_map/all_to_all | solution.py:694
  152.4 2.7 %collective-permute-start.5 = (f32[8,16,512]{2,1,0:T(8,128)S(1)}, f32[8,16,512]{2,1,0:T(8,128)S(1)}, u32[]{:S(2)}, u32[]{:S(2)}) collective-permute-start(f32[8,16,512]{2,1,0:T(8,128)S(1)} %get-tuple-element.37), channel_id=1, source_target_pairs={{1,0},{2,1},{3,2},{5,4},{6,5},{7,6},{9,8},{10,9},{11,10},{13,12},{... | collective-permute-start | bytes 786440 | tf_op jit(solution)/shard_map/ppermute | solution.py:743
  155.1 2.8 %collective-permute-start.4 = (f32[8,16,512]{2,1,0:T(8,128)S(1)}, f32[8,16,512]{2,1,0:T(8,128)S(1)}, u32[]{:S(2)}, u32[]{:S(2)}) collective-permute-start(f32[8,16,512]{2,1,0:T(8,128)S(1)} %get-tuple-element.38), channel_id=1, source_target_pairs={{0,1},{1,2},{2,3},{4,5},{5,6},{6,7},{8,9},{9,10},{10,11},{12,13},{... | collective-permute-start | bytes 786440 | tf_op jit(solution)/shard_map/ppermute | solution.py:740
  158.0 0.1 pad_add_fusion.ends_ref
  158.1 7.8 %all-to-all-done.4.refs_1_ = f32[8,32,512]{2,1,0:T(8,128)S(1)} async-done(((f32[8,32,512]{2,1,0:T(8,128)}), f32[8,32,512]{2,1,0:T(8,128)S(1)}, u32[]{:S(2)}, u32[]{:S(2)}) %all-to-all-start.4) | async-done | bytes 524320 | tf_op jit(solution)/shard_map/all_to_all | solution.py:694
  165.8 0.0 collective-permute-done.5.refs_3_
  165.8 0.0 collective-permute-done.4.refs_2_
  165.8 7.1 %relax.1 = (f32[4,16,4096]{2,1,0:T(8,128)}, f32[4,16,4096]{2,1,0:T(8,128)}) custom-call(s32[3]{0:T(128)S(1)} %pad_add_fusion.ends_ref, f32[8,32,512]{2,1,0:T(8,128)S(1)} %all_to_all.26.refs_0_, f32[8,32,512]{2,1,0:T(8,128)S(1)} %all-to-all-done.4.refs_1_, f32[8,16,512]{2,1,0:T(8,128)S(1)} %collective-permute-done.4.refs_2_, ...), custom_call_target="tpu_custom_call" | custom-call | flops 1000000000 | bytes 10000000 | tf_op jit(solution)/shard_map/relax/pallas_call | solution.py:679
  (1 shorter events, 0.0 us)
Async XLA Ops:
  0.6 29.2 %collective-permute-start.1 = (f32[8,16,4096]{2,1,0:T(8,128)}, f32[8,16,4096]{2,1,0:T(8,128)}, u32[]{:S(2)}, u32[]{:S(2)}) collective-permute-start(f32[8,16,4096]{2,1,0:T(8,128)} %psi_ref.1), channel_id=1, source_target_pairs={{1,0},{2,1},{3,2},{5,4},{6,5},{7,6},{9,8},{10,9},{11,10},{13,12},{... | collective-permute-start | bytes 6291464 | tf_op jit(solution)/shard_map/ppermute | solution.py:711
  2.6 27.8 %collective-permute-start = (f32[8,16,4096]{2,1,0:T(8,128)}, f32[8,16,4096]{2,1,0:T(8,128)}, u32[]{:S(2)}, u32[]{:S(2)}) collective-permute-start(f32[8,16,4096]{2,1,0:T(8,128)} %psi_ref.1), channel_id=1, source_target_pairs={{0,1},{1,2},{2,3},{4,5},{5,6},{6,7},{8,9},{9,10},{10,11},{12,13},{... | collective-permute-start | bytes 6291464 | tf_op jit(solution)/shard_map/ppermute | solution.py:710
  9.5 5.7 %copy-start = (f32[8,16,4096]{2,1,0:T(8,128)S(1)}, f32[8,16,4096]{2,1,0:T(8,128)}, u32[]{:S(2)}) copy-start(f32[8,16,4096]{2,1,0:T(8,128)} %psi_ref.1) | copy-start | bytes 6291460
  9.5 5.7 %copy-start.3 = (bf16[256,256]{1,0:T(8,128)(2,1)S(1)}, bf16[256,256]{1,0:T(8,128)(2,1)}, u32[]{:S(2)}) copy-start(bf16[256,256]{1,0:T(8,128)(2,1)} %constant.19.clone.fwd_ref) | copy-start | bytes 393220
  9.5 5.7 %copy-start.4 = (bf16[256,256]{1,0:T(8,128)(2,1)S(1)}, bf16[256,256]{1,0:T(8,128)(2,1)}, u32[]{:S(2)}) copy-start(bf16[256,256]{1,0:T(8,128)(2,1)} %constant.21.clone.kin_ref) | copy-start | bytes 393220
  9.5 53.2 %all-to-all-start = ((f32[8,8,16,512]{3,2,1,0:T(8,128)}), f32[8,8,16,512]{3,2,1,0:T(8,128)}, u32[]{:S(2)}, u32[]{:S(2)}) async-start(f32[8,8,16,512]{3,2,1,0:T(8,128)} %pack.1), calls=%async_computation | async-start | bytes 4194304 | tf_op jit(solution)/shard_map/all_to_all | solution.py:694
  15.2 8.5 %copy-start.1 = (f32[16,4096]{1,0:T(8,128)S(1)}, f32[16,4096]{1,0:T(8,128)}, u32[]{:S(2)}) copy-start(f32[16,4096]{1,0:T(8,128)} %v_ref.1) | copy-start | bytes 786436
  23.7 18.0 %copy-start.2 = (bf16[256,256]{1,0:T(8,128)(2,1)S(1)}, bf16[256,256]{1,0:T(8,128)(2,1)}, u32[]{:S(2)}) copy-start(bf16[256,256]{1,0:T(8,128)(2,1)} %constant.20.clone.bwd_ref) | copy-start | bytes 393220
  23.8 18.0 %collective-permute-start.3 = (f32[16,4096]{1,0:T(8,128)S(1)}, f32[16,4096]{1,0:T(8,128)S(1)}, u32[]{:S(2)}, u32[]{:S(2)}) collective-permute-start(f32[16,4096]{1,0:T(8,128)S(1)} %copy-done.1), channel_id=1, source_target_pairs={{1,0},{2,1},{3,2},{5,4},{6,5},{7,6},{9,8},{10,9},{11,10},{13,12},{... | collective-permute-start | bytes 786440 | tf_op jit(solution)/shard_map/ppermute | solution.py:717
  26.8 15.0 %collective-permute-start.2 = (f32[16,4096]{1,0:T(8,128)S(1)}, f32[16,4096]{1,0:T(8,128)S(1)}, u32[]{:S(2)}, u32[]{:S(2)}) collective-permute-start(f32[16,4096]{1,0:T(8,128)S(1)} %copy-done.1), channel_id=1, source_target_pairs={{0,1},{1,2},{2,3},{4,5},{5,6},{6,7},{8,9},{9,10},{10,11},{12,13},{... | collective-permute-start | bytes 786440 | tf_op jit(solution)/shard_map/ppermute | solution.py:716
  57.7 9.7 %copy-start.5 = (s32[32]{0:T(128)S(1)}, s32[32]{0:T(128)}, u32[]{:S(2)}) copy-start(s32[32]{0:T(128)} %param.8) | copy-start | bytes 388
  62.7 52.3 %all-to-all-start.1 = ((f32[8,16,8,512]{3,2,1,0:T(8,128)}), f32[8,16,8,512]{3,2,1,0:T(8,128)S(1)}, u32[]{:S(2)}, u32[]{:S(2)}) async-start(f32[8,16,8,512]{3,2,1,0:T(8,128)} %halo_part.1), calls=%async_computation.1 | async-start | bytes 4194304 | tf_op jit(solution)/shard_map/all_to_all | solution.py:694
  148.3 17.5 %all-to-all-start.4 = ((f32[8,32,512]{2,1,0:T(8,128)}), f32[8,32,512]{2,1,0:T(8,128)S(1)}, u32[]{:S(2)}, u32[]{:S(2)}) async-start(f32[8,32,512]{2,1,0:T(8,128)} %get-tuple-element.32), calls=%async_computation.4 | async-start | bytes 1048576 | tf_op jit(solution)/shard_map/all_to_all | solution.py:694
  152.4 13.4 %collective-permute-start.5 = (f32[8,16,512]{2,1,0:T(8,128)S(1)}, f32[8,16,512]{2,1,0:T(8,128)S(1)}, u32[]{:S(2)}, u32[]{:S(2)}) collective-permute-start(f32[8,16,512]{2,1,0:T(8,128)S(1)} %get-tuple-element.37), channel_id=1, source_target_pairs={{1,0},{2,1},{3,2},{5,4},{6,5},{7,6},{9,8},{10,9},{11,10},{13,12},{... | collective-permute-start | bytes 786440 | tf_op jit(solution)/shard_map/ppermute | solution.py:743
  155.1 10.7 %collective-permute-start.4 = (f32[8,16,512]{2,1,0:T(8,128)S(1)}, f32[8,16,512]{2,1,0:T(8,128)S(1)}, u32[]{:S(2)}, u32[]{:S(2)}) collective-permute-start(f32[8,16,512]{2,1,0:T(8,128)S(1)} %get-tuple-element.38), channel_id=1, source_target_pairs={{0,1},{1,2},{2,3},{4,5},{5,6},{6,7},{8,9},{9,10},{10,11},{12,13},{... | collective-permute-start | bytes 786440 | tf_op jit(solution)/shard_map/ppermute | solution.py:740

commit v4 on v3

--- a/solution.py
+++ b/solution.py
@@ -8,6 +8,7 @@
 from jax.experimental import pallas as pl
 from jax.experimental.pallas import tpu as pltpu
 from jax.sharding import PartitionSpec as P
+
 
 MTAPS = 16
 KREACH = 14
@@ -289,16 +290,28 @@
 
 
 def side_kernel(
-    sh, lo_hbm, hi_hbm, fwd_ref, clo_ref, chi_ref, wlo_ref, whi_ref, lo_ref, hi_ref, x_ref, sems
+    sh, far_hbm, near_hbm, fwd_ref, clo_ref, chi_ref, wlo_ref, whi_ref, lo_ref, hi_ref,
+    x_ref, sems,
 ):
     lane = half_mask(sh.slots)
     reach = sh.depth - 1
+
+    def bring(source_lo, source_hi):
+        pltpu.make_async_copy(source_lo, lo_ref, sems.at[0]).start()
+        pltpu.make_async_copy(source_hi, hi_ref, sems.at[1]).start()
+
+    @pl.when(lax.rem(lax.axis_index("box"), 2) == 0)
+    def _():
+        bring(far_hbm, near_hbm)
+
+    @pl.when(lax.rem(lax.axis_index("box"), 2) != 0)
+    def _():
+        bring(near_hbm, far_hbm)
+
     arrivals = [
-        pltpu.make_async_copy(lo_hbm, lo_ref, sems.at[0]),
-        pltpu.make_async_copy(hi_hbm, hi_ref, sems.at[1]),
+        pltpu.make_async_copy(far_hbm, lo_ref, sems.at[0]),
+        pltpu.make_async_copy(near_hbm, hi_ref, sems.at[1]),
     ]
-    for copy in arrivals:
-        copy.start()
     for copy, side_ref, kept, target, first in (
         (arrivals[0], lo_ref, clo_ref, wlo_ref, 1),
         (arrivals[1], hi_ref, chi_ref, whi_ref, 0),
@@ -315,28 +328,30 @@
         lax.fori_loop(first, first + reach, filter_rows, 0)
 
 
-def side_part(sh, lo, hi, fwd):
+def side_part(sh, far, near, fwd):
     full = (sh.depth, sh.chunks, sh.slots, LANES)
-    hbm = pl.BlockSpec(memory_space=pltpu.HBM)
-    lo, hi = (pltpu.with_memory_space_constraint(x, pltpu.HBM) for x in (lo, hi))
     return pl.pallas_call(
         functools.partial(side_kernel, sh),
         out_shape=(jax.ShapeDtypeStruct(full, jnp.float32),) * 4,
-        in_specs=[hbm] * 2 + [pl.BlockSpec(memory_space=pltpu.VMEM)],
-        scratch_shapes=[pltpu.VMEM(lo.shape, jnp.float32)] * 2
+        in_specs=[pl.BlockSpec(memory_space=pl.ANY)] * 2
+        + [pl.BlockSpec(memory_space=pltpu.VMEM)],
+        scratch_shapes=[pltpu.VMEM(far.shape, jnp.float32)] * 2
         + [pltpu.VMEM(full, jnp.float32), pltpu.SemaphoreType.DMA((2,))],
         compiler_params=params(12),
         cost_estimate=cost(10 * 10**9, 10**7),
         name="side_part",
-    )(lo, hi, fwd)
+    )(far, near, fwd)
 
 
 def halo_kernel(
-    sh, c_ref, w_ref, kin_ref, clo_ref, chi_ref, wlo_ref, whi_ref, vlo_ref, v_ref, vhi_ref,
-    bwd_ref, out_hbm, x_ref, y_ref, kz_ref, out_ref, sems,
+    sh, c_ref, w_ref, kin_ref, clo_ref, chi_ref, wlo_ref, whi_ref, vfar_ref, v_ref,
+    vnear_ref, bwd_ref, out_hbm, x_ref, y_ref, kz_ref, vlo_ref, vhi_ref, out_ref, sems,
 ):
     lane = half_mask(sh.slots)
     depth = sh.depth
+    even = lax.rem(lax.axis_index("box"), 2) == 0
+    vlo_ref[...] = jnp.where(even, vfar_ref[...], vnear_ref[...])
+    vhi_ref[...] = jnp.where(even, vnear_ref[...], vfar_ref[...])
 
     def along_z(chunk, carry):
         lanes = pl.ds(pl.multiple_of(chunk * LANES, LANES), LANES)
@@ -408,7 +423,7 @@
         piece(index).wait()
 
 
-def halo_part(sh, own, sides, v_lo, v, v_hi, bwd):
+def halo_part(sh, own, sides, v_far, v, v_near, bwd):
     full = pltpu.VMEM((sh.depth, sh.chunks, sh.slots, LANES), jnp.float32)
     out = (sh.owners, sh.layers, sh.slots, sh.width)
     return pl.pallas_call(
@@ -417,11 +432,12 @@
         in_specs=[pl.BlockSpec(memory_space=pltpu.VMEM)] * 11,
         out_specs=pl.BlockSpec(memory_space=pltpu.HBM),
         scratch_shapes=[full] * 3
+        + [pltpu.VMEM(v.shape, jnp.float32)] * 2
         + [pltpu.VMEM(out, jnp.float32), pltpu.SemaphoreType.DMA((sh.owners,))],
         compiler_params=params(14),
         cost_estimate=cost(20 * 10**9, 10**7),
         name="halo_part",
-    )(*own, *sides, v_lo, v, v_hi, bwd)
+    )(*own, *sides, v_far, v, v_near, bwd)
 
 
 def selection(slot_ref, count, slots_all):
@@ -546,18 +562,18 @@
     )(c, a, slot, part)
 
 
-def relax_kernel(sh, own, parts, ends_ref, *refs):
+def relax_kernel(sh, own, parts, boxes, *refs):
     r_refs = refs[: len(parts)]
     lo_ref, hi_ref, inv_ref, res_hbm, dir_hbm, *refs = refs[len(parts) :]
     res_ref, one_ref, two_ref, res_out, dir_out, sems = refs
     places = {layer: (ref, i) for part, ref in zip(parts, r_refs) for i, layer in enumerate(part)}
     rows = sh.depth * own
     edge = SWEEPS * own
-    first = pl.multiple_of(ends_ref[0] * own, own)
+    first = pl.multiple_of(lax.axis_index("orb") * own, own)
     inverse = inv_ref[pl.ds(first, own), :]
     inverse = jnp.concatenate([inverse] * (8 // own), 0)
-    keep_lo = inverse * ends_ref[1].astype(jnp.float32)
-    keep_hi = inverse * ends_ref[2].astype(jnp.float32)
+    keep_lo = inverse * (lax.axis_index("box") > 0).astype(jnp.float32)
+    keep_hi = inverse * (lax.axis_index("box") < boxes - 1).astype(jnp.float32)
     tiles = (rows + 2 * edge) // 8
     edge_tiles = edge // 8
 
@@ -669,7 +685,7 @@
         leave(dir_out, dir_hbm, 1, step, group * LANES).wait()
 
 
-def relax(sh, own, parts, ends, pieces, lo, hi, inverse):
+def relax(sh, own, parts, boxes, pieces, lo, hi, inverse):
     rows = (sh.depth + 2 * SWEEPS) * own
     scratch = pltpu.VMEM((sh.chunks, rows, LANES), jnp.float32)
     padded = pltpu.VMEM((sh.chunks + 2, rows, LANES), jnp.float32)
@@ -677,24 +693,29 @@
     hbm = pl.BlockSpec(memory_space=pltpu.HBM)
     vmem = pl.BlockSpec(memory_space=pltpu.VMEM)
     return pl.pallas_call(
-        functools.partial(relax_kernel, sh, own, parts),
+        functools.partial(relax_kernel, sh, own, parts, boxes),
         out_shape=(pltpu.HBM(out, jnp.float32),) * 2,
         out_specs=(hbm, hbm),
-        in_specs=[pl.BlockSpec(memory_space=pltpu.SMEM)] + [vmem] * (3 + len(parts)),
+        in_specs=[vmem] * (3 + len(parts)),
         scratch_shapes=[scratch, padded, padded]
         + [pltpu.VMEM(out, jnp.float32)] * 2
         + [pltpu.SemaphoreType.DMA((2, max(sh.across, sh.chunks)))],
         compiler_params=params(14),
         cost_estimate=cost(10**9, 10**7),
         name="relax",
-    )(ends, *pieces, lo, hi, inverse)
+    )(*pieces, lo, hi, inverse)
+
+
+def pairs(first, count):
+    lower = range(first, count - 1, 2)
+    return [(i, i + 1) for i in lower] + [(i + 1, i) for i in lower]
 
 
 def to_all(value, axes):
     return lax.all_to_all(value, axes, split_axis=0, concat_axis=0, tiled=True)
 
 
-def local(psi, potential, orbital_slot):
+def step(psi, potential, orbital_slot):
     slots, depth, plane = psi.shape
     owners = lax.axis_size("orb")
     boxes = lax.axis_size("box")
@@ -705,18 +726,19 @@
     kinetic = banded(sh.box, sh.box, 0, 0, second_weights(KREACH), -KREACH)
     fwd, bwd, kin = (jnp.asarray(two_part(m)) for m in (magic, magic.T, kinetic))
 
-    upward = [(i, i + 1) for i in range(boxes - 1)]
-    downward = [(i + 1, i) for i in range(boxes - 1)]
-    lo = lax.ppermute(psi, "box", upward)
-    hi = lax.ppermute(psi, "box", downward)
+    swap_far = pairs(1, boxes)
+    swap_near = pairs(0, boxes)
     slot = orbital_slot.reshape(count, 1)
-    pieces = choose(sh, slot, to_all(pack(sh, psi), "orb"))
+    far = lax.ppermute(psi, "box", swap_far)
+    packed = pack(sh, psi)
+    received = to_all(packed, "orb")
+    near = lax.ppermute(psi, "box", swap_near)
     c, w, kin_own = own_part(sh, psi, fwd, kin)
-    w, sent = lax.optimization_barrier((w, potential))
-    v_lo = lax.ppermute(sent, "box", upward)
-    v_hi = lax.ppermute(sent, "box", downward)
-    sides = side_part(sh, lo, hi, fwd)
-    applied = halo_part(sh, (c, w, kin_own), sides, v_lo, potential, v_hi, bwd)
+    pieces = choose(sh, slot, received)
+    v_far = lax.ppermute(potential, "box", swap_far)
+    v_near = lax.ppermute(potential, "box", swap_near)
+    sides = side_part(sh, far, near, fwd)
+    applied = halo_part(sh, (c, w, kin_own), sides, v_far, potential, v_near, bwd)
     applied_pieces = to_all(applied, "orb")
 
     fold = max(1, LANES // count)
@@ -736,18 +758,14 @@
     )
     returned = [to_all(value, "orb") for value in corrected]
     edge = SWEEPS * own
-    box = lax.axis_index("box")
     from_low = lax.ppermute(
         returned[0][-sh.across :, -edge:], "box", [(i, i + 1) for i in range(boxes - 1)]
     )
     from_high = lax.ppermute(
         returned[0][: sh.across, :edge], "box", [(i + 1, i) for i in range(boxes - 1)]
     )
-    ends = jnp.stack(
-        [lax.axis_index("orb"), (box > 0).astype(jnp.int32), (box < boxes - 1).astype(jnp.int32)]
-    ).astype(jnp.int32)
     residual, direction = relax(
-        sh, own, parts, ends, returned, from_low, from_high, inverse
+        sh, own, parts, boxes, returned, from_low, from_high, inverse
     )
     return (residual, direction, multipliers)
 
@@ -755,4 +773,4 @@
 def solution(mesh):
     in_specs = (P("orb", "box", None), P("box", None), P())
     out_specs = (P("orb", "box", None), P("orb", "box", None), P())
-    return jax.shard_map(local, mesh=mesh, in_specs=in_specs, out_specs=out_specs, check_vma=False)
+    return jax.shard_map(step, mesh=mesh, in_specs=in_specs, out_specs=out_specs, check_vma=False)

time: 176 us -> 176 us (level)
  waiting for transfers between devices: 57.2 us -> 64.5 us
  starting transfers between devices: 32.5 us -> 25.4 us
    ppermute x6, starting transfers between devices: 18.1 us -> 11.2 us  [the longest x1 4.53 us: step(): far = lax.ppermute(psi, 'box', swap_far)]
    ppermute x6, waiting for transfers between devices: 0.51 us -> 5.59 us  [the longest x1 5.57 us: step(): far = lax.ppermute(psi, 'box', swap_far)]
    all_to_all x3, waiting for transfers between devices: 56.7 us -> 58.9 us  [to_all(): return lax.all_to_all(value, axes, split_axis=0, concat_axis=0, tiled=True)]
where the time goes in v4:
time: 176 us; the launch traced here: 174 us
  waiting for transfers between devices  64.5 us (37%)
  Pallas kernels  52.5 us (30%)
  blocking collectives  30.2 us (17%)
  starting transfers between devices  25.4 us (14%)
    all_to_all x3, waiting for transfers between devices, to_all(): return lax.all_to_all(value, axes, split_axis=0, concat_axis=0, tiled=True)  58.9 us
    all_to_all x2, blocking collectives, to_all(): return lax.all_to_all(value, axes, split_axis=0, concat_axis=0, tiled=True)  30.2 us
    pallas_call x1, Pallas kernels, halo_part(): pl.pallas_call(functools.partial(halo_kernel, sh), out_shape=pltpu.HBM(ou...  16 us
    all_to_all x3, starting transfers between devices, to_all(): return lax.all_to_all(value, axes, split_axis=0, concat_axis=0, tiled=True)  14.2 us
    pallas_call x1, Pallas kernels, side_part(): pl.pallas_call(functools.partial(side_kernel, sh), out_shape=(jax.ShapeDt...  11.4 us
    pallas_call x1, Pallas kernels, own_part(): pl.pallas_call(functools.partial(own_kernel, sh), out_shape=(full, full,...  8.48 us
    pallas_call x1, Pallas kernels, relax(): pl.pallas_call(functools.partial(relax_kernel, sh, own, parts, boxes), ou...  6.6 us
    ppermute x1, waiting for transfers between devices, step(): far = lax.ppermute(psi, 'box', swap_far)  5.57 us
  transfers between devices with their start and end apart: 9, of which 4 were waited for; matrix products, arithmetic and copies ran while one was open for 0% of the time, Pallas kernels for 24%

profile of v4, /device:TPU:1, one launch (start us, length us, event | category | flops | bytes accessed | tf_op | source)
XLA Modules:
  0.0 173.6 jit_solution(1162999894886115270)
XLA Ops:
  0.6 4.5 %collective-permute-start = (f32[8,16,4096]{2,1,0:T(8,128)}, f32[8,16,4096]{2,1,0:T(8,128)}, u32[]{:S(2)}, u32[]{:S(2)}) collective-permute-start(f32[8,16,4096]{2,1,0:T(8,128)} %psi_ref.1), channel_id=1, source_target_pairs={{1,2},{2,1},{5,6},{6,5},{9,10},{10,9},{13,14},{14,13},{17,18},{18,... | collective-permute-start | bytes 6291464 | tf_op jit(solution)/shard_map/ppermute | solution.py:732
  5.2 0.1 collective-permute-start.1
  5.2 1.9 %collective-permute-start.2 = (f32[16,4096]{1,0:T(8,128)}, f32[16,4096]{1,0:T(8,128)S(1)}, u32[]{:S(2)}, u32[]{:S(2)}) collective-permute-start(f32[16,4096]{1,0:T(8,128)} %v_ref.1), channel_id=1, source_target_pairs={{1,2},{2,1},{5,6},{6,5},{9,10},{10,9},{13,14},{14,13},{17,18},{18,... | collective-permute-start | bytes 786440 | tf_op jit(solution)/shard_map/ppermute | solution.py:738
  7.2 0.1 collective-permute-start.3
  7.3 2.4 %pack.1 = f32[8,8,16,512]{3,2,1,0:T(8,128)} custom-call(f32[8,16,4096]{2,1,0:T(8,128)} %psi_ref.1), custom_call_target="tpu_custom_call" | custom-call | bytes 4194304 | tf_op jit(solution)/shard_map/pack/pallas_call | solution.py:144
  9.7 0.0 copy-start
  9.7 0.0 copy-start.3
  9.7 0.0 copy-start.4
  9.7 5.7 %all-to-all-start = ((f32[8,8,16,512]{3,2,1,0:T(8,128)}), f32[8,8,16,512]{3,2,1,0:T(8,128)}, u32[]{:S(2)}, u32[]{:S(2)}) async-start(f32[8,8,16,512]{3,2,1,0:T(8,128)} %pack.1), calls=%async_computation | async-start | bytes 4194304 | tf_op jit(solution)/shard_map/all_to_all | solution.py:715
  15.4 0.0 copy-done
  15.4 0.0 copy-done.3
  15.4 0.0 copy-done.4
  15.4 8.5 %own_part.1 = (f32[16,32,8,128]{3,2,1,0:T(8,128)S(1)}, f32[16,32,8,128]{3,2,1,0:T(8,128)S(1)}, f32[16,32,8,128]{3,2,1,0:T(8,128)S(1)}) custom-call(f32[8,16,4096]{2,1,0:T(8,128)S(1)} %copy-done, bf16[256,256]{1,0:T(8,128)(2,1)S(1)} %copy-done.3, bf16[256,256]{1,0:T(8,128)(2,1)S(1)} %copy-done.4), custom_call_target="tpu_custom_call" | custom-call | flops 10000000000 | bytes 10000000 | tf_op jit(solution)/shard_map/own_part/pallas_call | solution.py:282
  23.9 0.0 copy-start.1
  23.9 0.0 copy-start.2
  23.9 5.6 %collective-permute-done.far_hbm = f32[8,16,4096]{2,1,0:T(8,128)} collective-permute-done((f32[8,16,4096]{2,1,0:T(8,128)}, f32[8,16,4096]{2,1,0:T(8,128)}, u32[]{:S(2)}, u32[]{:S(2)}) %collective-permute-start) | collective-permute-done | bytes 2097184 | tf_op jit(solution)/shard_map/ppermute | solution.py:732
  29.5 0.0 collective-permute-done.1.near_hbm
  29.5 11.4 %side_part.1 = (f32[16,32,8,128]{3,2,1,0:T(8,128)S(1)}, f32[16,32,8,128]{3,2,1,0:T(8,128)S(1)}, f32[16,32,8,128]{3,2,1,0:T(8,128)S(1)}, f32[16,32,8,128]{3,2,1,0:T(8,128)S(1)}) custom-call(f32[8,16,4096]{2,1,0:T(8,128)} %collective-permute-done.far_hbm, f32[8,16,4096]{2,1,0:T(8,128)} %collective-permute-done.1.near_hbm, bf16[256,256]{1,0:T(8,128)(2,1)S(1)} %copy-done.3), custom_call_target="tpu_custom_call" | custom-call | flops 10000000000 | bytes 10000000 | tf_op jit(solution)/shard_map/side_part/pallas_call | solution.py:333
  40.9 0.0 collective-permute-done.2.vfar_ref
  40.9 0.0 collective-permute-done.3.vnear_ref
  40.9 0.0 copy-done.1
  40.9 0.0 copy-done.2
  40.9 16.0 %halo_part.1 = f32[8,16,8,512]{3,2,1,0:T(8,128)} custom-call(f32[16,32,8,128]{3,2,1,0:T(8,128)S(1)} %get-tuple-element.18.c_ref, f32[16,32,8,128]{3,2,1,0:T(8,128)S(1)} %get-tuple-element.19.w_ref, f32[16,32,8,128]{3,2,1,0:T(8,128)S(1)} %get-tuple-element.20.kin_ref, f32[16,32,8,128]{3,2,1,0:T(8,128)S(1)} %get-tuple-element.21.clo_ref, ...), custom_call_target="tpu_custom_call" | custom-call | flops 20000000000 | bytes 10000000 | tf_op jit(solution)/shard_map/halo_part/pallas_call | solution.py:429
  56.9 0.0 copy-start.5
  56.9 6.2 %all-to-all-done.in_ref = f32[8,8,16,512]{3,2,1,0:T(8,128)} async-done(((f32[8,8,16,512]{3,2,1,0:T(8,128)}), f32[8,8,16,512]{3,2,1,0:T(8,128)}, u32[]{:S(2)}, u32[]{:S(2)}) %all-to-all-start) | async-done | bytes 2097184 | tf_op jit(solution)/shard_map/all_to_all | solution.py:715
  63.1 4.4 %all-to-all-start.1 = ((f32[8,16,8,512]{3,2,1,0:T(8,128)}), f32[8,16,8,512]{3,2,1,0:T(8,128)S(1)}, u32[]{:S(2)}, u32[]{:S(2)}) async-start(f32[8,16,8,512]{3,2,1,0:T(8,128)} %halo_part.1), calls=%async_computation.1 | async-start | bytes 4194304 | tf_op jit(solution)/shard_map/all_to_all | solution.py:715
  67.5 0.0 copy-done.5
  67.5 0.1 copy.9.slot_ref
  67.6 3.5 %choose.1.c_hbm = bf16[16,64,512]{2,1,0:T(8,128)(2,1)} custom-call(s32[32,1]{1,0:T(8,128)S(1)} %copy.9.slot_ref, f32[8,8,16,512]{3,2,1,0:T(8,128)} %all-to-all-done.in_ref), custom_call_target="tpu_custom_call" | custom-call | flops 100000000 | bytes 4194304 | tf_op jit(solution)/shard_map/choose/pallas_call | solution.py:177
  71.2 44.0 %all-to-all-done.1.a_ref = f32[8,16,8,512]{3,2,1,0:T(8,128)S(1)} async-done(((f32[8,16,8,512]{3,2,1,0:T(8,128)}), f32[8,16,8,512]{3,2,1,0:T(8,128)S(1)}, u32[]{:S(2)}, u32[]{:S(2)}) %all-to-all-start.1) | async-done | bytes 2097184 | tf_op jit(solution)/shard_map/all_to_all | solution.py:715
  115.1 2.4 %gram.1 = (f32[32,8,128]{2,1,0:T(8,128)S(1)}, bf16[16,64,512]{2,1,0:T(8,128)(2,1)S(1)}) custom-call(bf16[16,64,512]{2,1,0:T(8,128)(2,1)} %choose.1.c_hbm, f32[8,16,8,512]{3,2,1,0:T(8,128)S(1)} %all-to-all-done.1.a_ref, s32[32,1]{1,0:T(8,128)S(1)} %copy.9.slot_ref), custom_call_target="tpu_custom_call" | custom-call | flops 1000000000 | bytes 10000000 | tf_op jit(solution)/shard_map/gram/pallas_call | solution.py:492
  117.6 13.6 %all_to_all.25.part_ref = f32[32,8,128]{2,1,0:T(8,128)S(1)} all-to-all(f32[32,8,128]{2,1,0:T(8,128)S(1)} %get-tuple-element.26), channel_id=1, replica_groups=mesh['orb'=8,'box'=4] {'orb','box'}, dimensions={0} | all-to-all | bytes 262144 | tf_op jit(solution)/shard_map/all_to_all | solution.py:715
  131.2 1.7 correct.1
  132.9 16.6 %all_to_all.26.refs_0_ = f32[8,32,512]{2,1,0:T(8,128)S(1)} all-to-all(f32[8,32,512]{2,1,0:T(8,128)S(1)} %get-tuple-element.27), channel_id=1, replica_groups=mesh['orb'=8,'box'=4] {'orb'}, dimensions={0} | all-to-all | bytes 1048576 | tf_op jit(solution)/shard_map/all_to_all | solution.py:715
  149.5 4.0 %all-to-all-start.4 = ((f32[8,32,512]{2,1,0:T(8,128)}), f32[8,32,512]{2,1,0:T(8,128)S(1)}, u32[]{:S(2)}, u32[]{:S(2)}) async-start(f32[8,32,512]{2,1,0:T(8,128)} %get-tuple-element.28), calls=%async_computation.4 | async-start | bytes 1048576 | tf_op jit(solution)/shard_map/all_to_all | solution.py:715
  153.6 2.7 %collective-permute-start.4 = (f32[8,16,512]{2,1,0:T(8,128)S(1)}, f32[8,16,512]{2,1,0:T(8,128)S(1)}, u32[]{:S(2)}, u32[]{:S(2)}) collective-permute-start(f32[8,16,512]{2,1,0:T(8,128)S(1)} %get-tuple-element.34), channel_id=1, source_target_pairs={{0,1},{1,2},{2,3},{4,5},{5,6},{6,7},{8,9},{9,10},{10,11},{12,13},{... | collective-permute-start | bytes 786440 | tf_op jit(solution)/shard_map/ppermute | solution.py:761
  156.3 1.9 %collective-permute-start.5 = (f32[8,16,512]{2,1,0:T(8,128)S(1)}, f32[8,16,512]{2,1,0:T(8,128)S(1)}, u32[]{:S(2)}, u32[]{:S(2)}) collective-permute-start(f32[8,16,512]{2,1,0:T(8,128)S(1)} %get-tuple-element.33), channel_id=1, source_target_pairs={{1,0},{2,1},{3,2},{5,4},{6,5},{7,6},{9,8},{10,9},{11,10},{13,12},{... | collective-permute-start | bytes 786440 | tf_op jit(solution)/shard_map/ppermute | solution.py:764
  158.2 8.8 %all-to-all-done.4.refs_1_ = f32[8,32,512]{2,1,0:T(8,128)S(1)} async-done(((f32[8,32,512]{2,1,0:T(8,128)}), f32[8,32,512]{2,1,0:T(8,128)S(1)}, u32[]{:S(2)}, u32[]{:S(2)}) %all-to-all-start.4) | async-done | bytes 524320 | tf_op jit(solution)/shard_map/all_to_all | solution.py:715
  167.0 0.0 collective-permute-done.4.refs_2_
  167.0 0.0 collective-permute-done.5.refs_3_
  167.0 6.6 %relax.1 = (f32[4,16,4096]{2,1,0:T(8,128)}, f32[4,16,4096]{2,1,0:T(8,128)}) custom-call(f32[8,32,512]{2,1,0:T(8,128)S(1)} %all_to_all.26.refs_0_, f32[8,32,512]{2,1,0:T(8,128)S(1)} %all-to-all-done.4.refs_1_, f32[8,16,512]{2,1,0:T(8,128)S(1)} %collective-permute-done.4.refs_2_, f32[8,16,512]{2,1,0:T(8,128)S(1)} %collective-permute-done.5.refs_3_, ...), custom_call_target="tpu_custom_call" | custom-call | flops 1000000000 | bytes 10000000 | tf_op jit(solution)/shard_map/relax/pallas_call | solution.py:695
  (1 shorter events, 0.0 us)
Async XLA Ops:
  0.6 28.9 %collective-permute-start = (f32[8,16,4096]{2,1,0:T(8,128)}, f32[8,16,4096]{2,1,0:T(8,128)}, u32[]{:S(2)}, u32[]{:S(2)}) collective-permute-start(f32[8,16,4096]{2,1,0:T(8,128)} %psi_ref.1), channel_id=1, source_target_pairs={{1,2},{2,1},{5,6},{6,5},{9,10},{10,9},{13,14},{14,13},{17,18},{18,... | collective-permute-start | bytes 6291464 | tf_op jit(solution)/shard_map/ppermute | solution.py:732
  5.2 24.3 %collective-permute-start.1 = (f32[8,16,4096]{2,1,0:T(8,128)}, f32[8,16,4096]{2,1,0:T(8,128)}, u32[]{:S(2)}, u32[]{:S(2)}) collective-permute-start(f32[8,16,4096]{2,1,0:T(8,128)} %psi_ref.1), channel_id=1, source_target_pairs={{0,1},{2,3},{1,0},{3,2},{4,5},{6,7},{5,4},{7,6},{8,9},{10,11},{9,8... | collective-permute-start | bytes 6291464 | tf_op jit(solution)/shard_map/ppermute | solution.py:735
  5.2 35.6 %collective-permute-start.2 = (f32[16,4096]{1,0:T(8,128)}, f32[16,4096]{1,0:T(8,128)S(1)}, u32[]{:S(2)}, u32[]{:S(2)}) collective-permute-start(f32[16,4096]{1,0:T(8,128)} %v_ref.1), channel_id=1, source_target_pairs={{1,2},{2,1},{5,6},{6,5},{9,10},{10,9},{13,14},{14,13},{17,18},{18,... | collective-permute-start | bytes 786440 | tf_op jit(solution)/shard_map/ppermute | solution.py:738
  7.2 33.7 %collective-permute-start.3 = (f32[16,4096]{1,0:T(8,128)}, f32[16,4096]{1,0:T(8,128)S(1)}, u32[]{:S(2)}, u32[]{:S(2)}) collective-permute-start(f32[16,4096]{1,0:T(8,128)} %v_ref.1), channel_id=1, source_target_pairs={{0,1},{2,3},{1,0},{3,2},{4,5},{6,7},{5,4},{7,6},{8,9},{10,11},{9,8... | collective-permute-start | bytes 786440 | tf_op jit(solution)/shard_map/ppermute | solution.py:739
  9.7 5.7 %copy-start = (f32[8,16,4096]{2,1,0:T(8,128)S(1)}, f32[8,16,4096]{2,1,0:T(8,128)}, u32[]{:S(2)}) copy-start(f32[8,16,4096]{2,1,0:T(8,128)} %psi_ref.1) | copy-start | bytes 6291460
  9.7 5.7 %copy-start.3 = (bf16[256,256]{1,0:T(8,128)(2,1)S(1)}, bf16[256,256]{1,0:T(8,128)(2,1)}, u32[]{:S(2)}) copy-start(bf16[256,256]{1,0:T(8,128)(2,1)} %constant.6.clone.fwd_ref) | copy-start | bytes 393220
  9.7 5.7 %copy-start.4 = (bf16[256,256]{1,0:T(8,128)(2,1)S(1)}, bf16[256,256]{1,0:T(8,128)(2,1)}, u32[]{:S(2)}) copy-start(bf16[256,256]{1,0:T(8,128)(2,1)} %constant.8.clone.kin_ref) | copy-start | bytes 393220
  9.7 53.4 %all-to-all-start = ((f32[8,8,16,512]{3,2,1,0:T(8,128)}), f32[8,8,16,512]{3,2,1,0:T(8,128)}, u32[]{:S(2)}, u32[]{:S(2)}) async-start(f32[8,8,16,512]{3,2,1,0:T(8,128)} %pack.1), calls=%async_computation | async-start | bytes 4194304 | tf_op jit(solution)/shard_map/all_to_all | solution.py:715
  23.9 17.0 %copy-start.1 = (f32[16,4096]{1,0:T(8,128)S(1)}, f32[16,4096]{1,0:T(8,128)}, u32[]{:S(2)}) copy-start(f32[16,4096]{1,0:T(8,128)} %v_ref.1) | copy-start | bytes 786436
  23.9 17.0 %copy-start.2 = (bf16[256,256]{1,0:T(8,128)(2,1)S(1)}, bf16[256,256]{1,0:T(8,128)(2,1)}, u32[]{:S(2)}) copy-start(bf16[256,256]{1,0:T(8,128)(2,1)} %constant.7.clone.bwd_ref) | copy-start | bytes 393220
  56.9 10.6 %copy-start.5 = (s32[32]{0:T(128)S(1)}, s32[32]{0:T(128)}, u32[]{:S(2)}) copy-start(s32[32]{0:T(128)} %param.8) | copy-start | bytes 388
  63.1 52.1 %all-to-all-start.1 = ((f32[8,16,8,512]{3,2,1,0:T(8,128)}), f32[8,16,8,512]{3,2,1,0:T(8,128)S(1)}, u32[]{:S(2)}, u32[]{:S(2)}) async-start(f32[8,16,8,512]{3,2,1,0:T(8,128)} %halo_part.1), calls=%async_computation.1 | async-start | bytes 4194304 | tf_op jit(solution)/shard_map/all_to_all | solution.py:715
  149.5 17.5 %all-to-all-start.4 = ((f32[8,32,512]{2,1,0:T(8,128)}), f32[8,32,512]{2,1,0:T(8,128)S(1)}, u32[]{:S(2)}, u32[]{:S(2)}) async-start(f32[8,32,512]{2,1,0:T(8,128)} %get-tuple-element.28), calls=%async_computation.4 | async-start | bytes 1048576 | tf_op jit(solution)/shard_map/all_to_all | solution.py:715
  153.6 13.4 %collective-permute-start.4 = (f32[8,16,512]{2,1,0:T(8,128)S(1)}, f32[8,16,512]{2,1,0:T(8,128)S(1)}, u32[]{:S(2)}, u32[]{:S(2)}) collective-permute-start(f32[8,16,512]{2,1,0:T(8,128)S(1)} %get-tuple-element.34), channel_id=1, source_target_pairs={{0,1},{1,2},{2,3},{4,5},{5,6},{6,7},{8,9},{9,10},{10,11},{12,13},{... | collective-permute-start | bytes 786440 | tf_op jit(solution)/shard_map/ppermute | solution.py:761
  156.3 10.7 %collective-permute-start.5 = (f32[8,16,512]{2,1,0:T(8,128)S(1)}, f32[8,16,512]{2,1,0:T(8,128)S(1)}, u32[]{:S(2)}, u32[]{:S(2)}) collective-permute-start(f32[8,16,512]{2,1,0:T(8,128)S(1)} %get-tuple-element.33), channel_id=1, source_target_pairs={{1,0},{2,1},{3,2},{5,4},{6,5},{7,6},{9,8},{10,9},{11,10},{13,12},{... | collective-permute-start | bytes 786440 | tf_op jit(solution)/shard_map/ppermute | solution.py:764

commit v5 on v4

--- a/solution.py
+++ b/solution.py
@@ -231,6 +231,23 @@
     return out
 
 
+def layer_sum(p, weights, layer, total=None):
+    for k, w in weights.items():
+        value = layer(p + k)
+        if value is not None:
+            total = value * w if total is None else total + value * w
+    return total
+
+
+def layer_sum_even(q, total, layer):
+    for d in range(1, KREACH + 1):
+        terms = [t for t in (layer(q - d), layer(q + d)) if t is not None]
+        if terms:
+            term = terms[0] if len(terms) == 1 else terms[0] + terms[1]
+            total = total + term * KINETIC[d]
+    return total
+
+
 def half_mask(slots):
     return lax.broadcasted_iota(jnp.int32, (slots, LANES), 1) < LANES // 2
 
@@ -260,14 +277,14 @@
     lax.fori_loop(0, sh.across, body, 0)
 
 
-def own_kernel(sh, psi_ref, fwd_ref, kin_ref, c_out, w_out, kin_out, x_ref):
+def own_kernel(sh, psi_ref, fwd_ref, kin_ref, c_out, grid_out, kin_out, x_ref, w_ref):
     lane_pass(sh, psi_ref, c_out, [fwd_ref, kin_ref], [x_ref, kin_out])
     lane = half_mask(sh.slots)
 
     def body(layer, carry):
         even = [x_ref[layer, b] for b in range(sh.chunks)]
         for b, v in enumerate(row_filter(even, odd_pairs(even, lane), MAGIC)):
-            w_out[layer, b] = v
+            w_ref[layer, b] = v
         even = [c_out[layer, b] for b in range(sh.chunks)]
         sums = row_filter_even(even, odd_pairs(even, lane), KINETIC, KREACH)
         for b, v in enumerate(sums):
@@ -275,76 +292,73 @@
         return carry
 
     lax.fori_loop(0, sh.depth, body, 0)
+    depth = sh.depth
+
+    def along_z(chunk, carry):
+        values = [w_ref[z, chunk] for z in range(depth)]
+        for p in range(-LOW, depth + HIGH):
+            grid_out[p + LOW, chunk] = layer_sum(
+                p, MAGIC, lambda z: values[z] if 0 <= z < depth else None
+            )
+        cs = [c_out[z, chunk] for z in range(depth)]
+        for q in range(depth):
+            total = kin_out[q, chunk] + cs[q] * KINETIC[0]
+            kin_out[q, chunk] = layer_sum_even(
+                q, total, lambda z: cs[z] if 0 <= z < depth else None
+            )
+        return carry
+
+    lax.fori_loop(0, sh.chunks, along_z, 0)
 
 
 def own_part(sh, psi, fwd, kin):
     full = jax.ShapeDtypeStruct((sh.depth, sh.chunks, sh.slots, LANES), jnp.float32)
+    grid = jax.ShapeDtypeStruct((sh.depth + LOW + HIGH,) + full.shape[1:], jnp.float32)
     return pl.pallas_call(
         functools.partial(own_kernel, sh),
-        out_shape=(full, full, full),
-        scratch_shapes=[pltpu.VMEM(full.shape, jnp.float32)],
-        compiler_params=params(14),
+        out_shape=(full, grid, full),
+        scratch_shapes=[pltpu.VMEM(full.shape, jnp.float32)] * 2,
+        compiler_params=params(18),
         cost_estimate=cost(10 * 10**9, 10**7),
         name="own_part",
     )(psi, fwd, kin)
 
 
-def side_kernel(
-    sh, far_hbm, near_hbm, fwd_ref, clo_ref, chi_ref, wlo_ref, whi_ref, lo_ref, hi_ref,
-    x_ref, sems,
-):
+def side_kernel(sh, slab_hbm, fwd_ref, c_out, w_out, slab_ref, x_ref, sem):
+    copy = pltpu.make_async_copy(slab_hbm, slab_ref, sem)
+    copy.start()
     lane = half_mask(sh.slots)
-    reach = sh.depth - 1
-
-    def bring(source_lo, source_hi):
-        pltpu.make_async_copy(source_lo, lo_ref, sems.at[0]).start()
-        pltpu.make_async_copy(source_hi, hi_ref, sems.at[1]).start()
-
-    @pl.when(lax.rem(lax.axis_index("box"), 2) == 0)
-    def _():
-        bring(far_hbm, near_hbm)
-
-    @pl.when(lax.rem(lax.axis_index("box"), 2) != 0)
-    def _():
-        bring(near_hbm, far_hbm)
-
-    arrivals = [
-        pltpu.make_async_copy(far_hbm, lo_ref, sems.at[0]),
-        pltpu.make_async_copy(near_hbm, hi_ref, sems.at[1]),
-    ]
-    for copy, side_ref, kept, target, first in (
-        (arrivals[0], lo_ref, clo_ref, wlo_ref, 1),
-        (arrivals[1], hi_ref, chi_ref, whi_ref, 0),
-    ):
-        copy.wait()
-        lane_pass(sh, side_ref, kept, [fwd_ref], [x_ref])
-
-        def filter_rows(layer, carry):
-            even = [x_ref[layer, b] for b in range(sh.chunks)]
-            for b, v in enumerate(row_filter(even, odd_pairs(even, lane), MAGIC)):
-                target[layer, b] = v
-            return carry
-
-        lax.fori_loop(first, first + reach, filter_rows, 0)
-
-
-def side_part(sh, far, near, fwd):
+    copy.wait()
+    lane_pass(sh, slab_ref, c_out, [fwd_ref], [x_ref])
+
+    def filter_rows(layer, carry):
+        even = [x_ref[layer, b] for b in range(sh.chunks)]
+        for b, v in enumerate(row_filter(even, odd_pairs(even, lane), MAGIC)):
+            w_out[layer, b] = v
+        return carry
+
+    lax.fori_loop(0, sh.depth, filter_rows, 0)
+
+
+def side_part(sh, slab, fwd):
     full = (sh.depth, sh.chunks, sh.slots, LANES)
     return pl.pallas_call(
         functools.partial(side_kernel, sh),
-        out_shape=(jax.ShapeDtypeStruct(full, jnp.float32),) * 4,
-        in_specs=[pl.BlockSpec(memory_space=pl.ANY)] * 2
-        + [pl.BlockSpec(memory_space=pltpu.VMEM)],
-        scratch_shapes=[pltpu.VMEM(far.shape, jnp.float32)] * 2
-        + [pltpu.VMEM(full, jnp.float32), pltpu.SemaphoreType.DMA((2,))],
-        compiler_params=params(12),
-        cost_estimate=cost(10 * 10**9, 10**7),
+        out_shape=(jax.ShapeDtypeStruct(full, jnp.float32),) * 2,
+        in_specs=[pl.BlockSpec(memory_space=pl.ANY), pl.BlockSpec(memory_space=pltpu.VMEM)],
+        scratch_shapes=[
+            pltpu.VMEM(slab.shape, jnp.float32),
+            pltpu.VMEM(full, jnp.float32),
+            pltpu.SemaphoreType.DMA,
+        ],
+        compiler_params=params(8),
+        cost_estimate=cost(5 * 10**9, 10**7),
         name="side_part",
-    )(far, near, fwd)
+    )(slab, fwd)
 
 
 def halo_kernel(
-    sh, c_ref, w_ref, kin_ref, clo_ref, chi_ref, wlo_ref, whi_ref, vfar_ref, v_ref,
+    sh, grid_ref, kin_ref, cfar_ref, wfar_ref, cnear_ref, wnear_ref, vfar_ref, v_ref,
     vnear_ref, bwd_ref, out_hbm, x_ref, y_ref, kz_ref, vlo_ref, vhi_ref, out_ref, sems,
 ):
     lane = half_mask(sh.slots)
@@ -353,42 +367,45 @@
     vlo_ref[...] = jnp.where(even, vfar_ref[...], vnear_ref[...])
     vhi_ref[...] = jnp.where(even, vnear_ref[...], vfar_ref[...])
 
-    def along_z(chunk, carry):
+    def along_z(clo_ref, wlo_ref, chi_ref, whi_ref, chunk, carry):
         lanes = pl.ds(pl.multiple_of(chunk * LANES, LANES), LANES)
 
-        def pick(below, here, above, z):
-            ref = below if z < 0 else (here if z < depth else above)
-            return ref[z % depth, chunk]
+        def outside(below, above):
+            places = {}
+
+            def layer(z):
+                if 0 <= z < depth:
+                    return None
+                if z not in places:
+                    places[z] = (below if z < 0 else above)[z % depth, chunk]
+                return places[z]
+
+            return layer
 
         def level(z):
             ref = vlo_ref if z < 0 else (v_ref if z < depth else vhi_ref)
             return jnp.broadcast_to(ref[z % depth : z % depth + 1, lanes], (sh.slots, LANES))
 
-        values = {
-            z: pick(wlo_ref, w_ref, whi_ref, z) for z in range(-LOW - HIGH, depth + LOW + HIGH)
-        }
+        mixed = outside(wlo_ref, whi_ref)
         grid = {}
         for p in range(-LOW, depth + HIGH):
-            total = None
-            for k, w in MAGIC.items():
-                term = values[p + k] * w
-                total = term if total is None else total + term
-            grid[p] = total * level(p)
+            grid[p] = layer_sum(p, MAGIC, mixed, grid_ref[p + LOW, chunk]) * level(p)
         for q in range(depth):
-            total = None
-            for k, w in MAGIC.items():
-                term = grid[q - k] * w
-                total = term if total is None else total + term
-            x_ref[q, chunk] = total
-        cs = {z: pick(clo_ref, c_ref, chi_ref, z) for z in range(-KREACH, depth + KREACH)}
+            x_ref[q, chunk] = layer_sum(q, MAGIC_T, grid.get)
+        coeffs = outside(clo_ref, chi_ref)
         for q in range(depth):
-            total = kin_ref[q, chunk] + cs[q] * KINETIC[0]
-            for d in range(1, KREACH + 1):
-                total = total + (cs[q + d] + cs[q - d]) * KINETIC[d]
-            kz_ref[q, chunk] = total
-        return carry
-
-    lax.fori_loop(0, sh.chunks, along_z, 0)
+            kz_ref[q, chunk] = layer_sum_even(q, kin_ref[q, chunk], coeffs)
+        return carry
+
+    far_pair, near_pair = (cfar_ref, wfar_ref), (cnear_ref, wnear_ref)
+
+    @pl.when(even)
+    def _():
+        lax.fori_loop(0, sh.chunks, functools.partial(along_z, *far_pair, *near_pair), 0)
+
+    @pl.when(jnp.logical_not(even))
+    def _():
+        lax.fori_loop(0, sh.chunks, functools.partial(along_z, *near_pair, *far_pair), 0)
 
     def filter_back(layer, carry):
         even = [x_ref[layer, b] for b in range(sh.chunks)]
@@ -429,7 +446,7 @@
     return pl.pallas_call(
         functools.partial(halo_kernel, sh),
         out_shape=pltpu.HBM(out, jnp.float32),
-        in_specs=[pl.BlockSpec(memory_space=pltpu.VMEM)] * 11,
+        in_specs=[pl.BlockSpec(memory_space=pltpu.VMEM)] * 10,
         out_specs=pl.BlockSpec(memory_space=pltpu.HBM),
         scratch_shapes=[full] * 3
         + [pltpu.VMEM(v.shape, jnp.float32)] * 2
@@ -733,12 +750,14 @@
     packed = pack(sh, psi)
     received = to_all(packed, "orb")
     near = lax.ppermute(psi, "box", swap_near)
-    c, w, kin_own = own_part(sh, psi, fwd, kin)
+    own_grid, own_kin = own_part(sh, psi, fwd, kin)[1:]
     pieces = choose(sh, slot, received)
     v_far = lax.ppermute(potential, "box", swap_far)
     v_near = lax.ppermute(potential, "box", swap_near)
-    sides = side_part(sh, far, near, fwd)
-    applied = halo_part(sh, (c, w, kin_own), sides, v_far, potential, v_near, bwd)
+    near_side = side_part(sh, near, fwd)
+    far_side = side_part(sh, far, fwd)
+    sides = tuple(far_side) + tuple(near_side)
+    applied = halo_part(sh, (own_grid, own_kin), sides, v_far, potential, v_near, bwd)
     applied_pieces = to_all(applied, "orb")
 
     fold = max(1, LANES // count)

time: 176 us -> 176 us (level)
  Pallas kernels: 52.5 us -> 56.6 us
  waiting for transfers between devices: 64.5 us -> 60.4 us
    pallas_call x1, Pallas kernels: 8.48 us -> 14.1 us  [own_part(): pl.pallas_call(functools.partial(own_kernel, sh), out_shape=(full, grid,...]
    ppermute x1, waiting for transfers between devices: 5.57 us -> 0.01 us  [step(): far = lax.ppermute(psi, 'box', swap_far)]
    pallas_call x1, Pallas kernels: 16 us -> 12.4 us  [halo_part(): pl.pallas_call(functools.partial(halo_kernel, sh), out_shape=pltpu.HBM(ou...]
    pallas_call x1 -> x2, Pallas kernels: 11.4 us -> 13.4 us  [side_part(): pl.pallas_call(functools.partial(side_kernel, sh), out_shape=(jax.ShapeDt...]
  transfers between devices with their start and end apart: 9 -> 9, of which waited for: 4 -> 3; matrix products, arithmetic and copies ran while one was open for 0% -> 0% of each run, Pallas kernels for 24% -> 26%
where the time goes in v5:
time: 176 us; the launch traced here: 174 us
  waiting for transfers between devices  60.4 us (34%)
  Pallas kernels  56.6 us (32%)
  blocking collectives  30.2 us (17%)
  starting transfers between devices  25.4 us (14%)
    all_to_all x3, waiting for transfers between devices, to_all(): return lax.all_to_all(value, axes, split_axis=0, concat_axis=0, tiled=True)  60.4 us
    all_to_all x2, blocking collectives, to_all(): return lax.all_to_all(value, axes, split_axis=0, concat_axis=0, tiled=True)  30.2 us
    all_to_all x3, starting transfers between devices, to_all(): return lax.all_to_all(value, axes, split_axis=0, concat_axis=0, tiled=True)  14.2 us
    pallas_call x1, Pallas kernels, own_part(): pl.pallas_call(functools.partial(own_kernel, sh), out_shape=(full, grid,...  14.1 us
    pallas_call x2, Pallas kernels, side_part(): pl.pallas_call(functools.partial(side_kernel, sh), out_shape=(jax.ShapeDt...  13.4 us
    pallas_call x1, Pallas kernels, halo_part(): pl.pallas_call(functools.partial(halo_kernel, sh), out_shape=pltpu.HBM(ou...  12.4 us
    pallas_call x1, Pallas kernels, relax(): pl.pallas_call(functools.partial(relax_kernel, sh, own, parts, boxes), ou...  6.6 us
    ppermute x1, starting transfers between devices, step(): far = lax.ppermute(psi, 'box', swap_far)  4.53 us
  transfers between devices with their start and end apart: 9, of which 3 were waited for; matrix products, arithmetic and copies ran while one was open for 0% of the time, Pallas kernels for 26%

profile of v5, /device:TPU:1, one launch (start us, length us, event | category | flops | bytes accessed | tf_op | source)
XLA Modules:
  0.0 173.6 jit_solution(1225481534553413645)
XLA Ops:
  0.6 4.5 %collective-permute-start = (f32[8,16,4096]{2,1,0:T(8,128)}, f32[8,16,4096]{2,1,0:T(8,128)}, u32[]{:S(2)}, u32[]{:S(2)}) collective-permute-start(f32[8,16,4096]{2,1,0:T(8,128)} %psi_ref.1), channel_id=1, source_target_pairs={{1,2},{2,1},{5,6},{6,5},{9,10},{10,9},{13,14},{14,13},{17,18},{18,... | collective-permute-start | bytes 6291464 | tf_op jit(solution)/shard_map/ppermute | solution.py:749
  5.2 0.1 collective-permute-start.1
  5.2 1.9 %collective-permute-start.2 = (f32[16,4096]{1,0:T(8,128)}, f32[16,4096]{1,0:T(8,128)S(1)}, u32[]{:S(2)}, u32[]{:S(2)}) collective-permute-start(f32[16,4096]{1,0:T(8,128)} %v_ref.1), channel_id=1, source_target_pairs={{1,2},{2,1},{5,6},{6,5},{9,10},{10,9},{13,14},{14,13},{17,18},{18,... | collective-permute-start | bytes 786440 | tf_op jit(solution)/shard_map/ppermute | solution.py:755
  7.2 0.1 collective-permute-start.3
  7.3 2.4 %pack.1 = f32[8,8,16,512]{3,2,1,0:T(8,128)} custom-call(f32[8,16,4096]{2,1,0:T(8,128)} %psi_ref.1), custom_call_target="tpu_custom_call" | custom-call | bytes 4194304 | tf_op jit(solution)/shard_map/pack/pallas_call | solution.py:144
  9.7 0.0 copy-start
  9.7 0.0 copy-start.3
  9.7 0.0 copy-start.4
  9.7 5.7 %all-to-all-start = ((f32[8,8,16,512]{3,2,1,0:T(8,128)}), f32[8,8,16,512]{3,2,1,0:T(8,128)}, u32[]{:S(2)}, u32[]{:S(2)}) async-start(f32[8,8,16,512]{3,2,1,0:T(8,128)} %pack.1), calls=%async_computation | async-start | bytes 4194304 | tf_op jit(solution)/shard_map/all_to_all | solution.py:732
  15.4 0.0 copy-done
  15.4 0.0 copy-done.3
  15.4 0.0 copy-done.4
  15.4 14.1 %own_part.1 = (f32[16,32,8,128]{3,2,1,0:T(8,128)}, f32[31,32,8,128]{3,2,1,0:T(8,128)S(1)}, f32[16,32,8,128]{3,2,1,0:T(8,128)S(1)}) custom-call(f32[8,16,4096]{2,1,0:T(8,128)S(1)} %copy-done, bf16[256,256]{1,0:T(8,128)(2,1)S(1)} %copy-done.3, bf16[256,256]{1,0:T(8,128)(2,1)S(1)} %copy-done.4), custom_call_target="tpu_custom_call" | custom-call | flops 10000000000 | bytes 10000000 | tf_op jit(solution)/shard_map/own_part/pallas_call | solution.py:317
  29.5 0.0 collective-permute-done.slab_hbm
  29.5 6.7 %side_part.2 = (f32[16,32,8,128]{3,2,1,0:T(8,128)S(1)}, f32[16,32,8,128]{3,2,1,0:T(8,128)S(1)}) custom-call(f32[8,16,4096]{2,1,0:T(8,128)} %collective-permute-done.slab_hbm, bf16[256,256]{1,0:T(8,128)(2,1)S(1)} %copy-done.3), custom_call_target="tpu_custom_call" | custom-call | flops 5000000000 | bytes 10000000 | tf_op jit(solution)/shard_map/side_part/pallas_call | solution.py:345
  36.2 0.0 copy-start.1
  36.2 0.0 copy-start.2
  36.2 0.0 collective-permute-done.1.slab_hbm
  36.2 6.7 %side_part.3 = (f32[16,32,8,128]{3,2,1,0:T(8,128)S(1)}, f32[16,32,8,128]{3,2,1,0:T(8,128)S(1)}) custom-call(f32[8,16,4096]{2,1,0:T(8,128)} %collective-permute-done.1.slab_hbm, bf16[256,256]{1,0:T(8,128)(2,1)S(1)} %copy-done.3), custom_call_target="tpu_custom_call" | custom-call | flops 5000000000 | bytes 10000000 | tf_op jit(solution)/shard_map/side_part/pallas_call | solution.py:345
  43.0 0.0 collective-permute-done.2.vfar_ref
  43.0 0.0 collective-permute-done.3.vnear_ref
  43.0 0.0 copy-done.1
  43.0 0.0 copy-done.2
  43.0 12.4 %halo_part.1 = f32[8,16,8,512]{3,2,1,0:T(8,128)} custom-call(f32[31,32,8,128]{3,2,1,0:T(8,128)S(1)} %get-tuple-element.17.grid_ref, f32[16,32,8,128]{3,2,1,0:T(8,128)S(1)} %get-tuple-element.18.kin_ref, f32[16,32,8,128]{3,2,1,0:T(8,128)S(1)} %get-tuple-element.19.cfar_ref, f32[16,32,8,128]{3,2,1,0:T(8,128)S(1)} %get-tuple-element.20.wfar_ref, ...), custom_call_target="tpu_custom_call" | custom-call | flops 20000000000 | bytes 10000000 | tf_op jit(solution)/shard_map/halo_part/pallas_call | solution.py:446
  55.4 0.0 copy-start.5
  55.5 7.6 %all-to-all-done.in_ref = f32[8,8,16,512]{3,2,1,0:T(8,128)} async-done(((f32[8,8,16,512]{3,2,1,0:T(8,128)}), f32[8,8,16,512]{3,2,1,0:T(8,128)}, u32[]{:S(2)}, u32[]{:S(2)}) %all-to-all-start) | async-done | bytes 2097184 | tf_op jit(solution)/shard_map/all_to_all | solution.py:732
  63.1 4.4 %all-to-all-start.1 = ((f32[8,16,8,512]{3,2,1,0:T(8,128)}), f32[8,16,8,512]{3,2,1,0:T(8,128)S(1)}, u32[]{:S(2)}, u32[]{:S(2)}) async-start(f32[8,16,8,512]{3,2,1,0:T(8,128)} %halo_part.1), calls=%async_computation.1 | async-start | bytes 4194304 | tf_op jit(solution)/shard_map/all_to_all | solution.py:732
  67.5 0.0 copy-done.5
  67.5 0.1 copy.9.slot_ref
  67.6 3.5 %choose.1.c_hbm = bf16[16,64,512]{2,1,0:T(8,128)(2,1)} custom-call(s32[32,1]{1,0:T(8,128)S(1)} %copy.9.slot_ref, f32[8,8,16,512]{3,2,1,0:T(8,128)} %all-to-all-done.in_ref), custom_call_target="tpu_custom_call" | custom-call | flops 100000000 | bytes 4194304 | tf_op jit(solution)/shard_map/choose/pallas_call | solution.py:177
  71.2 44.0 %all-to-all-done.1.a_ref = f32[8,16,8,512]{3,2,1,0:T(8,128)S(1)} async-done(((f32[8,16,8,512]{3,2,1,0:T(8,128)}), f32[8,16,8,512]{3,2,1,0:T(8,128)S(1)}, u32[]{:S(2)}, u32[]{:S(2)}) %all-to-all-start.1) | async-done | bytes 2097184 | tf_op jit(solution)/shard_map/all_to_all | solution.py:732
  115.2 2.4 %gram.1 = (f32[32,8,128]{2,1,0:T(8,128)S(1)}, bf16[16,64,512]{2,1,0:T(8,128)(2,1)S(1)}) custom-call(bf16[16,64,512]{2,1,0:T(8,128)(2,1)} %choose.1.c_hbm, f32[8,16,8,512]{3,2,1,0:T(8,128)S(1)} %all-to-all-done.1.a_ref, s32[32,1]{1,0:T(8,128)S(1)} %copy.9.slot_ref), custom_call_target="tpu_custom_call" | custom-call | flops 1000000000 | bytes 10000000 | tf_op jit(solution)/shard_map/gram/pallas_call | solution.py:509
  117.6 13.6 %all_to_all.25.part_ref = f32[32,8,128]{2,1,0:T(8,128)S(1)} all-to-all(f32[32,8,128]{2,1,0:T(8,128)S(1)} %get-tuple-element.24), channel_id=1, replica_groups=mesh['orb'=8,'box'=4] {'orb','box'}, dimensions={0} | all-to-all | bytes 262144 | tf_op jit(solution)/shard_map/all_to_all | solution.py:732
  131.2 1.7 correct.1
  132.9 16.6 %all_to_all.26.refs_0_ = f32[8,32,512]{2,1,0:T(8,128)S(1)} all-to-all(f32[8,32,512]{2,1,0:T(8,128)S(1)} %get-tuple-element.25), channel_id=1, replica_groups=mesh['orb'=8,'box'=4] {'orb'}, dimensions={0} | all-to-all | bytes 1048576 | tf_op jit(solution)/shard_map/all_to_all | solution.py:732
  149.5 4.0 %all-to-all-start.4 = ((f32[8,32,512]{2,1,0:T(8,128)}), f32[8,32,512]{2,1,0:T(8,128)S(1)}, u32[]{:S(2)}, u32[]{:S(2)}) async-start(f32[8,32,512]{2,1,0:T(8,128)} %get-tuple-element.26), calls=%async_computation.4 | async-start | bytes 1048576 | tf_op jit(solution)/shard_map/all_to_all | solution.py:732
  153.6 2.7 %collective-permute-start.4 = (f32[8,16,512]{2,1,0:T(8,128)S(1)}, f32[8,16,512]{2,1,0:T(8,128)S(1)}, u32[]{:S(2)}, u32[]{:S(2)}) collective-permute-start(f32[8,16,512]{2,1,0:T(8,128)S(1)} %get-tuple-element.32), channel_id=1, source_target_pairs={{0,1},{1,2},{2,3},{4,5},{5,6},{6,7},{8,9},{9,10},{10,11},{12,13},{... | collective-permute-start | bytes 786440 | tf_op jit(solution)/shard_map/ppermute | solution.py:780
  156.3 1.9 %collective-permute-start.5 = (f32[8,16,512]{2,1,0:T(8,128)S(1)}, f32[8,16,512]{2,1,0:T(8,128)S(1)}, u32[]{:S(2)}, u32[]{:S(2)}) collective-permute-start(f32[8,16,512]{2,1,0:T(8,128)S(1)} %get-tuple-element.31), channel_id=1, source_target_pairs={{1,0},{2,1},{3,2},{5,4},{6,5},{7,6},{9,8},{10,9},{11,10},{13,12},{... | collective-permute-start | bytes 786440 | tf_op jit(solution)/shard_map/ppermute | solution.py:783
  158.2 8.8 %all-to-all-done.4.refs_1_ = f32[8,32,512]{2,1,0:T(8,128)S(1)} async-done(((f32[8,32,512]{2,1,0:T(8,128)}), f32[8,32,512]{2,1,0:T(8,128)S(1)}, u32[]{:S(2)}, u32[]{:S(2)}) %all-to-all-start.4) | async-done | bytes 524320 | tf_op jit(solution)/shard_map/all_to_all | solution.py:732
  167.0 0.0 collective-permute-done.4.refs_2_
  167.0 0.0 collective-permute-done.5.refs_3_
  167.0 6.6 %relax.1 = (f32[4,16,4096]{2,1,0:T(8,128)}, f32[4,16,4096]{2,1,0:T(8,128)}) custom-call(f32[8,32,512]{2,1,0:T(8,128)S(1)} %all_to_all.26.refs_0_, f32[8,32,512]{2,1,0:T(8,128)S(1)} %all-to-all-done.4.refs_1_, f32[8,16,512]{2,1,0:T(8,128)S(1)} %collective-permute-done.4.refs_2_, f32[8,16,512]{2,1,0:T(8,128)S(1)} %collective-permute-done.5.refs_3_, ...), custom_call_target="tpu_custom_call" | custom-call | flops 1000000000 | bytes 10000000 | tf_op jit(solution)/shard_map/relax/pallas_call | solution.py:712
  (1 shorter events, 0.0 us)
Async XLA Ops:
  0.6 28.9 %collective-permute-start = (f32[8,16,4096]{2,1,0:T(8,128)}, f32[8,16,4096]{2,1,0:T(8,128)}, u32[]{:S(2)}, u32[]{:S(2)}) collective-permute-start(f32[8,16,4096]{2,1,0:T(8,128)} %psi_ref.1), channel_id=1, source_target_pairs={{1,2},{2,1},{5,6},{6,5},{9,10},{10,9},{13,14},{14,13},{17,18},{18,... | collective-permute-start | bytes 6291464 | tf_op jit(solution)/shard_map/ppermute | solution.py:749
  5.2 31.1 %collective-permute-start.1 = (f32[8,16,4096]{2,1,0:T(8,128)}, f32[8,16,4096]{2,1,0:T(8,128)}, u32[]{:S(2)}, u32[]{:S(2)}) collective-permute-start(f32[8,16,4096]{2,1,0:T(8,128)} %psi_ref.1), channel_id=1, source_target_pairs={{0,1},{2,3},{1,0},{3,2},{4,5},{6,7},{5,4},{7,6},{8,9},{10,11},{9,8... | collective-permute-start | bytes 6291464 | tf_op jit(solution)/shard_map/ppermute | solution.py:752
  5.2 37.7 %collective-permute-start.2 = (f32[16,4096]{1,0:T(8,128)}, f32[16,4096]{1,0:T(8,128)S(1)}, u32[]{:S(2)}, u32[]{:S(2)}) collective-permute-start(f32[16,4096]{1,0:T(8,128)} %v_ref.1), channel_id=1, source_target_pairs={{1,2},{2,1},{5,6},{6,5},{9,10},{10,9},{13,14},{14,13},{17,18},{18,... | collective-permute-start | bytes 786440 | tf_op jit(solution)/shard_map/ppermute | solution.py:755
  7.2 35.8 %collective-permute-start.3 = (f32[16,4096]{1,0:T(8,128)}, f32[16,4096]{1,0:T(8,128)S(1)}, u32[]{:S(2)}, u32[]{:S(2)}) collective-permute-start(f32[16,4096]{1,0:T(8,128)} %v_ref.1), channel_id=1, source_target_pairs={{0,1},{2,3},{1,0},{3,2},{4,5},{6,7},{5,4},{7,6},{8,9},{10,11},{9,8... | collective-permute-start | bytes 786440 | tf_op jit(solution)/shard_map/ppermute | solution.py:756
  9.7 5.7 %copy-start = (f32[8,16,4096]{2,1,0:T(8,128)S(1)}, f32[8,16,4096]{2,1,0:T(8,128)}, u32[]{:S(2)}) copy-start(f32[8,16,4096]{2,1,0:T(8,128)} %psi_ref.1) | copy-start | bytes 6291460
  9.7 5.7 %copy-start.3 = (bf16[256,256]{1,0:T(8,128)(2,1)S(1)}, bf16[256,256]{1,0:T(8,128)(2,1)}, u32[]{:S(2)}) copy-start(bf16[256,256]{1,0:T(8,128)(2,1)} %constant.6.clone.fwd_ref) | copy-start | bytes 393220
  9.7 5.7 %copy-start.4 = (bf16[256,256]{1,0:T(8,128)(2,1)S(1)}, bf16[256,256]{1,0:T(8,128)(2,1)}, u32[]{:S(2)}) copy-start(bf16[256,256]{1,0:T(8,128)(2,1)} %constant.8.clone.kin_ref) | copy-start | bytes 393220
  9.7 53.4 %all-to-all-start = ((f32[8,8,16,512]{3,2,1,0:T(8,128)}), f32[8,8,16,512]{3,2,1,0:T(8,128)}, u32[]{:S(2)}, u32[]{:S(2)}) async-start(f32[8,8,16,512]{3,2,1,0:T(8,128)} %pack.1), calls=%async_computation | async-start | bytes 4194304 | tf_op jit(solution)/shard_map/all_to_all | solution.py:732
  36.2 6.8 %copy-start.1 = (f32[16,4096]{1,0:T(8,128)S(1)}, f32[16,4096]{1,0:T(8,128)}, u32[]{:S(2)}) copy-start(f32[16,4096]{1,0:T(8,128)} %v_ref.1) | copy-start | bytes 786436
  36.2 6.8 %copy-start.2 = (bf16[256,256]{1,0:T(8,128)(2,1)S(1)}, bf16[256,256]{1,0:T(8,128)(2,1)}, u32[]{:S(2)}) copy-start(bf16[256,256]{1,0:T(8,128)(2,1)} %constant.7.clone.bwd_ref) | copy-start | bytes 393220
  55.4 12.1 %copy-start.5 = (s32[32]{0:T(128)S(1)}, s32[32]{0:T(128)}, u32[]{:S(2)}) copy-start(s32[32]{0:T(128)} %param.8) | copy-start | bytes 388
  63.1 52.1 %all-to-all-start.1 = ((f32[8,16,8,512]{3,2,1,0:T(8,128)}), f32[8,16,8,512]{3,2,1,0:T(8,128)S(1)}, u32[]{:S(2)}, u32[]{:S(2)}) async-start(f32[8,16,8,512]{3,2,1,0:T(8,128)} %halo_part.1), calls=%async_computation.1 | async-start | bytes 4194304 | tf_op jit(solution)/shard_map/all_to_all | solution.py:732
  149.5 17.5 %all-to-all-start.4 = ((f32[8,32,512]{2,1,0:T(8,128)}), f32[8,32,512]{2,1,0:T(8,128)S(1)}, u32[]{:S(2)}, u32[]{:S(2)}) async-start(f32[8,32,512]{2,1,0:T(8,128)} %get-tuple-element.26), calls=%async_computation.4 | async-start | bytes 1048576 | tf_op jit(solution)/shard_map/all_to_all | solution.py:732
  153.6 13.4 %collective-permute-start.4 = (f32[8,16,512]{2,1,0:T(8,128)S(1)}, f32[8,16,512]{2,1,0:T(8,128)S(1)}, u32[]{:S(2)}, u32[]{:S(2)}) collective-permute-start(f32[8,16,512]{2,1,0:T(8,128)S(1)} %get-tuple-element.32), channel_id=1, source_target_pairs={{0,1},{1,2},{2,3},{4,5},{5,6},{6,7},{8,9},{9,10},{10,11},{12,13},{... | collective-permute-start | bytes 786440 | tf_op jit(solution)/shard_map/ppermute | solution.py:780
  156.3 10.7 %collective-permute-start.5 = (f32[8,16,512]{2,1,0:T(8,128)S(1)}, f32[8,16,512]{2,1,0:T(8,128)S(1)}, u32[]{:S(2)}, u32[]{:S(2)}) collective-permute-start(f32[8,16,512]{2,1,0:T(8,128)S(1)} %get-tuple-element.31), channel_id=1, source_target_pairs={{1,0},{2,1},{3,2},{5,4},{6,5},{7,6},{9,8},{10,9},{11,10},{13,12},{... | collective-permute-start | bytes 786440 | tf_op jit(solution)/shard_map/ppermute | solution.py:783

commit v6 on v5

--- a/solution.py
+++ b/solution.py
@@ -599,7 +599,7 @@
             return keep_lo
         return keep_hi if tile >= tiles - edge_tiles else inverse
 
-    group = min(16, sh.chunks)
+    group = min(32, sh.chunks)
     blank = jnp.zeros((rows + 2 * edge, LANES), jnp.float32)
     for ref in (one_ref, two_ref):
         ref[0] = blank
@@ -611,34 +611,57 @@
             source.at[:, :, lanes], target.at[:, :, lanes], sems.at[kind, step]
         )
 
+    half = sh.chunks // 2
+    left = lax.broadcasted_iota(jnp.int32, (8, LANES), 1) < LANES // 2
+    assert sh.across % 2 == 0
+
+    def turned(value):
+        return pltpu.roll(value, LANES // 2, 1)
+
+    def column_of(block, inner):
+        lanes = slice(inner * LANES, (inner + 1) * LANES)
+        pieces = [lo_ref[block, :, lanes]]
+        for g in range(sh.layered):
+            for layer in range(sh.layers):
+                ref, i = places[layer]
+                pieces.append(ref[g * sh.across + block, i * own : (i + 1) * own, lanes])
+        pieces += [hi_ref[block, :, lanes]]
+        return jnp.concatenate(pieces, 0)
+
     def gather(block, carry):
+        other = block + sh.across // 2
         for inner in range(sh.inner):
             chunk = block * sh.inner + inner
-            lanes = slice(inner * LANES, (inner + 1) * LANES)
-            pieces = [lo_ref[block, :, lanes]]
-            for g in range(sh.layered):
-                for layer in range(sh.layers):
-                    ref, i = places[layer]
-                    pieces.append(ref[g * sh.across + block, i * own : (i + 1) * own, lanes])
-            pieces += [hi_ref[block, :, lanes]]
-            column = jnp.concatenate(pieces, 0)
+            columns = (column_of(block, inner), column_of(other, inner))
             for tile in range(tiles):
-                value = column[tile * 8 : (tile + 1) * 8]
-                res_ref[chunk, tile * 8 : (tile + 1) * 8] = value
-                one_ref[chunk + 1, tile * 8 : (tile + 1) * 8] = value * scale(tile)
-            out_lanes = pl.ds(pl.multiple_of(chunk * LANES, LANES), LANES)
-            for orbital in range(own):
-                here = pl.ds(edge + orbital, sh.depth, stride=own)
-                res_out[orbital, :, out_lanes] = res_ref[chunk, here, :]
+                here = slice(tile * 8, (tile + 1) * 8)
+                low, high = columns[0][here], columns[1][here]
+                mixed = (jnp.where(left, low, turned(high)), jnp.where(left, turned(low), high))
+                for k in range(2):
+                    res_ref[2 * chunk + k, here] = mixed[k]
+                    one_ref[2 * chunk + k + 1, here] = mixed[k] * scale(tile)
+            for column, place in zip(columns, (chunk, chunk + half)):
+                two_ref[place + 1] = column
+                out_lanes = pl.ds(pl.multiple_of(place * LANES, LANES), LANES)
+                for orbital in range(own):
+                    rows_of = pl.ds(edge + orbital, sh.depth, stride=own)
+                    res_out[orbital, :, out_lanes] = two_ref[place + 1, rows_of, :]
         leave(res_out, res_hbm, 0, block, sh.width).start()
+        leave(res_out, res_hbm, 0, other, sh.width).start()
         return carry
 
-    lax.fori_loop(0, sh.across, gather, 0)
-
+    lax.fori_loop(0, sh.across // 2, gather, 0)
+
+    def seal(ref):
+        for tile in range(tiles):
+            here = slice(tile * 8, (tile + 1) * 8)
+            ref[0, here] = jnp.where(left, 0.0, turned(ref[sh.chunks, here]))
+            ref[sh.chunks + 1, here] = jnp.where(left, turned(ref[1, here]), 0.0)
+
+    seal(one_ref)
     sub = lax.broadcasted_iota(jnp.int32, (8, LANES), 0)
     lane = lax.broadcasted_iota(jnp.int32, (8, LANES), 1)
     upper = sub >= own
-    right_half = lane >= LANES // 2
     not_last = (lane % sh.box) != sh.box - 1
     not_first = (lane % sh.box) != 0
     assert 8 // own == 2
@@ -662,10 +685,7 @@
                         upper, value_at(column, tile - 1), value_at(column, tile + 1)
                     )
                     along_z = pltpu.roll(value + beside, own, 0)
-                    beside = jnp.where(
-                        right_half, value_at(column - 1, tile), value_at(column + 1, tile)
-                    )
-                    along_y = pltpu.roll(value + beside, LANES // 2, 1)
+                    along_y = value_at(column - 1, tile) + value_at(column + 1, tile)
                     along_x = pltpu.roll(jnp.where(not_last, value, 0.0), 1, 1) + pltpu.roll(
                         jnp.where(not_first, value, 0.0), LANES - 1, 1
                     )
@@ -683,23 +703,34 @@
     for done in range(1, SWEEPS + 1):
         first_tile = done * own // 8
         sweep(source, target, range(first_tile, tiles - first_tile))
+        if done < SWEEPS:
+            seal(target)
         source, target = target, source
 
+    few = min(8, half)
+
     def spread(step, carry):
-        for column in range(group):
-            chunk = step * group + column
-            out_lanes = pl.ds(pl.multiple_of(chunk * LANES, LANES), LANES)
-            for orbital in range(own):
-                here = pl.ds(edge + orbital, sh.depth, stride=own)
-                dir_out[orbital, :, out_lanes] = source[chunk + 1, here, :]
-        leave(dir_out, dir_hbm, 1, step, group * LANES).start()
+        for column in range(few):
+            chunk = step * few + column
+            for tile in range(edge_tiles, tiles - edge_tiles):
+                here = slice(tile * 8, (tile + 1) * 8)
+                even, odd = source[2 * chunk + 1, here], source[2 * chunk + 2, here]
+                target[chunk + 1, here] = jnp.where(left, even, turned(odd))
+                target[chunk + half + 1, here] = jnp.where(left, turned(even), odd)
+            for place in (chunk, chunk + half):
+                out_lanes = pl.ds(pl.multiple_of(place * LANES, LANES), LANES)
+                for orbital in range(own):
+                    rows_of = pl.ds(edge + orbital, sh.depth, stride=own)
+                    dir_out[orbital, :, out_lanes] = target[place + 1, rows_of, :]
+        leave(dir_out, dir_hbm, 1, step, few * LANES).start()
+        leave(dir_out, dir_hbm, 1, step + half // few, few * LANES).start()
         return carry
 
-    lax.fori_loop(0, sh.chunks // group, spread, 0)
+    lax.fori_loop(0, half // few, spread, 0)
     for block in range(sh.across):
         leave(res_out, res_hbm, 0, block, sh.width).wait()
-    for step in range(sh.chunks // group):
-        leave(dir_out, dir_hbm, 1, step, group * LANES).wait()
+    for step in range(sh.chunks // few):
+        leave(dir_out, dir_hbm, 1, step, few * LANES).wait()
 
 
 def relax(sh, own, parts, boxes, pieces, lo, hi, inverse):

time: 176 us -> 175 us (level)
  transfers between devices with their start and end apart: 9 -> 9, of which waited for: 3 -> 3; matrix products, arithmetic and copies ran while one was open for 0% -> 0% of each run, Pallas kernels for 26% -> 27%
where the time goes in v6:
time: 175 us; the launch traced here: 173 us
  waiting for transfers between devices  60.4 us (35%)
  Pallas kernels  55.7 us (32%)
  blocking collectives  30.2 us (17%)
  starting transfers between devices  25.4 us (15%)
    all_to_all x3, waiting for transfers between devices, to_all(): return lax.all_to_all(value, axes, split_axis=0, concat_axis=0, tiled=True)  60.4 us
    all_to_all x2, blocking collectives, to_all(): return lax.all_to_all(value, axes, split_axis=0, concat_axis=0, tiled=True)  30.2 us
    all_to_all x3, starting transfers between devices, to_all(): return lax.all_to_all(value, axes, split_axis=0, concat_axis=0, tiled=True)  14.2 us
    pallas_call x1, Pallas kernels, own_part(): pl.pallas_call(functools.partial(own_kernel, sh), out_shape=(full, grid,...  14.1 us
    pallas_call x2, Pallas kernels, side_part(): pl.pallas_call(functools.partial(side_kernel, sh), out_shape=(jax.ShapeDt...  13.4 us
    pallas_call x1, Pallas kernels, halo_part(): pl.pallas_call(functools.partial(halo_kernel, sh), out_shape=pltpu.HBM(ou...  12.4 us
    pallas_call x1, Pallas kernels, relax(): pl.pallas_call(functools.partial(relax_kernel, sh, own, parts, boxes), ou...  5.68 us
    ppermute x1, starting transfers between devices, step(): far = lax.ppermute(psi, 'box', swap_far)  4.53 us
  transfers between devices with their start and end apart: 9, of which 3 were waited for; matrix products, arithmetic and copies ran while one was open for 0% of the time, Pallas kernels for 27%

profile of v6, /device:TPU:1, one launch (start us, length us, event | category | flops | bytes accessed | tf_op | source)
XLA Modules:
  0.0 172.7 jit_solution(17516212554278091109)
XLA Ops:
  0.6 4.5 %collective-permute-start = (f32[8,16,4096]{2,1,0:T(8,128)}, f32[8,16,4096]{2,1,0:T(8,128)}, u32[]{:S(2)}, u32[]{:S(2)}) collective-permute-start(f32[8,16,4096]{2,1,0:T(8,128)} %psi_ref.1), channel_id=1, source_target_pairs={{1,2},{2,1},{5,6},{6,5},{9,10},{10,9},{13,14},{14,13},{17,18},{18,... | collective-permute-start | bytes 6291464 | tf_op jit(solution)/shard_map/ppermute | solution.py:780
  5.2 0.1 collective-permute-start.1
  5.2 1.9 %collective-permute-start.2 = (f32[16,4096]{1,0:T(8,128)}, f32[16,4096]{1,0:T(8,128)S(1)}, u32[]{:S(2)}, u32[]{:S(2)}) collective-permute-start(f32[16,4096]{1,0:T(8,128)} %v_ref.1), channel_id=1, source_target_pairs={{1,2},{2,1},{5,6},{6,5},{9,10},{10,9},{13,14},{14,13},{17,18},{18,... | collective-permute-start | bytes 786440 | tf_op jit(solution)/shard_map/ppermute | solution.py:786
  7.2 0.1 collective-permute-start.3
  7.3 2.4 %pack.1 = f32[8,8,16,512]{3,2,1,0:T(8,128)} custom-call(f32[8,16,4096]{2,1,0:T(8,128)} %psi_ref.1), custom_call_target="tpu_custom_call" | custom-call | bytes 4194304 | tf_op jit(solution)/shard_map/pack/pallas_call | solution.py:144
  9.7 0.0 copy-start
  9.7 0.0 copy-start.3
  9.7 0.0 copy-start.4
  9.7 5.7 %all-to-all-start = ((f32[8,8,16,512]{3,2,1,0:T(8,128)}), f32[8,8,16,512]{3,2,1,0:T(8,128)}, u32[]{:S(2)}, u32[]{:S(2)}) async-start(f32[8,8,16,512]{3,2,1,0:T(8,128)} %pack.1), calls=%async_computation | async-start | bytes 4194304 | tf_op jit(solution)/shard_map/all_to_all | solution.py:763
  15.4 0.0 copy-done
  15.4 0.0 copy-done.3
  15.4 0.0 copy-done.4
  15.4 14.1 %own_part.1 = (f32[16,32,8,128]{3,2,1,0:T(8,128)}, f32[31,32,8,128]{3,2,1,0:T(8,128)S(1)}, f32[16,32,8,128]{3,2,1,0:T(8,128)S(1)}) custom-call(f32[8,16,4096]{2,1,0:T(8,128)S(1)} %copy-done, bf16[256,256]{1,0:T(8,128)(2,1)S(1)} %copy-done.3, bf16[256,256]{1,0:T(8,128)(2,1)S(1)} %copy-done.4), custom_call_target="tpu_custom_call" | custom-call | flops 10000000000 | bytes 10000000 | tf_op jit(solution)/shard_map/own_part/pallas_call | solution.py:317
  29.5 0.0 collective-permute-done.slab_hbm
  29.5 6.7 %side_part.2 = (f32[16,32,8,128]{3,2,1,0:T(8,128)S(1)}, f32[16,32,8,128]{3,2,1,0:T(8,128)S(1)}) custom-call(f32[8,16,4096]{2,1,0:T(8,128)} %collective-permute-done.slab_hbm, bf16[256,256]{1,0:T(8,128)(2,1)S(1)} %copy-done.3), custom_call_target="tpu_custom_call" | custom-call | flops 5000000000 | bytes 10000000 | tf_op jit(solution)/shard_map/side_part/pallas_call | solution.py:345
  36.2 0.0 copy-start.1
  36.2 0.0 copy-start.2
  36.2 0.0 collective-permute-done.1.slab_hbm
  36.2 6.7 %side_part.3 = (f32[16,32,8,128]{3,2,1,0:T(8,128)S(1)}, f32[16,32,8,128]{3,2,1,0:T(8,128)S(1)}) custom-call(f32[8,16,4096]{2,1,0:T(8,128)} %collective-permute-done.1.slab_hbm, bf16[256,256]{1,0:T(8,128)(2,1)S(1)} %copy-done.3), custom_call_target="tpu_custom_call" | custom-call | flops 5000000000 | bytes 10000000 | tf_op jit(solution)/shard_map/side_part/pallas_call | solution.py:345
  43.0 0.0 collective-permute-done.2.vfar_ref
  43.0 0.0 collective-permute-done.3.vnear_ref
  43.0 0.0 copy-done.1
  43.0 0.0 copy-done.2
  43.0 12.4 %halo_part.1 = f32[8,16,8,512]{3,2,1,0:T(8,128)} custom-call(f32[31,32,8,128]{3,2,1,0:T(8,128)S(1)} %get-tuple-element.17.grid_ref, f32[16,32,8,128]{3,2,1,0:T(8,128)S(1)} %get-tuple-element.18.kin_ref, f32[16,32,8,128]{3,2,1,0:T(8,128)S(1)} %get-tuple-element.19.cfar_ref, f32[16,32,8,128]{3,2,1,0:T(8,128)S(1)} %get-tuple-element.20.wfar_ref, ...), custom_call_target="tpu_custom_call" | custom-call | flops 20000000000 | bytes 10000000 | tf_op jit(solution)/shard_map/halo_part/pallas_call | solution.py:446
  55.4 0.0 copy-start.5
  55.5 7.6 %all-to-all-done.in_ref = f32[8,8,16,512]{3,2,1,0:T(8,128)} async-done(((f32[8,8,16,512]{3,2,1,0:T(8,128)}), f32[8,8,16,512]{3,2,1,0:T(8,128)}, u32[]{:S(2)}, u32[]{:S(2)}) %all-to-all-start) | async-done | bytes 2097184 | tf_op jit(solution)/shard_map/all_to_all | solution.py:763
  63.1 4.4 %all-to-all-start.1 = ((f32[8,16,8,512]{3,2,1,0:T(8,128)}), f32[8,16,8,512]{3,2,1,0:T(8,128)S(1)}, u32[]{:S(2)}, u32[]{:S(2)}) async-start(f32[8,16,8,512]{3,2,1,0:T(8,128)} %halo_part.1), calls=%async_computation.1 | async-start | bytes 4194304 | tf_op jit(solution)/shard_map/all_to_all | solution.py:763
  67.5 0.0 copy-done.5
  67.5 0.1 copy.9.slot_ref
  67.6 3.5 %choose.1.c_hbm = bf16[16,64,512]{2,1,0:T(8,128)(2,1)} custom-call(s32[32,1]{1,0:T(8,128)S(1)} %copy.9.slot_ref, f32[8,8,16,512]{3,2,1,0:T(8,128)} %all-to-all-done.in_ref), custom_call_target="tpu_custom_call" | custom-call | flops 100000000 | bytes 4194304 | tf_op jit(solution)/shard_map/choose/pallas_call | solution.py:177
  71.2 44.0 %all-to-all-done.1.a_ref = f32[8,16,8,512]{3,2,1,0:T(8,128)S(1)} async-done(((f32[8,16,8,512]{3,2,1,0:T(8,128)}), f32[8,16,8,512]{3,2,1,0:T(8,128)S(1)}, u32[]{:S(2)}, u32[]{:S(2)}) %all-to-all-start.1) | async-done | bytes 2097184 | tf_op jit(solution)/shard_map/all_to_all | solution.py:763
  115.2 2.4 %gram.1 = (f32[32,8,128]{2,1,0:T(8,128)S(1)}, bf16[16,64,512]{2,1,0:T(8,128)(2,1)S(1)}) custom-call(bf16[16,64,512]{2,1,0:T(8,128)(2,1)} %choose.1.c_hbm, f32[8,16,8,512]{3,2,1,0:T(8,128)S(1)} %all-to-all-done.1.a_ref, s32[32,1]{1,0:T(8,128)S(1)} %copy.9.slot_ref), custom_call_target="tpu_custom_call" | custom-call | flops 1000000000 | bytes 10000000 | tf_op jit(solution)/shard_map/gram/pallas_call | solution.py:509
  117.6 13.6 %all_to_all.25.part_ref = f32[32,8,128]{2,1,0:T(8,128)S(1)} all-to-all(f32[32,8,128]{2,1,0:T(8,128)S(1)} %get-tuple-element.24), channel_id=1, replica_groups=mesh['orb'=8,'box'=4] {'orb','box'}, dimensions={0} | all-to-all | bytes 262144 | tf_op jit(solution)/shard_map/all_to_all | solution.py:763
  131.2 1.7 correct.1
  132.9 16.6 %all_to_all.26.refs_0_ = f32[8,32,512]{2,1,0:T(8,128)S(1)} all-to-all(f32[8,32,512]{2,1,0:T(8,128)S(1)} %get-tuple-element.25), channel_id=1, replica_groups=mesh['orb'=8,'box'=4] {'orb'}, dimensions={0} | all-to-all | bytes 1048576 | tf_op jit(solution)/shard_map/all_to_all | solution.py:763
  149.5 4.0 %all-to-all-start.4 = ((f32[8,32,512]{2,1,0:T(8,128)}), f32[8,32,512]{2,1,0:T(8,128)S(1)}, u32[]{:S(2)}, u32[]{:S(2)}) async-start(f32[8,32,512]{2,1,0:T(8,128)} %get-tuple-element.26), calls=%async_computation.4 | async-start | bytes 1048576 | tf_op jit(solution)/shard_map/all_to_all | solution.py:763
  153.6 2.7 %collective-permute-start.4 = (f32[8,16,512]{2,1,0:T(8,128)S(1)}, f32[8,16,512]{2,1,0:T(8,128)S(1)}, u32[]{:S(2)}, u32[]{:S(2)}) collective-permute-start(f32[8,16,512]{2,1,0:T(8,128)S(1)} %get-tuple-element.32), channel_id=1, source_target_pairs={{0,1},{1,2},{2,3},{4,5},{5,6},{6,7},{8,9},{9,10},{10,11},{12,13},{... | collective-permute-start | bytes 786440 | tf_op jit(solution)/shard_map/ppermute | solution.py:811
  156.3 1.9 %collective-permute-start.5 = (f32[8,16,512]{2,1,0:T(8,128)S(1)}, f32[8,16,512]{2,1,0:T(8,128)S(1)}, u32[]{:S(2)}, u32[]{:S(2)}) collective-permute-start(f32[8,16,512]{2,1,0:T(8,128)S(1)} %get-tuple-element.31), channel_id=1, source_target_pairs={{1,0},{2,1},{3,2},{5,4},{6,5},{7,6},{9,8},{10,9},{11,10},{13,12},{... | collective-permute-start | bytes 786440 | tf_op jit(solution)/shard_map/ppermute | solution.py:814
  158.2 8.8 %all-to-all-done.4.refs_1_ = f32[8,32,512]{2,1,0:T(8,128)S(1)} async-done(((f32[8,32,512]{2,1,0:T(8,128)}), f32[8,32,512]{2,1,0:T(8,128)S(1)}, u32[]{:S(2)}, u32[]{:S(2)}) %all-to-all-start.4) | async-done | bytes 524320 | tf_op jit(solution)/shard_map/all_to_all | solution.py:763
  167.0 0.0 collective-permute-done.4.refs_2_
  167.0 0.0 collective-permute-done.5.refs_3_
  167.0 5.7 %relax.1 = (f32[4,16,4096]{2,1,0:T(8,128)}, f32[4,16,4096]{2,1,0:T(8,128)}) custom-call(f32[8,32,512]{2,1,0:T(8,128)S(1)} %all_to_all.26.refs_0_, f32[8,32,512]{2,1,0:T(8,128)S(1)} %all-to-all-done.4.refs_1_, f32[8,16,512]{2,1,0:T(8,128)S(1)} %collective-permute-done.4.refs_2_, f32[8,16,512]{2,1,0:T(8,128)S(1)} %collective-permute-done.5.refs_3_, ...), custom_call_target="tpu_custom_call" | custom-call | flops 1000000000 | bytes 10000000 | tf_op jit(solution)/shard_map/relax/pallas_call | solution.py:743
  (1 shorter events, 0.0 us)
Async XLA Ops:
  0.6 28.9 %collective-permute-start = (f32[8,16,4096]{2,1,0:T(8,128)}, f32[8,16,4096]{2,1,0:T(8,128)}, u32[]{:S(2)}, u32[]{:S(2)}) collective-permute-start(f32[8,16,4096]{2,1,0:T(8,128)} %psi_ref.1), channel_id=1, source_target_pairs={{1,2},{2,1},{5,6},{6,5},{9,10},{10,9},{13,14},{14,13},{17,18},{18,... | collective-permute-start | bytes 6291464 | tf_op jit(solution)/shard_map/ppermute | solution.py:780
  5.2 31.1 %collective-permute-start.1 = (f32[8,16,4096]{2,1,0:T(8,128)}, f32[8,16,4096]{2,1,0:T(8,128)}, u32[]{:S(2)}, u32[]{:S(2)}) collective-permute-start(f32[8,16,4096]{2,1,0:T(8,128)} %psi_ref.1), channel_id=1, source_target_pairs={{0,1},{2,3},{1,0},{3,2},{4,5},{6,7},{5,4},{7,6},{8,9},{10,11},{9,8... | collective-permute-start | bytes 6291464 | tf_op jit(solution)/shard_map/ppermute | solution.py:783
  5.2 37.7 %collective-permute-start.2 = (f32[16,4096]{1,0:T(8,128)}, f32[16,4096]{1,0:T(8,128)S(1)}, u32[]{:S(2)}, u32[]{:S(2)}) collective-permute-start(f32[16,4096]{1,0:T(8,128)} %v_ref.1), channel_id=1, source_target_pairs={{1,2},{2,1},{5,6},{6,5},{9,10},{10,9},{13,14},{14,13},{17,18},{18,... | collective-permute-start | bytes 786440 | tf_op jit(solution)/shard_map/ppermute | solution.py:786
  7.2 35.8 %collective-permute-start.3 = (f32[16,4096]{1,0:T(8,128)}, f32[16,4096]{1,0:T(8,128)S(1)}, u32[]{:S(2)}, u32[]{:S(2)}) collective-permute-start(f32[16,4096]{1,0:T(8,128)} %v_ref.1), channel_id=1, source_target_pairs={{0,1},{2,3},{1,0},{3,2},{4,5},{6,7},{5,4},{7,6},{8,9},{10,11},{9,8... | collective-permute-start | bytes 786440 | tf_op jit(solution)/shard_map/ppermute | solution.py:787
  9.7 5.7 %copy-start = (f32[8,16,4096]{2,1,0:T(8,128)S(1)}, f32[8,16,4096]{2,1,0:T(8,128)}, u32[]{:S(2)}) copy-start(f32[8,16,4096]{2,1,0:T(8,128)} %psi_ref.1) | copy-start | bytes 6291460
  9.7 5.7 %copy-start.3 = (bf16[256,256]{1,0:T(8,128)(2,1)S(1)}, bf16[256,256]{1,0:T(8,128)(2,1)}, u32[]{:S(2)}) copy-start(bf16[256,256]{1,0:T(8,128)(2,1)} %constant.6.clone.fwd_ref) | copy-start | bytes 393220
  9.7 5.7 %copy-start.4 = (bf16[256,256]{1,0:T(8,128)(2,1)S(1)}, bf16[256,256]{1,0:T(8,128)(2,1)}, u32[]{:S(2)}) copy-start(bf16[256,256]{1,0:T(8,128)(2,1)} %constant.8.clone.kin_ref) | copy-start | bytes 393220
  9.7 53.4 %all-to-all-start = ((f32[8,8,16,512]{3,2,1,0:T(8,128)}), f32[8,8,16,512]{3,2,1,0:T(8,128)}, u32[]{:S(2)}, u32[]{:S(2)}) async-start(f32[8,8,16,512]{3,2,1,0:T(8,128)} %pack.1), calls=%async_computation | async-start | bytes 4194304 | tf_op jit(solution)/shard_map/all_to_all | solution.py:763
  36.2 6.8 %copy-start.1 = (f32[16,4096]{1,0:T(8,128)S(1)}, f32[16,4096]{1,0:T(8,128)}, u32[]{:S(2)}) copy-start(f32[16,4096]{1,0:T(8,128)} %v_ref.1) | copy-start | bytes 786436
  36.2 6.8 %copy-start.2 = (bf16[256,256]{1,0:T(8,128)(2,1)S(1)}, bf16[256,256]{1,0:T(8,128)(2,1)}, u32[]{:S(2)}) copy-start(bf16[256,256]{1,0:T(8,128)(2,1)} %constant.7.clone.bwd_ref) | copy-start | bytes 393220
  55.4 12.1 %copy-start.5 = (s32[32]{0:T(128)S(1)}, s32[32]{0:T(128)}, u32[]{:S(2)}) copy-start(s32[32]{0:T(128)} %param.8) | copy-start | bytes 388
  63.1 52.1 %all-to-all-start.1 = ((f32[8,16,8,512]{3,2,1,0:T(8,128)}), f32[8,16,8,512]{3,2,1,0:T(8,128)S(1)}, u32[]{:S(2)}, u32[]{:S(2)}) async-start(f32[8,16,8,512]{3,2,1,0:T(8,128)} %halo_part.1), calls=%async_computation.1 | async-start | bytes 4194304 | tf_op jit(solution)/shard_map/all_to_all | solution.py:763
  149.5 17.5 %all-to-all-start.4 = ((f32[8,32,512]{2,1,0:T(8,128)}), f32[8,32,512]{2,1,0:T(8,128)S(1)}, u32[]{:S(2)}, u32[]{:S(2)}) async-start(f32[8,32,512]{2,1,0:T(8,128)} %get-tuple-element.26), calls=%async_computation.4 | async-start | bytes 1048576 | tf_op jit(solution)/shard_map/all_to_all | solution.py:763
  153.6 13.4 %collective-permute-start.4 = (f32[8,16,512]{2,1,0:T(8,128)S(1)}, f32[8,16,512]{2,1,0:T(8,128)S(1)}, u32[]{:S(2)}, u32[]{:S(2)}) collective-permute-start(f32[8,16,512]{2,1,0:T(8,128)S(1)} %get-tuple-element.32), channel_id=1, source_target_pairs={{0,1},{1,2},{2,3},{4,5},{5,6},{6,7},{8,9},{9,10},{10,11},{12,13},{... | collective-permute-start | bytes 786440 | tf_op jit(solution)/shard_map/ppermute | solution.py:811
  156.3 10.7 %collective-permute-start.5 = (f32[8,16,512]{2,1,0:T(8,128)S(1)}, f32[8,16,512]{2,1,0:T(8,128)S(1)}, u32[]{:S(2)}, u32[]{:S(2)}) collective-permute-start(f32[8,16,512]{2,1,0:T(8,128)S(1)} %get-tuple-element.31), channel_id=1, source_target_pairs={{1,0},{2,1},{3,2},{5,4},{6,5},{7,6},{9,8},{10,9},{11,10},{13,12},{... | collective-permute-start | bytes 786440 | tf_op jit(solution)/shard_map/ppermute | solution.py:814

commit v7 on v6

--- a/solution.py
+++ b/solution.py
@@ -15,7 +15,6 @@
 SWEEPS = 4
 LANES = 128
 
-highest = lax.Precision.HIGHEST
 coupling_z = 4.0
 coupling_xy = 1.0
 
@@ -478,20 +477,24 @@
     total_slots = sh.owners * sh.slots
     count = slot_ref.shape[0]
     chosen = selection(slot_ref, count, total_slots)
-    both = jnp.zeros((2 * count, 2 * total_slots), jnp.float32)
+    both = jnp.zeros((2 * total_slots, 2 * count), jnp.float32)
     copy.wait()
     for layer in range(sh.layers):
         rows = a_ref[:, layer].reshape(total_slots, sh.width)
         both = both + lax.dot_general(
+            jnp.concatenate(split(rows), 0),
             c_ref[layer],
-            jnp.concatenate(split(rows), 0),
             (((1,), (1,)), ((), ())),
             preferred_element_type=jnp.float32,
         )
-    wide = both[:count] + both[count:]
-    rows = wide[:, :total_slots] + wide[:, total_slots:]
+    wide = both[:total_slots] + both[total_slots:]
+    columns = wide[:, :count] + wide[:, count:]
+    parts = jnp.concatenate(split(columns), 0)
+    chosen = chosen.astype(jnp.bfloat16)
     picked = lax.dot_general(
-        rows, chosen, (((1,), (1,)), ((), ())), precision=highest,
+        parts,
+        jnp.concatenate([chosen, chosen], 1),
+        (((0,), (1,)), ((), ())),
         preferred_element_type=jnp.float32,
     ) * (1.0 / sh.box**3)
     picked = packed_rows(picked, fold)
@@ -600,10 +603,6 @@
         return keep_hi if tile >= tiles - edge_tiles else inverse
 
     group = min(32, sh.chunks)
-    blank = jnp.zeros((rows + 2 * edge, LANES), jnp.float32)
-    for ref in (one_ref, two_ref):
-        ref[0] = blank
-        ref[sh.chunks + 1] = blank
 
     def leave(source, target, kind, step, width):
         lanes = pl.ds(pl.multiple_of(step * width, LANES), width)

time: 175 us -> 175 us (level)
  no operation moved by 1% of the time
where the time goes in v7:
time: 175 us; the launch traced here: 172 us
  waiting for transfers between devices  60.4 us (35%)
  Pallas kernels  55.5 us (32%)
  blocking collectives  30.2 us (17%)
  starting transfers between devices  25.4 us (15%)
    all_to_all x3, waiting for transfers between devices, to_all(): return lax.all_to_all(value, axes, split_axis=0, concat_axis=0, tiled=True)  60.4 us
    all_to_all x2, blocking collectives, to_all(): return lax.all_to_all(value, axes, split_axis=0, concat_axis=0, tiled=True)  30.2 us
    all_to_all x3, starting transfers between devices, to_all(): return lax.all_to_all(value, axes, split_axis=0, concat_axis=0, tiled=True)  14.2 us
    pallas_call x1, Pallas kernels, own_part(): pl.pallas_call(functools.partial(own_kernel, sh), out_shape=(full, grid,...  14.1 us
    pallas_call x2, Pallas kernels, side_part(): pl.pallas_call(functools.partial(side_kernel, sh), out_shape=(jax.ShapeDt...  13.4 us
    pallas_call x1, Pallas kernels, halo_part(): pl.pallas_call(functools.partial(halo_kernel, sh), out_shape=pltpu.HBM(ou...  12.4 us
    pallas_call x1, Pallas kernels, relax(): pl.pallas_call(functools.partial(relax_kernel, sh, own, parts, boxes), ou...  5.67 us
    ppermute x1, starting transfers between devices, step(): far = lax.ppermute(psi, 'box', swap_far)  4.53 us
  transfers between devices with their start and end apart: 9, of which 3 were waited for; matrix products, arithmetic and copies ran while one was open for 0% of the time, Pallas kernels for 27%

profile of v7, /device:TPU:1, one launch (start us, length us, event | category | flops | bytes accessed | tf_op | source)
XLA Modules:
  0.0 172.5 jit_solution(15502405280724019459)
XLA Ops:
  0.6 4.5 %collective-permute-start = (f32[8,16,4096]{2,1,0:T(8,128)}, f32[8,16,4096]{2,1,0:T(8,128)}, u32[]{:S(2)}, u32[]{:S(2)}) collective-permute-start(f32[8,16,4096]{2,1,0:T(8,128)} %psi_ref.1), channel_id=1, source_target_pairs={{1,2},{2,1},{5,6},{6,5},{9,10},{10,9},{13,14},{14,13},{17,18},{18,... | collective-permute-start | bytes 6291464 | tf_op jit(solution)/shard_map/ppermute | solution.py:779
  5.2 0.1 collective-permute-start.1
  5.2 1.9 %collective-permute-start.2 = (f32[16,4096]{1,0:T(8,128)}, f32[16,4096]{1,0:T(8,128)S(1)}, u32[]{:S(2)}, u32[]{:S(2)}) collective-permute-start(f32[16,4096]{1,0:T(8,128)} %v_ref.1), channel_id=1, source_target_pairs={{1,2},{2,1},{5,6},{6,5},{9,10},{10,9},{13,14},{14,13},{17,18},{18,... | collective-permute-start | bytes 786440 | tf_op jit(solution)/shard_map/ppermute | solution.py:785
  7.2 0.1 collective-permute-start.3
  7.3 2.4 %pack.1 = f32[8,8,16,512]{3,2,1,0:T(8,128)} custom-call(f32[8,16,4096]{2,1,0:T(8,128)} %psi_ref.1), custom_call_target="tpu_custom_call" | custom-call | bytes 4194304 | tf_op jit(solution)/shard_map/pack/pallas_call | solution.py:143
  9.7 0.0 copy-start
  9.7 0.0 copy-start.3
  9.7 0.0 copy-start.4
  9.7 5.7 %all-to-all-start = ((f32[8,8,16,512]{3,2,1,0:T(8,128)}), f32[8,8,16,512]{3,2,1,0:T(8,128)}, u32[]{:S(2)}, u32[]{:S(2)}) async-start(f32[8,8,16,512]{3,2,1,0:T(8,128)} %pack.1), calls=%async_computation | async-start | bytes 4194304 | tf_op jit(solution)/shard_map/all_to_all | solution.py:762
  15.4 0.0 copy-done
  15.4 0.0 copy-done.3
  15.4 0.0 copy-done.4
  15.4 14.1 %own_part.1 = (f32[16,32,8,128]{3,2,1,0:T(8,128)}, f32[31,32,8,128]{3,2,1,0:T(8,128)S(1)}, f32[16,32,8,128]{3,2,1,0:T(8,128)S(1)}) custom-call(f32[8,16,4096]{2,1,0:T(8,128)S(1)} %copy-done, bf16[256,256]{1,0:T(8,128)(2,1)S(1)} %copy-done.3, bf16[256,256]{1,0:T(8,128)(2,1)S(1)} %copy-done.4), custom_call_target="tpu_custom_call" | custom-call | flops 10000000000 | bytes 10000000 | tf_op jit(solution)/shard_map/own_part/pallas_call | solution.py:316
  29.5 0.0 collective-permute-done.slab_hbm
  29.5 6.7 %side_part.2 = (f32[16,32,8,128]{3,2,1,0:T(8,128)S(1)}, f32[16,32,8,128]{3,2,1,0:T(8,128)S(1)}) custom-call(f32[8,16,4096]{2,1,0:T(8,128)} %collective-permute-done.slab_hbm, bf16[256,256]{1,0:T(8,128)(2,1)S(1)} %copy-done.3), custom_call_target="tpu_custom_call" | custom-call | flops 5000000000 | bytes 10000000 | tf_op jit(solution)/shard_map/side_part/pallas_call | solution.py:344
  36.2 0.0 copy-start.1
  36.2 0.0 copy-start.2
  36.2 0.0 collective-permute-done.1.slab_hbm
  36.2 6.7 %side_part.3 = (f32[16,32,8,128]{3,2,1,0:T(8,128)S(1)}, f32[16,32,8,128]{3,2,1,0:T(8,128)S(1)}) custom-call(f32[8,16,4096]{2,1,0:T(8,128)} %collective-permute-done.1.slab_hbm, bf16[256,256]{1,0:T(8,128)(2,1)S(1)} %copy-done.3), custom_call_target="tpu_custom_call" | custom-call | flops 5000000000 | bytes 10000000 | tf_op jit(solution)/shard_map/side_part/pallas_call | solution.py:344
  43.0 0.0 collective-permute-done.2.vfar_ref
  43.0 0.0 collective-permute-done.3.vnear_ref
  43.0 0.0 copy-done.1
  43.0 0.0 copy-done.2
  43.0 12.4 %halo_part.1 = f32[8,16,8,512]{3,2,1,0:T(8,128)} custom-call(f32[31,32,8,128]{3,2,1,0:T(8,128)S(1)} %get-tuple-element.17.grid_ref, f32[16,32,8,128]{3,2,1,0:T(8,128)S(1)} %get-tuple-element.18.kin_ref, f32[16,32,8,128]{3,2,1,0:T(8,128)S(1)} %get-tuple-element.19.cfar_ref, f32[16,32,8,128]{3,2,1,0:T(8,128)S(1)} %get-tuple-element.20.wfar_ref, ...), custom_call_target="tpu_custom_call" | custom-call | flops 20000000000 | bytes 10000000 | tf_op jit(solution)/shard_map/halo_part/pallas_call | solution.py:445
  55.4 0.0 copy-start.5
  55.5 7.6 %all-to-all-done.in_ref = f32[8,8,16,512]{3,2,1,0:T(8,128)} async-done(((f32[8,8,16,512]{3,2,1,0:T(8,128)}), f32[8,8,16,512]{3,2,1,0:T(8,128)}, u32[]{:S(2)}, u32[]{:S(2)}) %all-to-all-start) | async-done | bytes 2097184 | tf_op jit(solution)/shard_map/all_to_all | solution.py:762
  63.1 4.4 %all-to-all-start.1 = ((f32[8,16,8,512]{3,2,1,0:T(8,128)}), f32[8,16,8,512]{3,2,1,0:T(8,128)S(1)}, u32[]{:S(2)}, u32[]{:S(2)}) async-start(f32[8,16,8,512]{3,2,1,0:T(8,128)} %halo_part.1), calls=%async_computation.1 | async-start | bytes 4194304 | tf_op jit(solution)/shard_map/all_to_all | solution.py:762
  67.5 0.0 copy-done.5
  67.5 0.1 copy.9.slot_ref
  67.6 3.5 %choose.1.c_hbm = bf16[16,64,512]{2,1,0:T(8,128)(2,1)} custom-call(s32[32,1]{1,0:T(8,128)S(1)} %copy.9.slot_ref, f32[8,8,16,512]{3,2,1,0:T(8,128)} %all-to-all-done.in_ref), custom_call_target="tpu_custom_call" | custom-call | flops 100000000 | bytes 4194304 | tf_op jit(solution)/shard_map/choose/pallas_call | solution.py:176
  71.2 44.0 %all-to-all-done.1.a_ref = f32[8,16,8,512]{3,2,1,0:T(8,128)S(1)} async-done(((f32[8,16,8,512]{3,2,1,0:T(8,128)}), f32[8,16,8,512]{3,2,1,0:T(8,128)S(1)}, u32[]{:S(2)}, u32[]{:S(2)}) %all-to-all-start.1) | async-done | bytes 2097184 | tf_op jit(solution)/shard_map/all_to_all | solution.py:762
  115.2 2.2 %gram.1 = (f32[32,8,128]{2,1,0:T(8,128)S(1)}, bf16[16,64,512]{2,1,0:T(8,128)(2,1)S(1)}) custom-call(bf16[16,64,512]{2,1,0:T(8,128)(2,1)} %choose.1.c_hbm, f32[8,16,8,512]{3,2,1,0:T(8,128)S(1)} %all-to-all-done.1.a_ref, s32[32,1]{1,0:T(8,128)S(1)} %copy.9.slot_ref), custom_call_target="tpu_custom_call" | custom-call | flops 1000000000 | bytes 10000000 | tf_op jit(solution)/shard_map/gram/pallas_call | solution.py:512
  117.4 13.6 %all_to_all.25.part_ref = f32[32,8,128]{2,1,0:T(8,128)S(1)} all-to-all(f32[32,8,128]{2,1,0:T(8,128)S(1)} %get-tuple-element.24), channel_id=1, replica_groups=mesh['orb'=8,'box'=4] {'orb','box'}, dimensions={0} | all-to-all | bytes 262144 | tf_op jit(solution)/shard_map/all_to_all | solution.py:762
  131.0 1.7 correct.1
  132.7 16.6 %all_to_all.26.refs_0_ = f32[8,32,512]{2,1,0:T(8,128)S(1)} all-to-all(f32[8,32,512]{2,1,0:T(8,128)S(1)} %get-tuple-element.25), channel_id=1, replica_groups=mesh['orb'=8,'box'=4] {'orb'}, dimensions={0} | all-to-all | bytes 1048576 | tf_op jit(solution)/shard_map/all_to_all | solution.py:762
  149.3 4.0 %all-to-all-start.4 = ((f32[8,32,512]{2,1,0:T(8,128)}), f32[8,32,512]{2,1,0:T(8,128)S(1)}, u32[]{:S(2)}, u32[]{:S(2)}) async-start(f32[8,32,512]{2,1,0:T(8,128)} %get-tuple-element.26), calls=%async_computation.4 | async-start | bytes 1048576 | tf_op jit(solution)/shard_map/all_to_all | solution.py:762
  153.4 2.7 %collective-permute-start.4 = (f32[8,16,512]{2,1,0:T(8,128)S(1)}, f32[8,16,512]{2,1,0:T(8,128)S(1)}, u32[]{:S(2)}, u32[]{:S(2)}) collective-permute-start(f32[8,16,512]{2,1,0:T(8,128)S(1)} %get-tuple-element.32), channel_id=1, source_target_pairs={{0,1},{1,2},{2,3},{4,5},{5,6},{6,7},{8,9},{9,10},{10,11},{12,13},{... | collective-permute-start | bytes 786440 | tf_op jit(solution)/shard_map/ppermute | solution.py:810
  156.1 1.9 %collective-permute-start.5 = (f32[8,16,512]{2,1,0:T(8,128)S(1)}, f32[8,16,512]{2,1,0:T(8,128)S(1)}, u32[]{:S(2)}, u32[]{:S(2)}) collective-permute-start(f32[8,16,512]{2,1,0:T(8,128)S(1)} %get-tuple-element.31), channel_id=1, source_target_pairs={{1,0},{2,1},{3,2},{5,4},{6,5},{7,6},{9,8},{10,9},{11,10},{13,12},{... | collective-permute-start | bytes 786440 | tf_op jit(solution)/shard_map/ppermute | solution.py:813
  158.0 8.8 %all-to-all-done.4.refs_1_ = f32[8,32,512]{2,1,0:T(8,128)S(1)} async-done(((f32[8,32,512]{2,1,0:T(8,128)}), f32[8,32,512]{2,1,0:T(8,128)S(1)}, u32[]{:S(2)}, u32[]{:S(2)}) %all-to-all-start.4) | async-done | bytes 524320 | tf_op jit(solution)/shard_map/all_to_all | solution.py:762
  166.8 0.0 collective-permute-done.4.refs_2_
  166.8 0.0 collective-permute-done.5.refs_3_
  166.8 5.7 %relax.1 = (f32[4,16,4096]{2,1,0:T(8,128)}, f32[4,16,4096]{2,1,0:T(8,128)}) custom-call(f32[8,32,512]{2,1,0:T(8,128)S(1)} %all_to_all.26.refs_0_, f32[8,32,512]{2,1,0:T(8,128)S(1)} %all-to-all-done.4.refs_1_, f32[8,16,512]{2,1,0:T(8,128)S(1)} %collective-permute-done.4.refs_2_, f32[8,16,512]{2,1,0:T(8,128)S(1)} %collective-permute-done.5.refs_3_, ...), custom_call_target="tpu_custom_call" | custom-call | flops 1000000000 | bytes 10000000 | tf_op jit(solution)/shard_map/relax/pallas_call | solution.py:742
  (1 shorter events, 0.0 us)
Async XLA Ops:
  0.6 28.9 %collective-permute-start = (f32[8,16,4096]{2,1,0:T(8,128)}, f32[8,16,4096]{2,1,0:T(8,128)}, u32[]{:S(2)}, u32[]{:S(2)}) collective-permute-start(f32[8,16,4096]{2,1,0:T(8,128)} %psi_ref.1), channel_id=1, source_target_pairs={{1,2},{2,1},{5,6},{6,5},{9,10},{10,9},{13,14},{14,13},{17,18},{18,... | collective-permute-start | bytes 6291464 | tf_op jit(solution)/shard_map/ppermute | solution.py:779
  5.2 31.1 %collective-permute-start.1 = (f32[8,16,4096]{2,1,0:T(8,128)}, f32[8,16,4096]{2,1,0:T(8,128)}, u32[]{:S(2)}, u32[]{:S(2)}) collective-permute-start(f32[8,16,4096]{2,1,0:T(8,128)} %psi_ref.1), channel_id=1, source_target_pairs={{0,1},{2,3},{1,0},{3,2},{4,5},{6,7},{5,4},{7,6},{8,9},{10,11},{9,8... | collective-permute-start | bytes 6291464 | tf_op jit(solution)/shard_map/ppermute | solution.py:782
  5.2 37.7 %collective-permute-start.2 = (f32[16,4096]{1,0:T(8,128)}, f32[16,4096]{1,0:T(8,128)S(1)}, u32[]{:S(2)}, u32[]{:S(2)}) collective-permute-start(f32[16,4096]{1,0:T(8,128)} %v_ref.1), channel_id=1, source_target_pairs={{1,2},{2,1},{5,6},{6,5},{9,10},{10,9},{13,14},{14,13},{17,18},{18,... | collective-permute-start | bytes 786440 | tf_op jit(solution)/shard_map/ppermute | solution.py:785
  7.2 35.8 %collective-permute-start.3 = (f32[16,4096]{1,0:T(8,128)}, f32[16,4096]{1,0:T(8,128)S(1)}, u32[]{:S(2)}, u32[]{:S(2)}) collective-permute-start(f32[16,4096]{1,0:T(8,128)} %v_ref.1), channel_id=1, source_target_pairs={{0,1},{2,3},{1,0},{3,2},{4,5},{6,7},{5,4},{7,6},{8,9},{10,11},{9,8... | collective-permute-start | bytes 786440 | tf_op jit(solution)/shard_map/ppermute | solution.py:786
  9.7 5.7 %copy-start = (f32[8,16,4096]{2,1,0:T(8,128)S(1)}, f32[8,16,4096]{2,1,0:T(8,128)}, u32[]{:S(2)}) copy-start(f32[8,16,4096]{2,1,0:T(8,128)} %psi_ref.1) | copy-start | bytes 6291460
  9.7 5.7 %copy-start.3 = (bf16[256,256]{1,0:T(8,128)(2,1)S(1)}, bf16[256,256]{1,0:T(8,128)(2,1)}, u32[]{:S(2)}) copy-start(bf16[256,256]{1,0:T(8,128)(2,1)} %constant.6.clone.fwd_ref) | copy-start | bytes 393220
  9.7 5.7 %copy-start.4 = (bf16[256,256]{1,0:T(8,128)(2,1)S(1)}, bf16[256,256]{1,0:T(8,128)(2,1)}, u32[]{:S(2)}) copy-start(bf16[256,256]{1,0:T(8,128)(2,1)} %constant.8.clone.kin_ref) | copy-start | bytes 393220
  9.7 53.4 %all-to-all-start = ((f32[8,8,16,512]{3,2,1,0:T(8,128)}), f32[8,8,16,512]{3,2,1,0:T(8,128)}, u32[]{:S(2)}, u32[]{:S(2)}) async-start(f32[8,8,16,512]{3,2,1,0:T(8,128)} %pack.1), calls=%async_computation | async-start | bytes 4194304 | tf_op jit(solution)/shard_map/all_to_all | solution.py:762
  36.2 6.8 %copy-start.1 = (f32[16,4096]{1,0:T(8,128)S(1)}, f32[16,4096]{1,0:T(8,128)}, u32[]{:S(2)}) copy-start(f32[16,4096]{1,0:T(8,128)} %v_ref.1) | copy-start | bytes 786436
  36.2 6.8 %copy-start.2 = (bf16[256,256]{1,0:T(8,128)(2,1)S(1)}, bf16[256,256]{1,0:T(8,128)(2,1)}, u32[]{:S(2)}) copy-start(bf16[256,256]{1,0:T(8,128)(2,1)} %constant.7.clone.bwd_ref) | copy-start | bytes 393220
  55.4 12.1 %copy-start.5 = (s32[32]{0:T(128)S(1)}, s32[32]{0:T(128)}, u32[]{:S(2)}) copy-start(s32[32]{0:T(128)} %param.8) | copy-start | bytes 388
  63.1 52.1 %all-to-all-start.1 = ((f32[8,16,8,512]{3,2,1,0:T(8,128)}), f32[8,16,8,512]{3,2,1,0:T(8,128)S(1)}, u32[]{:S(2)}, u32[]{:S(2)}) async-start(f32[8,16,8,512]{3,2,1,0:T(8,128)} %halo_part.1), calls=%async_computation.1 | async-start | bytes 4194304 | tf_op jit(solution)/shard_map/all_to_all | solution.py:762
  149.3 17.5 %all-to-all-start.4 = ((f32[8,32,512]{2,1,0:T(8,128)}), f32[8,32,512]{2,1,0:T(8,128)S(1)}, u32[]{:S(2)}, u32[]{:S(2)}) async-start(f32[8,32,512]{2,1,0:T(8,128)} %get-tuple-element.26), calls=%async_computation.4 | async-start | bytes 1048576 | tf_op jit(solution)/shard_map/all_to_all | solution.py:762
  153.4 13.4 %collective-permute-start.4 = (f32[8,16,512]{2,1,0:T(8,128)S(1)}, f32[8,16,512]{2,1,0:T(8,128)S(1)}, u32[]{:S(2)}, u32[]{:S(2)}) collective-permute-start(f32[8,16,512]{2,1,0:T(8,128)S(1)} %get-tuple-element.32), channel_id=1, source_target_pairs={{0,1},{1,2},{2,3},{4,5},{5,6},{6,7},{8,9},{9,10},{10,11},{12,13},{... | collective-permute-start | bytes 786440 | tf_op jit(solution)/shard_map/ppermute | solution.py:810
  156.1 10.7 %collective-permute-start.5 = (f32[8,16,512]{2,1,0:T(8,128)S(1)}, f32[8,16,512]{2,1,0:T(8,128)S(1)}, u32[]{:S(2)}, u32[]{:S(2)}) collective-permute-start(f32[8,16,512]{2,1,0:T(8,128)S(1)} %get-tuple-element.31), channel_id=1, source_target_pairs={{1,0},{2,1},{3,2},{5,4},{6,5},{7,6},{9,8},{10,9},{11,10},{13,12},{... | collective-permute-start | bytes 786440 | tf_op jit(solution)/shard_map/ppermute | solution.py:813

commit v8 on v6

--- a/solution.py
+++ b/solution.py
@@ -600,10 +600,6 @@
         return keep_hi if tile >= tiles - edge_tiles else inverse
 
     group = min(32, sh.chunks)
-    blank = jnp.zeros((rows + 2 * edge, LANES), jnp.float32)
-    for ref in (one_ref, two_ref):
-        ref[0] = blank
-        ref[sh.chunks + 1] = blank
 
     def leave(source, target, kind, step, width):
         lanes = pl.ds(pl.multiple_of(step * width, LANES), width)
@@ -707,7 +703,7 @@
             seal(target)
         source, target = target, source
 
-    few = min(8, half)
+    few = min(4, half)
 
     def spread(step, carry):
         for column in range(few):

time: 175 us -> 175 us (level)
  no operation moved by 1% of the time
where the time goes in v8:
time: 175 us; the launch traced here: 173 us
  waiting for transfers between devices  60.4 us (35%)
  Pallas kernels  55.7 us (32%)
  blocking collectives  30.2 us (17%)
  starting transfers between devices  25.4 us (15%)
    all_to_all x3, waiting for transfers between devices, to_all(): return lax.all_to_all(value, axes, split_axis=0, concat_axis=0, tiled=True)  60.4 us
    all_to_all x2, blocking collectives, to_all(): return lax.all_to_all(value, axes, split_axis=0, concat_axis=0, tiled=True)  30.2 us
    all_to_all x3, starting transfers between devices, to_all(): return lax.all_to_all(value, axes, split_axis=0, concat_axis=0, tiled=True)  14.2 us
    pallas_call x1, Pallas kernels, own_part(): pl.pallas_call(functools.partial(own_kernel, sh), out_shape=(full, grid,...  14.1 us
    pallas_call x2, Pallas kernels, side_part(): pl.pallas_call(functools.partial(side_kernel, sh), out_shape=(jax.ShapeDt...  13.4 us
    pallas_call x1, Pallas kernels, halo_part(): pl.pallas_call(functools.partial(halo_kernel, sh), out_shape=pltpu.HBM(ou...  12.4 us
    pallas_call x1, Pallas kernels, relax(): pl.pallas_call(functools.partial(relax_kernel, sh, own, parts, boxes), ou...  5.72 us
    ppermute x1, starting transfers between devices, step(): far = lax.ppermute(psi, 'box', swap_far)  4.53 us
  transfers between devices with their start and end apart: 9, of which 3 were waited for; matrix products, arithmetic and copies ran while one was open for 0% of the time, Pallas kernels for 27%

profile of v8, /device:TPU:1, one launch (start us, length us, event | category | flops | bytes accessed | tf_op | source)
XLA Modules:
  0.0 172.7 jit_solution(13363887674975171300)
XLA Ops:
  0.6 4.5 %collective-permute-start = (f32[8,16,4096]{2,1,0:T(8,128)}, f32[8,16,4096]{2,1,0:T(8,128)}, u32[]{:S(2)}, u32[]{:S(2)}) collective-permute-start(f32[8,16,4096]{2,1,0:T(8,128)} %psi_ref.1), channel_id=1, source_target_pairs={{1,2},{2,1},{5,6},{6,5},{9,10},{10,9},{13,14},{14,13},{17,18},{18,... | collective-permute-start | bytes 6291464 | tf_op jit(solution)/shard_map/ppermute | solution.py:776
  5.2 0.1 collective-permute-start.1
  5.2 1.9 %collective-permute-start.2 = (f32[16,4096]{1,0:T(8,128)}, f32[16,4096]{1,0:T(8,128)S(1)}, u32[]{:S(2)}, u32[]{:S(2)}) collective-permute-start(f32[16,4096]{1,0:T(8,128)} %v_ref.1), channel_id=1, source_target_pairs={{1,2},{2,1},{5,6},{6,5},{9,10},{10,9},{13,14},{14,13},{17,18},{18,... | collective-permute-start | bytes 786440 | tf_op jit(solution)/shard_map/ppermute | solution.py:782
  7.2 0.1 collective-permute-start.3
  7.3 2.4 %pack.1 = f32[8,8,16,512]{3,2,1,0:T(8,128)} custom-call(f32[8,16,4096]{2,1,0:T(8,128)} %psi_ref.1), custom_call_target="tpu_custom_call" | custom-call | bytes 4194304 | tf_op jit(solution)/shard_map/pack/pallas_call | solution.py:144
  9.7 0.0 copy-start
  9.7 0.0 copy-start.3
  9.7 0.0 copy-start.4
  9.7 5.7 %all-to-all-start = ((f32[8,8,16,512]{3,2,1,0:T(8,128)}), f32[8,8,16,512]{3,2,1,0:T(8,128)}, u32[]{:S(2)}, u32[]{:S(2)}) async-start(f32[8,8,16,512]{3,2,1,0:T(8,128)} %pack.1), calls=%async_computation | async-start | bytes 4194304 | tf_op jit(solution)/shard_map/all_to_all | solution.py:759
  15.4 0.0 copy-done
  15.4 0.0 copy-done.3
  15.4 0.0 copy-done.4
  15.4 14.1 %own_part.1 = (f32[16,32,8,128]{3,2,1,0:T(8,128)}, f32[31,32,8,128]{3,2,1,0:T(8,128)S(1)}, f32[16,32,8,128]{3,2,1,0:T(8,128)S(1)}) custom-call(f32[8,16,4096]{2,1,0:T(8,128)S(1)} %copy-done, bf16[256,256]{1,0:T(8,128)(2,1)S(1)} %copy-done.3, bf16[256,256]{1,0:T(8,128)(2,1)S(1)} %copy-done.4), custom_call_target="tpu_custom_call" | custom-call | flops 10000000000 | bytes 10000000 | tf_op jit(solution)/shard_map/own_part/pallas_call | solution.py:317
  29.5 0.0 collective-permute-done.slab_hbm
  29.5 6.7 %side_part.2 = (f32[16,32,8,128]{3,2,1,0:T(8,128)S(1)}, f32[16,32,8,128]{3,2,1,0:T(8,128)S(1)}) custom-call(f32[8,16,4096]{2,1,0:T(8,128)} %collective-permute-done.slab_hbm, bf16[256,256]{1,0:T(8,128)(2,1)S(1)} %copy-done.3), custom_call_target="tpu_custom_call" | custom-call | flops 5000000000 | bytes 10000000 | tf_op jit(solution)/shard_map/side_part/pallas_call | solution.py:345
  36.2 0.0 copy-start.1
  36.2 0.0 copy-start.2
  36.2 0.0 collective-permute-done.1.slab_hbm
  36.2 6.7 %side_part.3 = (f32[16,32,8,128]{3,2,1,0:T(8,128)S(1)}, f32[16,32,8,128]{3,2,1,0:T(8,128)S(1)}) custom-call(f32[8,16,4096]{2,1,0:T(8,128)} %collective-permute-done.1.slab_hbm, bf16[256,256]{1,0:T(8,128)(2,1)S(1)} %copy-done.3), custom_call_target="tpu_custom_call" | custom-call | flops 5000000000 | bytes 10000000 | tf_op jit(solution)/shard_map/side_part/pallas_call | solution.py:345
  43.0 0.0 collective-permute-done.2.vfar_ref
  43.0 0.0 collective-permute-done.3.vnear_ref
  43.0 0.0 copy-done.1
  43.0 0.0 copy-done.2
  43.0 12.4 %halo_part.1 = f32[8,16,8,512]{3,2,1,0:T(8,128)} custom-call(f32[31,32,8,128]{3,2,1,0:T(8,128)S(1)} %get-tuple-element.17.grid_ref, f32[16,32,8,128]{3,2,1,0:T(8,128)S(1)} %get-tuple-element.18.kin_ref, f32[16,32,8,128]{3,2,1,0:T(8,128)S(1)} %get-tuple-element.19.cfar_ref, f32[16,32,8,128]{3,2,1,0:T(8,128)S(1)} %get-tuple-element.20.wfar_ref, ...), custom_call_target="tpu_custom_call" | custom-call | flops 20000000000 | bytes 10000000 | tf_op jit(solution)/shard_map/halo_part/pallas_call | solution.py:446
  55.4 0.0 copy-start.5
  55.5 7.6 %all-to-all-done.in_ref = f32[8,8,16,512]{3,2,1,0:T(8,128)} async-done(((f32[8,8,16,512]{3,2,1,0:T(8,128)}), f32[8,8,16,512]{3,2,1,0:T(8,128)}, u32[]{:S(2)}, u32[]{:S(2)}) %all-to-all-start) | async-done | bytes 2097184 | tf_op jit(solution)/shard_map/all_to_all | solution.py:759
  63.1 4.4 %all-to-all-start.1 = ((f32[8,16,8,512]{3,2,1,0:T(8,128)}), f32[8,16,8,512]{3,2,1,0:T(8,128)S(1)}, u32[]{:S(2)}, u32[]{:S(2)}) async-start(f32[8,16,8,512]{3,2,1,0:T(8,128)} %halo_part.1), calls=%async_computation.1 | async-start | bytes 4194304 | tf_op jit(solution)/shard_map/all_to_all | solution.py:759
  67.5 0.0 copy-done.5
  67.5 0.1 copy.9.slot_ref
  67.6 3.5 %choose.1.c_hbm = bf16[16,64,512]{2,1,0:T(8,128)(2,1)} custom-call(s32[32,1]{1,0:T(8,128)S(1)} %copy.9.slot_ref, f32[8,8,16,512]{3,2,1,0:T(8,128)} %all-to-all-done.in_ref), custom_call_target="tpu_custom_call" | custom-call | flops 100000000 | bytes 4194304 | tf_op jit(solution)/shard_map/choose/pallas_call | solution.py:177
  71.2 44.0 %all-to-all-done.1.a_ref = f32[8,16,8,512]{3,2,1,0:T(8,128)S(1)} async-done(((f32[8,16,8,512]{3,2,1,0:T(8,128)}), f32[8,16,8,512]{3,2,1,0:T(8,128)S(1)}, u32[]{:S(2)}, u32[]{:S(2)}) %all-to-all-start.1) | async-done | bytes 2097184 | tf_op jit(solution)/shard_map/all_to_all | solution.py:759
  115.2 2.4 %gram.1 = (f32[32,8,128]{2,1,0:T(8,128)S(1)}, bf16[16,64,512]{2,1,0:T(8,128)(2,1)S(1)}) custom-call(bf16[16,64,512]{2,1,0:T(8,128)(2,1)} %choose.1.c_hbm, f32[8,16,8,512]{3,2,1,0:T(8,128)S(1)} %all-to-all-done.1.a_ref, s32[32,1]{1,0:T(8,128)S(1)} %copy.9.slot_ref), custom_call_target="tpu_custom_call" | custom-call | flops 1000000000 | bytes 10000000 | tf_op jit(solution)/shard_map/gram/pallas_call | solution.py:509
  117.6 13.6 %all_to_all.25.part_ref = f32[32,8,128]{2,1,0:T(8,128)S(1)} all-to-all(f32[32,8,128]{2,1,0:T(8,128)S(1)} %get-tuple-element.24), channel_id=1, replica_groups=mesh['orb'=8,'box'=4] {'orb','box'}, dimensions={0} | all-to-all | bytes 262144 | tf_op jit(solution)/shard_map/all_to_all | solution.py:759
  131.2 1.7 correct.1
  132.9 16.6 %all_to_all.26.refs_0_ = f32[8,32,512]{2,1,0:T(8,128)S(1)} all-to-all(f32[8,32,512]{2,1,0:T(8,128)S(1)} %get-tuple-element.25), channel_id=1, replica_groups=mesh['orb'=8,'box'=4] {'orb'}, dimensions={0} | all-to-all | bytes 1048576 | tf_op jit(solution)/shard_map/all_to_all | solution.py:759
  149.5 4.0 %all-to-all-start.4 = ((f32[8,32,512]{2,1,0:T(8,128)}), f32[8,32,512]{2,1,0:T(8,128)S(1)}, u32[]{:S(2)}, u32[]{:S(2)}) async-start(f32[8,32,512]{2,1,0:T(8,128)} %get-tuple-element.26), calls=%async_computation.4 | async-start | bytes 1048576 | tf_op jit(solution)/shard_map/all_to_all | solution.py:759
  153.6 2.7 %collective-permute-start.4 = (f32[8,16,512]{2,1,0:T(8,128)S(1)}, f32[8,16,512]{2,1,0:T(8,128)S(1)}, u32[]{:S(2)}, u32[]{:S(2)}) collective-permute-start(f32[8,16,512]{2,1,0:T(8,128)S(1)} %get-tuple-element.32), channel_id=1, source_target_pairs={{0,1},{1,2},{2,3},{4,5},{5,6},{6,7},{8,9},{9,10},{10,11},{12,13},{... | collective-permute-start | bytes 786440 | tf_op jit(solution)/shard_map/ppermute | solution.py:807
  156.3 1.9 %collective-permute-start.5 = (f32[8,16,512]{2,1,0:T(8,128)S(1)}, f32[8,16,512]{2,1,0:T(8,128)S(1)}, u32[]{:S(2)}, u32[]{:S(2)}) collective-permute-start(f32[8,16,512]{2,1,0:T(8,128)S(1)} %get-tuple-element.31), channel_id=1, source_target_pairs={{1,0},{2,1},{3,2},{5,4},{6,5},{7,6},{9,8},{10,9},{11,10},{13,12},{... | collective-permute-start | bytes 786440 | tf_op jit(solution)/shard_map/ppermute | solution.py:810
  158.2 8.8 %all-to-all-done.4.refs_1_ = f32[8,32,512]{2,1,0:T(8,128)S(1)} async-done(((f32[8,32,512]{2,1,0:T(8,128)}), f32[8,32,512]{2,1,0:T(8,128)S(1)}, u32[]{:S(2)}, u32[]{:S(2)}) %all-to-all-start.4) | async-done | bytes 524320 | tf_op jit(solution)/shard_map/all_to_all | solution.py:759
  167.0 0.0 collective-permute-done.4.refs_2_
  167.0 0.0 collective-permute-done.5.refs_3_
  167.0 5.7 %relax.1 = (f32[4,16,4096]{2,1,0:T(8,128)}, f32[4,16,4096]{2,1,0:T(8,128)}) custom-call(f32[8,32,512]{2,1,0:T(8,128)S(1)} %all_to_all.26.refs_0_, f32[8,32,512]{2,1,0:T(8,128)S(1)} %all-to-all-done.4.refs_1_, f32[8,16,512]{2,1,0:T(8,128)S(1)} %collective-permute-done.4.refs_2_, f32[8,16,512]{2,1,0:T(8,128)S(1)} %collective-permute-done.5.refs_3_, ...), custom_call_target="tpu_custom_call" | custom-call | flops 1000000000 | bytes 10000000 | tf_op jit(solution)/shard_map/relax/pallas_call | solution.py:739
  (1 shorter events, 0.0 us)
Async XLA Ops:
  0.6 28.9 %collective-permute-start = (f32[8,16,4096]{2,1,0:T(8,128)}, f32[8,16,4096]{2,1,0:T(8,128)}, u32[]{:S(2)}, u32[]{:S(2)}) collective-permute-start(f32[8,16,4096]{2,1,0:T(8,128)} %psi_ref.1), channel_id=1, source_target_pairs={{1,2},{2,1},{5,6},{6,5},{9,10},{10,9},{13,14},{14,13},{17,18},{18,... | collective-permute-start | bytes 6291464 | tf_op jit(solution)/shard_map/ppermute | solution.py:776
  5.2 31.1 %collective-permute-start.1 = (f32[8,16,4096]{2,1,0:T(8,128)}, f32[8,16,4096]{2,1,0:T(8,128)}, u32[]{:S(2)}, u32[]{:S(2)}) collective-permute-start(f32[8,16,4096]{2,1,0:T(8,128)} %psi_ref.1), channel_id=1, source_target_pairs={{0,1},{2,3},{1,0},{3,2},{4,5},{6,7},{5,4},{7,6},{8,9},{10,11},{9,8... | collective-permute-start | bytes 6291464 | tf_op jit(solution)/shard_map/ppermute | solution.py:779
  5.2 37.7 %collective-permute-start.2 = (f32[16,4096]{1,0:T(8,128)}, f32[16,4096]{1,0:T(8,128)S(1)}, u32[]{:S(2)}, u32[]{:S(2)}) collective-permute-start(f32[16,4096]{1,0:T(8,128)} %v_ref.1), channel_id=1, source_target_pairs={{1,2},{2,1},{5,6},{6,5},{9,10},{10,9},{13,14},{14,13},{17,18},{18,... | collective-permute-start | bytes 786440 | tf_op jit(solution)/shard_map/ppermute | solution.py:782
  7.2 35.8 %collective-permute-start.3 = (f32[16,4096]{1,0:T(8,128)}, f32[16,4096]{1,0:T(8,128)S(1)}, u32[]{:S(2)}, u32[]{:S(2)}) collective-permute-start(f32[16,4096]{1,0:T(8,128)} %v_ref.1), channel_id=1, source_target_pairs={{0,1},{2,3},{1,0},{3,2},{4,5},{6,7},{5,4},{7,6},{8,9},{10,11},{9,8... | collective-permute-start | bytes 786440 | tf_op jit(solution)/shard_map/ppermute | solution.py:783
  9.7 5.7 %copy-start = (f32[8,16,4096]{2,1,0:T(8,128)S(1)}, f32[8,16,4096]{2,1,0:T(8,128)}, u32[]{:S(2)}) copy-start(f32[8,16,4096]{2,1,0:T(8,128)} %psi_ref.1) | copy-start | bytes 6291460
  9.7 5.7 %copy-start.3 = (bf16[256,256]{1,0:T(8,128)(2,1)S(1)}, bf16[256,256]{1,0:T(8,128)(2,1)}, u32[]{:S(2)}) copy-start(bf16[256,256]{1,0:T(8,128)(2,1)} %constant.6.clone.fwd_ref) | copy-start | bytes 393220
  9.7 5.7 %copy-start.4 = (bf16[256,256]{1,0:T(8,128)(2,1)S(1)}, bf16[256,256]{1,0:T(8,128)(2,1)}, u32[]{:S(2)}) copy-start(bf16[256,256]{1,0:T(8,128)(2,1)} %constant.8.clone.kin_ref) | copy-start | bytes 393220
  9.7 53.4 %all-to-all-start = ((f32[8,8,16,512]{3,2,1,0:T(8,128)}), f32[8,8,16,512]{3,2,1,0:T(8,128)}, u32[]{:S(2)}, u32[]{:S(2)}) async-start(f32[8,8,16,512]{3,2,1,0:T(8,128)} %pack.1), calls=%async_computation | async-start | bytes 4194304 | tf_op jit(solution)/shard_map/all_to_all | solution.py:759
  36.2 6.8 %copy-start.1 = (f32[16,4096]{1,0:T(8,128)S(1)}, f32[16,4096]{1,0:T(8,128)}, u32[]{:S(2)}) copy-start(f32[16,4096]{1,0:T(8,128)} %v_ref.1) | copy-start | bytes 786436
  36.2 6.8 %copy-start.2 = (bf16[256,256]{1,0:T(8,128)(2,1)S(1)}, bf16[256,256]{1,0:T(8,128)(2,1)}, u32[]{:S(2)}) copy-start(bf16[256,256]{1,0:T(8,128)(2,1)} %constant.7.clone.bwd_ref) | copy-start | bytes 393220
  55.4 12.1 %copy-start.5 = (s32[32]{0:T(128)S(1)}, s32[32]{0:T(128)}, u32[]{:S(2)}) copy-start(s32[32]{0:T(128)} %param.8) | copy-start | bytes 388
  63.1 52.1 %all-to-all-start.1 = ((f32[8,16,8,512]{3,2,1,0:T(8,128)}), f32[8,16,8,512]{3,2,1,0:T(8,128)S(1)}, u32[]{:S(2)}, u32[]{:S(2)}) async-start(f32[8,16,8,512]{3,2,1,0:T(8,128)} %halo_part.1), calls=%async_computation.1 | async-start | bytes 4194304 | tf_op jit(solution)/shard_map/all_to_all | solution.py:759
  149.5 17.5 %all-to-all-start.4 = ((f32[8,32,512]{2,1,0:T(8,128)}), f32[8,32,512]{2,1,0:T(8,128)S(1)}, u32[]{:S(2)}, u32[]{:S(2)}) async-start(f32[8,32,512]{2,1,0:T(8,128)} %get-tuple-element.26), calls=%async_computation.4 | async-start | bytes 1048576 | tf_op jit(solution)/shard_map/all_to_all | solution.py:759
  153.6 13.4 %collective-permute-start.4 = (f32[8,16,512]{2,1,0:T(8,128)S(1)}, f32[8,16,512]{2,1,0:T(8,128)S(1)}, u32[]{:S(2)}, u32[]{:S(2)}) collective-permute-start(f32[8,16,512]{2,1,0:T(8,128)S(1)} %get-tuple-element.32), channel_id=1, source_target_pairs={{0,1},{1,2},{2,3},{4,5},{5,6},{6,7},{8,9},{9,10},{10,11},{12,13},{... | collective-permute-start | bytes 786440 | tf_op jit(solution)/shard_map/ppermute | solution.py:807
  156.3 10.7 %collective-permute-start.5 = (f32[8,16,512]{2,1,0:T(8,128)S(1)}, f32[8,16,512]{2,1,0:T(8,128)S(1)}, u32[]{:S(2)}, u32[]{:S(2)}) collective-permute-start(f32[8,16,512]{2,1,0:T(8,128)S(1)} %get-tuple-element.31), channel_id=1, source_target_pairs={{1,0},{2,1},{3,2},{5,4},{6,5},{7,6},{9,8},{10,9},{11,10},{13,12},{... | collective-permute-start | bytes 786440 | tf_op jit(solution)/shard_map/ppermute | solution.py:810
